TPU v7x, 256 devices: a whole 4x4x8 slice. The times are simulated.
256 devices in a mesh: user: 16 (over y, x_hi, core), item: 16 (over z, x_lo).
Axes of the slice: x: 4 (x_hi: 2, x_lo: 2; x = x_hi * 2 + x_lo), y: 4, z: 8, core: 2. Of those that a mesh axis runs over, the one named last changes fastest.
Arguments:
- ratings: bfloat16 [12288, 24576], P('user', 'item')
- presence: int32 [96, 192], P('user', 'item'), may hold values from 0 to 1
- user_factors: float32 [12288, 128], P('user'), may hold values from -4 to 4
- item_factors: float32 [24576, 128], P('item'), may hold values from -4 to 4
- step_sizes: float32 [2], replicated, may hold values from 0.3 to 0.7
Outputs:
- new_users: float32 [12288, 128], P('user')
- new_items: float32 [24576, 128], P('item')
All inputs are finite; a program needn't handle non-finite values.
Results may differ from a plain program's by a relative error of at most 0.0003.
Values sent between devices are 32-bit elements; how exact they have to be, the bound alone decides.
No kernel may reach another device: no remote copies, remote signals or barrier semaphores. Data moves between devices by JAX's collectives and lax.ppermute only.
A program may use at most 64 MiB of HBM per device.

v0:
```python
import math

import jax
import jax.numpy as jnp
from jax import lax
from jax.sharding import PartitionSpec as P

BLK = 128


highest = lax.Precision.HIGHEST


def cut_along(shard, dim, devices):
    dims = shard.shape
    pieces = shard.reshape(*dims[:dim], devices, dims[dim] // devices, *dims[dim + 1 :])
    return jnp.moveaxis(pieces, dim, 0)


def sent_and_summed(shard, axis, dim):
    pieces = cut_along(shard, dim, lax.axis_size(axis))
    arrived = lax.all_to_all(pieces, axis, split_axis=0, concat_axis=0, tiled=True)
    return arrived.sum(axis=0)


def sent_together(arrays, axis, dim, along):
    widths = [math.prod(a.shape[along:]) for a in arrays]
    both = jnp.concatenate(
        [a.reshape(*a.shape[:along], w) for a, w in zip(arrays, widths)], axis=along
    )
    filled = sent_and_summed(both, axis, dim)
    pieces = jnp.split(filled, [sum(widths[:k]) for k in range(1, len(widths))], axis=along)
    return tuple(
        (b.reshape(*filled.shape[:along], *a.shape[along:]) for a, b in zip(arrays, pieces))
    )


def in_order(pieces, dim):
    pieces = jnp.moveaxis(pieces, 0, dim)
    dims = pieces.shape
    return pieces.reshape(*dims[:dim], dims[dim] * dims[dim + 1], *dims[dim + 2 :])


def sent_to_all(shard, axis):
    devices = lax.axis_size(axis)
    return lax.all_to_all(
        jnp.broadcast_to(shard[None], (devices, *shard.shape)), axis, 0, 0, tiled=True
    )


def gathered_copies(shard, axis, dim):
    return in_order(sent_to_all(shard, axis), dim)


def residual(ratings, presence, users, item_factors):
    predicted = lax.dot_general(
        users,
        item_factors,
        (((1,), (1,)), ((), ())),
        precision=highest,
        preferred_element_type=jnp.float32,
    )
    user_count, item_count = ratings.shape
    blocked = (ratings.astype(jnp.float32) - predicted).reshape(
        user_count // BLK, BLK, item_count // BLK, BLK
    )
    blocked = blocked * presence.astype(jnp.float32)[:, None, :, None]
    return blocked.reshape(user_count, item_count)


def user_partial(ratings, presence, users, item_factors):
    resid = residual(ratings, presence, users, item_factors)
    return jnp.dot(resid, item_factors, precision=highest, preferred_element_type=jnp.float32)


def body(ratings, presence, user_factors, item_factors, step_sizes):
    row_counts = jnp.repeat(jnp.sum(presence, axis=1).astype(jnp.float32), BLK)
    col_counts = jnp.repeat(jnp.sum(presence, axis=0).astype(jnp.float32), BLK)
    users = user_factors
    partial_value = user_partial(ratings, presence, users, item_factors)
    share = users.shape[0] // lax.axis_size("item")
    start = lax.axis_index("item") * share
    summed, counts = sent_together((partial_value, row_counts), "item", 0, 1)
    scaling = step_sizes[0] / (BLK * (1.0 + counts))
    owned = lax.dynamic_slice_in_dim(users, start, share, 0) + summed * scaling[:, None]
    users = gathered_copies(owned, "item", 0)
    partial_value = user_partial(ratings, presence, users, item_factors)
    summed = sent_and_summed(partial_value, "item", 0)
    owned = owned + summed * scaling[:, None]
    users = gathered_copies(owned, "item", 0)
    resid = residual(ratings, presence, users, item_factors)
    item_part = lax.dot_general(
        resid,
        users,
        (((0,), (0,)), ((), ())),
        precision=highest,
        preferred_element_type=jnp.float32,
    )
    share = item_factors.shape[0] // lax.axis_size("user")
    start = lax.axis_index("user") * share
    summed, counts = sent_together((item_part, col_counts), "user", 0, 1)
    scaling = step_sizes[1] / (BLK * (1.0 + counts))
    owned = lax.dynamic_slice_in_dim(item_factors, start, share, 0) + summed * scaling[:, None]
    new_items = gathered_copies(owned, "user", 0)
    return (users, new_items)


def solution(mesh):
    return jax.shard_map(
        body,
        mesh=mesh,
        in_specs=(P("user", "item"), P("user", "item"), P("user", None), P("item", None), P()),
        out_specs=(P("user", None), P("item", None)),
        check_vma=False,
    )
```

profile of v0, /device:TPU:1, one launch (start us, length us, event | category | flops | bytes accessed | tf_op | source)
XLA Modules:
  0.0 186.2 jit_solution(1907288162072941377)
XLA Ops:
  0.6 0.0 copy-start
  0.6 0.9 fusion.18
  1.6 0.1 broadcast_in_dim.10
  1.6 1.0 concatenate.19
  2.6 0.0 copy-done
  2.6 0.0 copy-start.2
  2.7 5.1 %fusion.20 = f32[768,1536]{1,0:T(8,128)S(1)} fusion(f32[768,128]{1,0:T(8,128)} %param.7, f32[1536,128]{1,0:T(8,128)S(1)} %copy-done), kind=kOutput, calls=%fused_computation.30 | convolution fusion | flops 1811939328 | bytes 5898240 | tf_op jit(solution)/shard_map/dot_general | solution.py:56
  7.8 0.5 mul.72
  8.2 0.0 copy-start.1
  8.3 0.0 copy-done.2
  8.3 0.0 copy-start.4
  8.3 0.0 copy-start.6
  8.3 5.1 %fusion.1 = f32[768,128]{1,0:T(8,128)S(1)} fusion(f32[1536,128]{1,0:T(8,128)S(1)} %copy-done, f32[768,1536]{1,0:T(8,128)S(1)} %fusion.20, bf16[768,1536]{1,0:T(8,128)(2,1)S(1)} %copy-done.2, f32[96,8,12,128]{3,2,1,0:T(8,128)S(1)} %bitcast.36), kind=kOutput, calls=%fused_computation.4 | convolution fusion | flops 1815478272 | bytes 12976128 | tf_op jit(solution)/shard_map/dot_general | solution.py:73
  13.4 0.0 copy-done.1
  13.4 0.0 copy-done.4
  13.4 0.9 pad_maximum_fusion.1
  14.4 10.1 %all-to-all-start = ((f32[16,48,129]{2,1,0:T(8,128)}), f32[16,48,129]{2,1,0:T(8,128)}, u32[]{:S(2)}, u32[]{:S(2)}) async-start(f32[16,48,129]{2,1,0:T(8,128)} %pad_maximum_fusion.1), calls=%async_computation | async-start | bytes 1572864 | tf_op jit(solution)/shard_map/all_to_all | solution.py:22
  24.5 0.0 copy-done.6
  24.5 0.6 fusion.19
  25.0 20.2 %all-to-all-done = f32[16,48,129]{2,1,0:T(8,128)} async-done(((f32[16,48,129]{2,1,0:T(8,128)}), f32[16,48,129]{2,1,0:T(8,128)}, u32[]{:S(2)}, u32[]{:S(2)}) %all-to-all-start) | async-done | bytes 396320 | tf_op jit(solution)/shard_map/all_to_all | solution.py:22
  45.3 1.2 reduce_sum.46
  46.5 0.8 fusion.14
  47.2 0.8 fusion.13
  48.0 0.0 copy-start.5
  48.0 0.6 copy-done.5
  48.7 18.6 %all_to_all.30 = f32[16,48,128]{2,1,0:T(8,128)S(1)} all-to-all(f32[16,48,128]{2,1,0:T(8,128)S(1)} %broadcast_in_dim.11), channel_id=1, replica_groups=mesh['user'=16,'item'=16] {'item'}, dimensions={0} | all-to-all | bytes 786432 | tf_op jit(solution)/shard_map/all_to_all | solution.py:46
  67.3 8.0 %fusion.3 = f32[768,1536]{1,0:T(8,128)S(1)} fusion(bf16[768,1536]{1,0:T(8,128)(2,1)S(1)} %copy-done.2, f32[768,128]{1,0:T(8,128)S(1)} %bitcast.45, f32[1536,128]{1,0:T(8,128)S(1)} %copy-done, f32[96,8,12,128]{3,2,1,0:T(8,128)} %bitcast.37), kind=kOutput, calls=%fused_computation.5 | convolution fusion | flops 1815478272 | bytes 12976128 | tf_op jit(solution)/shard_map/dot_general | solution.py:56
  75.2 3.8 %fusion.8 = f32[16,48,128]{2,1,0:T(8,128)S(1)} fusion(f32[16,48,1536]{2,1,0:T(8,128)S(1)} %bitcast.39, f32[1536,128]{1,0:T(8,128)S(1)} %copy-done), kind=kOutput, calls=%fused_computation.12 | convolution fusion | flops 1811939328 | bytes 5898240 | tf_op jit(solution)/shard_map/dot_general | solution.py:73
  79.1 17.3 %all_to_all.31 = f32[16,48,128]{2,1,0:T(8,128)} all-to-all(f32[16,48,128]{2,1,0:T(8,128)S(1)} %fusion.8), channel_id=1, replica_groups=mesh['user'=16,'item'=16] {'item'}, dimensions={0} | all-to-all | bytes 786432 | tf_op jit(solution)/shard_map/all_to_all | solution.py:22
  96.4 1.0 reduce_sum.47
  97.4 0.8 multiply_add_fusion
  98.2 0.8 broadcast_in_dim.12
  99.0 4.2 %all-to-all-start.3 = ((f32[16,48,128]{2,1,0:T(8,128)}), f32[16,48,128]{2,1,0:T(8,128)S(1)}, u32[]{:S(2)}, u32[]{:S(2)}) async-start(f32[16,48,128]{2,1,0:T(8,128)} %broadcast_in_dim.12), calls=%async_computation.3 | async-start | bytes 786432 | tf_op jit(solution)/shard_map/all_to_all | solution.py:46
  103.3 0.1 broadcast_in_dim.13
  103.3 1.5 concatenate.20
  104.8 11.3 %all-to-all-done.3 = f32[16,48,128]{2,1,0:T(8,128)S(1)} async-done(((f32[16,48,128]{2,1,0:T(8,128)}), f32[16,48,128]{2,1,0:T(8,128)S(1)}, u32[]{:S(2)}, u32[]{:S(2)}) %all-to-all-start.3) | async-done | bytes 393248 | tf_op jit(solution)/shard_map/all_to_all | solution.py:46
  116.1 9.2 %fusion.5 = f32[1536,768]{0,1:T(8,128)} fusion(bf16[768,1536]{1,0:T(8,128)(2,1)S(1)} %copy-done.2, f32[768,128]{1,0:T(8,128)S(1)} %bitcast.41, f32[1536,128]{1,0:T(8,128)S(1)} %copy-done, f32[96,8,12,128]{3,2,1,0:T(8,128)} %bitcast.38), kind=kOutput, calls=%fused_computation.7 | convolution fusion | flops 1815478272 | bytes 12976128 | tf_op jit(solution)/shard_map/dot_general | solution.py:56
  125.3 6.0 %copy.17 = f32[1536,768]{1,0:T(8,128)} copy(f32[1536,768]{0,1:T(8,128)} %fusion.5) | data formatting | bytes 9437184 | tf_op jit(solution)/shard_map/dot_general | solution.py:92
  131.3 0.0 copy-start.3
  131.3 5.8 %fusion.21 = f32[16,96,128]{2,1,0:T(8,128)S(1)} fusion(f32[16,96,768]{2,1,0:T(8,128)} %bitcast.40, f32[768,128,1]{1,0,2:T(8,128)S(1)} %bitcast.42), kind=kOutput, calls=%fused_computation.31 | convolution fusion | flops 1811939328 | bytes 5898240 | tf_op jit(solution)/shard_map/dot_general | solution.py:92
  137.1 0.0 copy-done.3
  137.1 0.1 pad_maximum_fusion
  137.2 1.5 copy.19
  138.8 9.4 %all-to-all-start.4 = ((f32[16,96,129]{1,2,0:T(8,128)}), f32[16,96,129]{1,2,0:T(8,128)S(1)}, u32[]{:S(2)}, u32[]{:S(2)}) async-start(f32[16,96,129]{1,2,0:T(8,128)} %copy.19), calls=%async_computation.4 | async-start | bytes 2228224 | tf_op jit(solution)/shard_map/all_to_all | solution.py:22
  148.2 0.1 copy.21
  148.3 17.7 %all-to-all-done.4 = f32[16,96,129]{1,2,0:T(8,128)S(1)} async-done(((f32[16,96,129]{1,2,0:T(8,128)}), f32[16,96,129]{1,2,0:T(8,128)S(1)}, u32[]{:S(2)}, u32[]{:S(2)}) %all-to-all-start.4) | async-done | bytes 792608 | tf_op jit(solution)/shard_map/all_to_all | solution.py:22
  166.0 0.1 reduce_sum.49
  166.0 0.5 fusion.17
  166.6 0.1 copy.20
  166.7 0.1 broadcast_in_dim.14
  166.8 17.8 %all_to_all.32 = f32[16,96,128]{2,1,0:T(8,128)S(1)} all-to-all(f32[16,96,128]{2,1,0:T(8,128)S(1)} %broadcast_in_dim.14), channel_id=1, replica_groups=mesh['user'=16,'item'=16] {'user'}, dimensions={0} | all-to-all | bytes 1572864 | tf_op jit(solution)/shard_map/all_to_all | solution.py:46
  184.6 0.7 copy.31
  185.3 0.9 copy.32
  (5 shorter events, 0.1 us)
Async XLA Ops:
  0.6 2.0 %copy-start = (f32[1536,128]{1,0:T(8,128)S(1)}, f32[1536,128]{1,0:T(8,128)}, u32[]{:S(2)}) copy-start(f32[1536,128]{1,0:T(8,128)} %param.8) | copy-start | bytes 2359300
  2.6 5.6 %copy-start.2 = (bf16[768,1536]{1,0:T(8,128)(2,1)S(1)}, bf16[768,1536]{1,0:T(8,128)(2,1)}, u32[]{:S(2)}) copy-start(bf16[768,1536]{1,0:T(8,128)(2,1)} %param.5) | copy-start | bytes 7077892
  8.2 5.2 %copy-start.1 = (f32[6,128,12,128]{3,2,1,0:T(8,128)}, f32[6,128,12,128]{3,2,1,0:T(8,128)S(1)}, u32[]{:S(2)}) copy-start(f32[6,128,12,128]{3,2,1,0:T(8,128)S(1)} %mul.72) | copy-start | bytes 14155780
  8.3 5.2 %copy-start.4 = (f32[16,48,1]{2,1,0:T(8,128)S(1)}, f32[16,48,1]{2,1,0:T(8,128)}, u32[]{:S(2)}) copy-start(f32[16,48,1]{2,1,0:T(8,128)} %concatenate.19) | copy-start | bytes 9220
  8.3 16.2 %copy-start.6 = (f32[2]{0:T(128)S(1)}, f32[2]{0:T(128)}, u32[]{:S(2)}) copy-start(f32[2]{0:T(128)} %param.9) | copy-start | bytes 28
  14.4 30.9 %all-to-all-start = ((f32[16,48,129]{2,1,0:T(8,128)}), f32[16,48,129]{2,1,0:T(8,128)}, u32[]{:S(2)}, u32[]{:S(2)}) async-start(f32[16,48,129]{2,1,0:T(8,128)} %pad_maximum_fusion.1), calls=%async_computation | async-start | bytes 1572864 | tf_op jit(solution)/shard_map/all_to_all | solution.py:22
  48.0 0.6 copy-start.5
  99.0 17.1 %all-to-all-start.3 = ((f32[16,48,128]{2,1,0:T(8,128)}), f32[16,48,128]{2,1,0:T(8,128)S(1)}, u32[]{:S(2)}, u32[]{:S(2)}) async-start(f32[16,48,128]{2,1,0:T(8,128)} %broadcast_in_dim.12), calls=%async_computation.3 | async-start | bytes 786432 | tf_op jit(solution)/shard_map/all_to_all | solution.py:46
  131.3 5.8 %copy-start.3 = (f32[16,96,1]{2,1,0:T(8,128)S(1)}, f32[16,96,1]{2,1,0:T(8,128)}, u32[]{:S(2)}) copy-start(f32[16,96,1]{2,1,0:T(8,128)} %concatenate.20) | copy-start | bytes 18436
  138.8 27.2 %all-to-all-start.4 = ((f32[16,96,129]{1,2,0:T(8,128)}), f32[16,96,129]{1,2,0:T(8,128)S(1)}, u32[]{:S(2)}, u32[]{:S(2)}) async-start(f32[16,96,129]{1,2,0:T(8,128)} %copy.19), calls=%async_computation.4 | async-start | bytes 2228224 | tf_op jit(solution)/shard_map/all_to_all | solution.py:22
where the time goes:
time: 187 us; the launch traced here: 186 us
  blocking collectives  53.7 us (29%)
  waiting for transfers between devices  49.2 us (26%)
  matrix products  37 us (20%)
  starting transfers between devices  23.7 us (13%)
  local copies, waits for them, and re-layouts  14.6 us (8%)
  other arithmetic  7.21 us (4%)
    all_to_all x2, waiting for transfers between devices, sent_and_summed(): lax.all_to_all(pieces, axis, split_axis=0, concat_axis=0, tiled=True)  37.9 us
    all_to_all x2, blocking collectives, sent_to_all(): lax.all_to_all(jnp.broadcast_to(shard[None], (devices, *shard.shape)), ax...  36.4 us
    dot_general x3, matrix products, residual(): lax.dot_general(users, item_factors, (((1,), (1,)), ((), ())), precision=...  22.3 us
    all_to_all x2, starting transfers between devices, sent_and_summed(): lax.all_to_all(pieces, axis, split_axis=0, concat_axis=0, tiled=True)  19.5 us
    all_to_all x1, blocking collectives, sent_and_summed(): lax.all_to_all(pieces, axis, split_axis=0, concat_axis=0, tiled=True)  17.3 us
    all_to_all x1, waiting for transfers between devices, sent_to_all(): lax.all_to_all(jnp.broadcast_to(shard[None], (devices, *shard.shape)), ax...  11.3 us
    dot_general x2, matrix products, user_partial(): jnp.dot(resid, item_factors, precision=highest, preferred_element_type=jn...  8.92 us
    dot_general x1, local copies, waits for them, and re-layouts, body(): lax.dot_general(resid, users, (((0,), (0,)), ((), ())), precision=highest...  6.04 us
  transfers between devices with their start and end apart: 3, of which 3 were waited for; matrix products, arithmetic and copies ran while one was open for 1% of the time, Pallas kernels for 0%

commit v1 on v0

v1 whole, which is shorter than its diff:
```python
import jax
import jax.numpy as jnp
from jax import lax
from jax.experimental import pallas as pl
from jax.experimental.pallas import tpu as pltpu
from jax.sharding import PartitionSpec as P

BLK = 128
UB = 6
IB = 12
USERS = UB * BLK
ITEMS = IB * BLK
PIECES = 16
ROWS = USERS // PIECES
HROWS = UB * 64 // PIECES
PIECE = ROWS + HROWS + 8
CHUNK = ITEMS // 16
F32 = jnp.float32
BF16 = jnp.bfloat16
VMEM = pl.BlockSpec(memory_space=pltpu.VMEM)
SMEM = pl.BlockSpec(memory_space=pltpu.SMEM)
ANY = pl.BlockSpec(memory_space=pl.ANY)


def split(value):
    high = value.astype(BF16)
    low = (value - high.astype(F32)).astype(BF16)
    return jnp.concatenate([high, low], axis=1)


def gram(both):
    square = lax.dot_general(both, both, (((0,), (0,)), ((), ())), preferred_element_type=F32)
    return (square[:BLK, :BLK] + square[BLK:, BLK:]) + (square[:BLK, BLK:] + square[BLK:, :BLK])


def exact(a, b, dims):
    return lax.dot_general(a, b, (dims, ((), ())), precision=lax.Precision.HIGHEST, preferred_element_type=F32)


def lanes(shape):
    return lax.broadcasted_iota(jnp.int32, shape, 1)


def sublanes(shape):
    return lax.broadcasted_iota(jnp.int32, shape, 0)


def fetch_ratings(r_hbm, r_vmem, sem):
    copies = []
    for b in range(UB):
        rows = pl.ds(b * BLK, BLK)
        copies.append(pltpu.make_async_copy(r_hbm.at[rows], r_vmem.at[rows], sem.at[b]))
        copies[-1].start()
    return copies


def user_kernel(m_ref, r_hbm, p_ref, q_ref, x_ref, r_vmem, qcat, grams, packed, sem):
    copies = fetch_ratings(r_hbm, r_vmem, sem)
    for j in range(IB):
        rows = slice(j * BLK, (j + 1) * BLK)
        both = split(q_ref[rows])
        qcat[rows] = both
        grams[j] = gram(both)
    row64, lane64 = sublanes((64, BLK)), lanes((64, BLK))
    extra_row = sublanes((8, BLK))
    extra_lane = lanes((8, BLK))
    extra = jnp.zeros((8, BLK), F32)
    for b in range(UB):
        h = jnp.zeros((BLK, BLK), F32)
        count = jnp.int32(0)
        for j in range(IB):
            h = h + m_ref[b, j].astype(F32) * grams[j]
            count = count + m_ref[b, j]
        turned = jnp.concatenate([h[64:, 64:], h[64:, :64]], axis=1)
        packed[b * 64 : (b + 1) * 64] = jnp.where((lane64 < 64) & (lane64 > row64), turned, h[:64])
        diagonal = jnp.sum(jnp.where(lane64 == row64 + 64, h[64:], 0.0), axis=0, keepdims=True)
        extra = extra + jnp.where(extra_row == b, jnp.broadcast_to(diagonal, (8, BLK)), 0.0)
        extra = extra + jnp.where((extra_row == 6) & (extra_lane == b), count.astype(F32), 0.0)
        copies[b].wait()
        rows = slice(b * BLK, (b + 1) * BLK)
        masked = jnp.concatenate(
            [r_vmem[rows, j * BLK : (j + 1) * BLK] * m_ref[b, j].astype(F32).astype(BF16) for j in range(IB)],
            axis=1,
        )
        found = jnp.dot(masked, qcat[...], preferred_element_type=F32)
        d = found[:, :BLK] + found[:, BLK:] - exact(p_ref[rows], h, ((1,), (0,)))
        for k in range(0, BLK, 16):
            piece, at = divmod(b * BLK + k, ROWS)
            x_ref[piece, at : at + 16] = d[k : k + 16]
    for piece in range(PIECES):
        x_ref[piece, ROWS : ROWS + HROWS] = packed[piece * HROWS : (piece + 1) * HROWS]
        x_ref[piece, ROWS + HROWS :] = extra if piece == 0 else jnp.zeros((8, BLK), F32)


def total_kernel(y_ref, z_ref):
    total = y_ref[0]
    for k in range(1, PIECES):
        total = total + y_ref[k]
    for k in range(PIECES):
        z_ref[k] = total


def item_kernel(
    m_ref, step_ref, core_ref, r_hbm, p_ref, q_ref, z_ref, new_ref, own_ref, other_ref, r_vmem, pcat, grams, grads, sem
):
    copies = fetch_ratings(r_hbm, r_vmem, sem)
    extra = z_ref[0, ROWS + HROWS :]
    scales = step_ref[0] / (BLK * (1.0 + extra[6:7]))
    row64, lane64 = sublanes((64, BLK)), lanes((64, BLK))
    for b in range(UB):
        rows = slice(b * BLK, (b + 1) * BLK)
        tiles = []
        for k in range(0, BLK, 16):
            piece, at = divmod(b * BLK + k, ROWS)
            tiles.append(z_ref[piece, at : at + 16])
        d = jnp.concatenate(tiles, axis=0)
        tiles = []
        for k in range(0, 64, 8):
            piece, at = divmod(b * 64 + k, HROWS)
            tiles.append(z_ref[piece, ROWS + at : ROWS + at + 8])
        half = jnp.concatenate(tiles, axis=0)
        turned = jnp.concatenate([half[:, 64:], half[:, :64]], axis=1)
        top = jnp.where(lane64 < row64, half, jnp.where(lane64 == row64, 0.5 * half, 0.0))
        top = jnp.where(lane64 >= 64, half, top)
        bottom = jnp.where(lane64 > row64 + 64, turned, 0.0)
        bottom = jnp.where(lane64 == row64 + 64, 0.5 * extra[b : b + 1], bottom)
        w = jnp.concatenate([top, bottom], axis=0)
        dh = exact(d, w, ((1,), (0,))) + exact(d, w, ((1,), (1,)))
        s = scales[:, b : b + 1]
        new = p_ref[rows] + (2.0 * s) * d - (s * s) * dh
        new_ref[rows] = new
        both = split(new)
        pcat[rows] = both
        grams[b] = gram(both)
    for b in range(UB):
        copies[b].wait()
        rows = slice(b * BLK, (b + 1) * BLK)
        for j in range(IB):
            columns = slice(j * BLK, (j + 1) * BLK)
            r_vmem[rows, columns] = r_vmem[rows, columns] * m_ref[b, j].astype(F32).astype(BF16)
    counts = jnp.zeros((8, BLK), F32)
    lane8 = lanes((8, BLK))
    for j in range(IB):
        columns = slice(j * BLK, (j + 1) * BLK)
        s = jnp.zeros((BLK, BLK), F32)
        count = jnp.int32(0)
        for b in range(UB):
            s = s + m_ref[b, j].astype(F32) * grams[b]
            count = count + m_ref[b, j]
        counts = counts + jnp.where(lane8 == j, count.astype(F32), 0.0)
        found = lax.dot_general(
            pcat[...], r_vmem[:, columns], (((0,), (0,)), ((), ())), preferred_element_type=F32
        )
        grads[columns] = (found[:BLK] + found[BLK:]).T - exact(q_ref[columns], s, ((1,), (0,)))
    core = core_ref[0]
    for k in range(8):
        own_ref[k, :CHUNK] = grads[pl.ds(pl.multiple_of(k * 2 * CHUNK + core * CHUNK, 8), CHUNK)]
        other_ref[k, :CHUNK] = grads[pl.ds(pl.multiple_of(k * 2 * CHUNK + (1 - core) * CHUNK, 8), CHUNK)]
        own_ref[k, CHUNK:] = counts
        other_ref[k, CHUNK:] = counts


def scale_kernel(step_ref, user_ref, v_ref, q_ref, o_ref):
    total = v_ref[0]
    for k in range(1, 8):
        total = total + v_ref[k]
    scales = step_ref[1] / (BLK * (1.0 + total[CHUNK : CHUNK + 1]))
    lane1 = lanes((1, BLK))
    for k in range(3):
        block = (user_ref[0] * 3 + k) // 4
        t = jnp.sum(jnp.where(lane1 == block, scales, 0.0), axis=1, keepdims=True)
        start = pl.multiple_of(user_ref[0] * CHUNK + k * 32, 8)
        o_ref[k * 32 : (k + 1) * 32] = q_ref[pl.ds(start, 32)] + t * total[k * 32 : (k + 1) * 32]


def spread_kernel(core_ref, own_ref, other_ref, o_ref):
    core = core_ref[0]
    for k in range(8):
        o_ref[k, pl.ds(pl.multiple_of(core * CHUNK, 8), CHUNK)] = own_ref[...]
        o_ref[k, pl.ds(pl.multiple_of((1 - core) * CHUNK, 8), CHUNK)] = other_ref[...]


def call(kernel, out_shapes, specs, scratch=(), single=True):
    shapes = [jax.ShapeDtypeStruct(s, F32) for s in out_shapes]
    return pl.pallas_call(
        kernel,
        out_shape=shapes[0] if single else shapes,
        in_specs=specs,
        out_specs=VMEM if single else [VMEM] * len(shapes),
        scratch_shapes=scratch,
    )


def body(ratings, presence, user_factors, item_factors, step_sizes):
    user = lax.axis_index("user")
    core = lax.rem(user, 2)
    user1, core1 = user.reshape(1), core.reshape(1)
    swap = [(k, k ^ 1) for k in range(16)]
    chips = [[k + 2 * j for j in range(8)] for k in range(2)]
    x = call(
        user_kernel,
        [(PIECES, PIECE, BLK)],
        [SMEM, ANY, VMEM, VMEM],
        [
            pltpu.VMEM((USERS, ITEMS), BF16),
            pltpu.VMEM((ITEMS, 2 * BLK), BF16),
            pltpu.VMEM((IB, BLK, BLK), F32),
            pltpu.VMEM((UB * 64, BLK), F32),
            pltpu.SemaphoreType.DMA((UB,)),
        ],
    )(presence, ratings, user_factors, item_factors)
    y = lax.all_to_all(x, "item", 0, 0, tiled=True)
    z = call(total_kernel, [(PIECES, PIECE, BLK)], [VMEM])(y)
    z = lax.all_to_all(z, "item", 0, 0, tiled=True)
    new_users, own, other = call(
        item_kernel,
        [(USERS, BLK), (8, CHUNK + 8, BLK), (8, CHUNK + 8, BLK)],
        [SMEM, SMEM, SMEM, ANY, VMEM, VMEM, VMEM],
        [
            pltpu.VMEM((USERS, ITEMS), BF16),
            pltpu.VMEM((USERS, 2 * BLK), BF16),
            pltpu.VMEM((UB, BLK, BLK), F32),
            pltpu.VMEM((ITEMS, BLK), F32),
            pltpu.SemaphoreType.DMA((UB,)),
        ],
        single=False,
    )(presence, step_sizes, core1, ratings, user_factors, item_factors, z)
    v = own + lax.ppermute(other, "user", swap)
    v = lax.all_to_all(v, "user", 0, 0, tiled=True, axis_index_groups=chips)
    owned = call(scale_kernel, [(CHUNK, BLK)], [SMEM, SMEM, VMEM, VMEM])(step_sizes, user1, v, item_factors)
    partner = lax.ppermute(owned, "user", swap)
    w = call(spread_kernel, [(8, 2 * CHUNK, BLK)], [SMEM, VMEM, VMEM])(core1, owned, partner)
    w = lax.all_to_all(w, "user", 0, 0, tiled=True, axis_index_groups=chips)
    return new_users, w.reshape(ITEMS, BLK)


def solution(mesh):
    return jax.shard_map(
        body,
        mesh=mesh,
        in_specs=(P("user", "item"), P("user", "item"), P("user", None), P("item", None), P()),
        out_specs=(P("user", None), P("item", None)),
        check_vma=False,
    )
```

time: 187 us -> 117 us (0.63)
  matrix products: 37 us -> 0 us
  waiting for transfers between devices: 49.2 us -> 19.7 us
  Pallas kernels: 0 us -> 20.1 us
  starting transfers between devices: 23.7 us -> 9.34 us
  local copies, waits for them, and re-layouts: 14.6 us -> 2.33 us
  blocking collectives: 53.7 us -> 63.6 us
  other arithmetic: 7.21 us -> 1.07 us
    dot_general x6 -> x0, matrix products: 37 us -> none  [the longest x3 22.3 us: residual(): lax.dot_general(users, item_factors, (((1,), (1,)), ((), ())), precision=...]
    all_to_all x3 -> x1, waiting for transfers between devices: 49.2 us -> 17 us  [body(): z = lax.all_to_all(z, 'item', 0, 0, tiled=True)]
    all_to_all x3 -> x1, starting transfers between devices: 23.7 us -> 3.59 us  [body(): z = lax.all_to_all(z, 'item', 0, 0, tiled=True)]
    pallas_call x0 -> x5, Pallas kernels: none -> 20.1 us  [the longest x1 8.71 us: body(): call(item_kernel, [(USERS, BLK), (8, CHUNK + 8, BLK), (8, CHUNK + 8, BLK)...]
    all_to_all x3, blocking collectives: 53.7 us -> 63.6 us  [the longest x1 29.8 us: body(): y = lax.all_to_all(x, 'item', 0, 0, tiled=True)]
    dot_general x1 -> x0, local copies, waits for them, and re-layouts: 6.04 us -> none  [body(): lax.dot_general(resid, users, (((0,), (0,)), ((), ())), precision=highest...]
    ppermute x0 -> x2, starting transfers between devices: none -> 5.75 us  [the longest x1 4.16 us: body(): v = own + lax.ppermute(other, 'user', swap)]
    concatenate x3 -> x0, local copies, waits for them, and re-layouts: 4.05 us -> none  [sent_together(): jnp.concatenate([a.reshape(*a.shape[:along], w) for a, w in zip(arrays, w...]
  transfers between devices with their start and end apart: 3 -> 3, of which waited for: 3 -> 3; matrix products, arithmetic and copies ran while one was open for 1% -> 0% of each run, Pallas kernels for 0% -> 0%
where the time goes in v1:
time: 117 us
  blocking collectives  63.6 us (54%)
  Pallas kernels  20.1 us (17%)
  waiting for transfers between devices  19.7 us (17%)
  starting transfers between devices  9.34 us (8%)
  local copies, waits for them, and re-layouts  2.33 us (2%)
    all_to_all x1, blocking collectives, body(): y = lax.all_to_all(x, 'item', 0, 0, tiled=True)  29.8 us
    all_to_all x1, blocking collectives, body(): w = lax.all_to_all(w, 'user', 0, 0, tiled=True, axis_index_groups=chips)  17.6 us
    all_to_all x1, waiting for transfers between devices, body(): z = lax.all_to_all(z, 'item', 0, 0, tiled=True)  17 us
    all_to_all x1, blocking collectives, body(): v = lax.all_to_all(v, 'user', 0, 0, tiled=True, axis_index_groups=chips)  16.2 us
    pallas_call x1, Pallas kernels, body(): call(item_kernel, [(USERS, BLK), (8, CHUNK + 8, BLK), (8, CHUNK + 8, BLK)...  8.71 us
    pallas_call x1, Pallas kernels, body(): call(user_kernel, [(PIECES, PIECE, BLK)], [SMEM, ANY, VMEM, VMEM], [pltpu...  5.69 us
    ppermute x1, starting transfers between devices, body(): v = own + lax.ppermute(other, 'user', swap)  4.16 us
    all_to_all x1, starting transfers between devices, body(): z = lax.all_to_all(z, 'item', 0, 0, tiled=True)  3.59 us
  transfers between devices with their start and end apart: 3, of which 3 were waited for; matrix products, arithmetic and copies ran while one was open for 0% of the time, Pallas kernels for 0%

profile of v1, /device:TPU:1, one launch (start us, length us, event | category | flops | bytes accessed | tf_op | source)
XLA Modules:
  0.0 116.9 jit_solution(17350349377433232533)
XLA Ops:
  0.6 5.7 %shard_map.68 = f32[16,80,128]{2,1,0:T(8,128)} custom-call(s32[6,12]{1,0:T(8,128)} %m_ref.3, bf16[768,1536]{1,0:T(8,128)(2,1)} %r_hbm.3, f32[768,128]{1,0:T(8,128)} %p_ref.3, f32[1536,128]{1,0:T(8,128)} %q_ref.5), custom_call_target="tpu_custom_call" | custom-call | tf_op jit(solution)/shard_map/pallas_call | solution.py:200
  6.3 29.8 %all_to_all.20.y_ref = f32[16,80,128]{2,1,0:T(8,128)} all-to-all(f32[16,80,128]{2,1,0:T(8,128)} %shard_map.68), channel_id=1, replica_groups=mesh['user'=16,'item'=16] {'item'}, dimensions={0} | all-to-all | bytes 1310720 | tf_op jit(solution)/shard_map/all_to_all | solution.py:212
  36.1 2.0 %shard_map.69 = f32[16,80,128]{2,1,0:T(8,128)} custom-call(f32[16,80,128]{2,1,0:T(8,128)} %all_to_all.20.y_ref), custom_call_target="tpu_custom_call" | custom-call | tf_op jit(solution)/shard_map/pallas_call | solution.py:213
  38.1 3.6 %all-to-all-start.1 = ((f32[16,80,128]{2,1,0:T(8,128)}), f32[16,80,128]{2,1,0:T(8,128)S(1)}, u32[]{:S(2)}, u32[]{:S(2)}) async-start(f32[16,80,128]{2,1,0:T(8,128)} %shard_map.69), calls=%async_computation.1 | async-start | bytes 1310720 | tf_op jit(solution)/shard_map/all_to_all | solution.py:214
  41.7 17.0 %all-to-all-done.1.z_ref = f32[16,80,128]{2,1,0:T(8,128)S(1)} async-done(((f32[16,80,128]{2,1,0:T(8,128)}), f32[16,80,128]{2,1,0:T(8,128)S(1)}, u32[]{:S(2)}, u32[]{:S(2)}) %all-to-all-start.1) | async-done | bytes 655392 | tf_op jit(solution)/shard_map/all_to_all | solution.py:214
  58.7 0.0 copy-start
  58.7 0.8 copy-done
  59.5 8.7 %shard_map.70 = (f32[768,128]{1,0:T(8,128)}, f32[8,104,128]{2,1,0:T(8,128)}, f32[8,104,128]{2,1,0:T(8,128)}) custom-call(s32[6,12]{1,0:T(8,128)} %m_ref.3, f32[2]{0:T(128)} %step_ref.3, s32[1]{0:T(128)} %bitcast.core_ref, bf16[768,1536]{1,0:T(8,128)(2,1)} %r_hbm.3, f32[768,128]{1,0:T(8,128)} %p_ref.3, f32[1536,128]{1,0:T(8,128)} %q_ref.5, f32[16,80,128]{2,1,0:T(8,128)} %copy-done), custom_call_target="tpu_custom_call" | custom-call | tf_op jit(solution)/shard_map/pallas_call | solution.py:215
  68.3 4.2 %collective-permute-start = (f32[8,104,128]{2,1,0:T(8,128)}, f32[8,104,128]{2,1,0:T(8,128)S(1)}, u32[]{:S(2)}, u32[]{:S(2)}) collective-permute-start(f32[8,104,128]{2,1,0:T(8,128)} %get-tuple-element.7), channel_id=1, source_target_pairs={{0,16},{16,0},{32,48},{48,32},{64,80},{80,64},{96,112},{112,96},{1... | collective-permute-start | bytes 1277960 | tf_op jit(solution)/shard_map/ppermute | solution.py:228
  72.4 1.6 %collective-permute-done = f32[8,104,128]{2,1,0:T(8,128)S(1)} collective-permute-done((f32[8,104,128]{2,1,0:T(8,128)}, f32[8,104,128]{2,1,0:T(8,128)S(1)}, u32[]{:S(2)}, u32[]{:S(2)}) %collective-permute-start) | collective-permute-done | bytes 426016 | tf_op jit(solution)/shard_map/ppermute | solution.py:228
  74.0 1.1 add.3
  75.1 16.2 %all_to_all.21.v_ref = f32[8,104,128]{2,1,0:T(8,128)} all-to-all(f32[8,104,128]{2,1,0:T(8,128)S(1)} %add.3), channel_id=1, replica_groups={{0,32,64,96,128,160,192,224},{16,48,80,112,144,176,208,240},{1,33,65,97..., dimensions={0} | all-to-all | bytes 851968 | tf_op jit(solution)/shard_map/all_to_all | solution.py:229
  91.3 2.0 %shard_map.71.own_ref = f32[96,128]{1,0:T(8,128)} custom-call(f32[2]{0:T(128)} %step_ref.3, s32[1]{0:T(128)} %bitcast.1.user_ref, f32[8,104,128]{2,1,0:T(8,128)} %all_to_all.21.v_ref, f32[1536,128]{1,0:T(8,128)} %q_ref.5), custom_call_target="tpu_custom_call" | custom-call | tf_op jit(solution)/shard_map/pallas_call | solution.py:230
  93.3 1.6 %collective-permute-start.1 = (f32[96,128]{1,0:T(8,128)}, f32[96,128]{1,0:T(8,128)S(1)}, u32[]{:S(2)}, u32[]{:S(2)}) collective-permute-start(f32[96,128]{1,0:T(8,128)} %shard_map.71.own_ref), channel_id=1, source_target_pairs={{0,16},{16,0},{32,48},{48,32},{64,80},{80,64},{96,112},{112,96},{1... | collective-permute-start | bytes 147464 | tf_op jit(solution)/shard_map/ppermute | solution.py:231
  94.9 1.1 collective-permute-done.1.other_ref
  96.0 0.0 copy-start.1
  96.0 0.6 copy-done.1
  96.6 1.8 %shard_map.72 = f32[8,192,128]{2,1,0:T(8,128)} custom-call(s32[1]{0:T(128)} %bitcast.core_ref, f32[96,128]{1,0:T(8,128)} %shard_map.71.own_ref, f32[96,128]{1,0:T(8,128)} %copy-done.1), custom_call_target="tpu_custom_call" | custom-call | tf_op jit(solution)/shard_map/pallas_call | solution.py:232
  98.4 17.6 %all_to_all.22 = f32[8,192,128]{2,1,0:T(8,128)S(1)} all-to-all(f32[8,192,128]{2,1,0:T(8,128)} %shard_map.72), channel_id=1, replica_groups={{0,32,64,96,128,160,192,224},{16,48,80,112,144,176,208,240},{1,33,65,97..., dimensions={0} | all-to-all | bytes 1572864 | tf_op jit(solution)/shard_map/all_to_all | solution.py:233
  116.0 0.9 copy.8
Async XLA Ops:
  38.1 20.6 %all-to-all-start.1 = ((f32[16,80,128]{2,1,0:T(8,128)}), f32[16,80,128]{2,1,0:T(8,128)S(1)}, u32[]{:S(2)}, u32[]{:S(2)}) async-start(f32[16,80,128]{2,1,0:T(8,128)} %shard_map.69), calls=%async_computation.1 | async-start | bytes 1310720 | tf_op jit(solution)/shard_map/all_to_all | solution.py:214
  58.7 0.8 copy-start
  68.3 5.8 %collective-permute-start = (f32[8,104,128]{2,1,0:T(8,128)}, f32[8,104,128]{2,1,0:T(8,128)S(1)}, u32[]{:S(2)}, u32[]{:S(2)}) collective-permute-start(f32[8,104,128]{2,1,0:T(8,128)} %get-tuple-element.7), channel_id=1, source_target_pairs={{0,16},{16,0},{32,48},{48,32},{64,80},{80,64},{96,112},{112,96},{1... | collective-permute-start | bytes 1277960 | tf_op jit(solution)/shard_map/ppermute | solution.py:228
  93.3 2.7 %collective-permute-start.1 = (f32[96,128]{1,0:T(8,128)}, f32[96,128]{1,0:T(8,128)S(1)}, u32[]{:S(2)}, u32[]{:S(2)}) collective-permute-start(f32[96,128]{1,0:T(8,128)} %shard_map.71.own_ref), channel_id=1, source_target_pairs={{0,16},{16,0},{32,48},{48,32},{64,80},{80,64},{96,112},{112,96},{1... | collective-permute-start | bytes 147464 | tf_op jit(solution)/shard_map/ppermute | solution.py:231
  96.0 0.6 copy-start.1

commit v2 on v1

v2 whole, which is shorter than its diff:
```python
import jax
import jax.numpy as jnp
from jax import lax
from jax.experimental import pallas as pl
from jax.experimental.pallas import tpu as pltpu
from jax.sharding import PartitionSpec as P

BLK = 128
UB = 6
IB = 12
USERS = UB * BLK
ITEMS = IB * BLK
PIECES = 16
ROWS = USERS // PIECES
HROWS = UB * 64 // PIECES
PIECE = ROWS + HROWS + 8
CHUNK = ITEMS // 16
F32 = jnp.float32
BF16 = jnp.bfloat16
VMEM = pl.BlockSpec(memory_space=pltpu.VMEM)
SMEM = pl.BlockSpec(memory_space=pltpu.SMEM)
HBM = pl.BlockSpec(memory_space=pltpu.HBM)


def split(value, axis):
    high = value.astype(BF16)
    low = (value - high.astype(F32)).astype(BF16)
    return jnp.concatenate([high, low], axis=axis)


def halves(value):
    return value[:, :BLK] + value[:, BLK:]


def gram(both, turned):
    square = jnp.dot(turned, both, preferred_element_type=F32)
    return halves(square[:BLK] + square[BLK:])


def thirds(value):
    high = value.astype(BF16)
    rest = value - high.astype(F32)
    middle = rest.astype(BF16)
    return high, middle, (rest - middle.astype(F32)).astype(BF16)


def exact(a, b):
    ah, am, al = thirds(a)
    bh, bm, bl = thirds(b)
    left = jnp.concatenate([ah, am, ah, al], axis=1)
    near_zero = jnp.zeros_like(bl)
    right = jnp.concatenate(
        [
            jnp.concatenate([bh, bh, bl, bh], axis=0),
            jnp.concatenate([bm, bm, near_zero, near_zero], axis=0),
        ],
        axis=1,
    )
    return halves(jnp.dot(left, right, preferred_element_type=F32))


def lanes(shape):
    return lax.broadcasted_iota(jnp.int32, shape, 1)


def sublanes(shape):
    return lax.broadcasted_iota(jnp.int32, shape, 0)


def block(index):
    return slice(index * BLK, (index + 1) * BLK)


def present(m_ref, b, j):
    return m_ref[b, j].astype(F32)


def fetch_ratings(r_hbm, r_ref, sem):
    copies = []
    for b in range(UB):
        rows = pl.ds(b * BLK, BLK)
        copies.append(pltpu.make_async_copy(r_hbm.at[rows], r_ref.at[rows], sem.at[b]))
        copies[-1].start()
    return copies


def keep_present(m_ref, r_ref, b):
    for j in range(IB):
        r_ref[block(b), block(j)] = r_ref[block(b), block(j)] * present(m_ref, b, j).astype(BF16)


def user_kernel(m_ref, r_hbm, p_hbm, q_hbm, x_ref, r_ref, p_ref, q_ref, qcat, grams, packed, r_sem, q_sem, p_sem):
    q_copies = []
    for k in range(4):
        rows = pl.ds(k * 3 * BLK, 3 * BLK)
        q_copies.append(pltpu.make_async_copy(q_hbm.at[rows], q_ref.at[rows], q_sem.at[k]))
        q_copies[-1].start()
    r_copies = fetch_ratings(r_hbm, r_ref, r_sem)
    p_copy = pltpu.make_async_copy(p_hbm, p_ref, p_sem)
    p_copy.start()
    for j in range(IB):
        if j % 3 == 0:
            q_copies[j // 3].wait()
        q = q_ref[block(j)]
        both = split(q, 1)
        qcat[block(j)] = both
        grams[j] = gram(both, split(q.T, 0))
    row64, lane64 = sublanes((64, BLK)), lanes((64, BLK))
    extra_row, extra_lane = sublanes((8, BLK)), lanes((8, BLK))
    extra = jnp.zeros((8, BLK), F32)
    p_copy.wait()
    for half in range(2):
        three = range(half * 3, half * 3 + 3)
        corrections = []
        for b in three:
            h = jnp.zeros((BLK, BLK), F32)
            count = jnp.int32(0)
            for j in range(IB):
                h = h + present(m_ref, b, j) * grams[j]
                count = count + m_ref[b, j]
            turned = jnp.concatenate([h[64:, 64:], h[64:, :64]], axis=1)
            packed[b * 64 : (b + 1) * 64] = jnp.where((lane64 < 64) & (lane64 > row64), turned, h[:64])
            diagonal = jnp.sum(jnp.where(lane64 == row64 + 64, h[64:], 0.0), axis=0, keepdims=True)
            extra = extra + jnp.where(extra_row == b, jnp.broadcast_to(diagonal, (8, BLK)), 0.0)
            extra = extra + jnp.where((extra_row == 6) & (extra_lane == b), count.astype(F32), 0.0)
            corrections.append(exact(p_ref[block(b)], h))
            r_copies[b].wait()
            keep_present(m_ref, r_ref, b)
        found = halves(
            jnp.dot(r_ref[half * 3 * BLK : (half + 1) * 3 * BLK], qcat[...], preferred_element_type=F32)
        )
        d = found - jnp.concatenate(corrections, axis=0)
        for k in range(8):
            x_ref[half * 8 + k, :ROWS] = d[k * ROWS : (k + 1) * ROWS]
    for piece in range(PIECES):
        x_ref[piece, ROWS : ROWS + HROWS] = packed[piece * HROWS : (piece + 1) * HROWS]
        x_ref[piece, ROWS + HROWS :] = extra if piece == 0 else jnp.zeros((8, BLK), F32)


def total_kernel(y_ref, z_ref):
    total = y_ref[0]
    for k in range(1, PIECES):
        total = total + y_ref[k]
    for k in range(PIECES):
        z_ref[k] = total


def item_kernel(
    m_ref, step_ref, core_ref, r_hbm, p_ref, q_ref, z_ref, new_ref, own_ref, other_ref, r_ref, turned_ref, grams, grads, sem
):
    copies = fetch_ratings(r_hbm, r_ref, sem)
    extra = z_ref[0, ROWS + HROWS :]
    scales = step_ref[0] / (BLK * (1.0 + extra[6:7]))
    row64, lane64 = sublanes((64, BLK)), lanes((64, BLK))
    for b in range(UB):
        tiles = []
        for k in range(0, BLK, 16):
            piece, at = divmod(b * BLK + k, ROWS)
            tiles.append(z_ref[piece, at : at + 16])
        d = jnp.concatenate(tiles, axis=0)
        tiles = []
        for k in range(0, 64, 8):
            piece, at = divmod(b * 64 + k, HROWS)
            tiles.append(z_ref[piece, ROWS + at : ROWS + at + 8])
        half = jnp.concatenate(tiles, axis=0)
        turned = jnp.concatenate([half[:, 64:], half[:, :64]], axis=1)
        top = jnp.where(lane64 < row64, half, jnp.where(lane64 == row64, 0.5 * half, 0.0))
        top = jnp.where(lane64 >= 64, half, top)
        bottom = jnp.where(lane64 > row64 + 64, turned, 0.0)
        bottom = jnp.where(lane64 == row64 + 64, 0.5 * extra[b : b + 1], bottom)
        w = jnp.concatenate([top, bottom], axis=0)
        s = scales[:, b : b + 1]
        new = p_ref[block(b)] + (2.0 * s) * d - (s * s) * exact(d, w + w.T)
        new_ref[block(b)] = new
        turned = split(new.T, 0)
        turned_ref[:, block(b)] = turned
        grams[b] = gram(split(new, 1), turned)
        copies[b].wait()
        keep_present(m_ref, r_ref, b)
    counts = jnp.zeros((8, BLK), F32)
    lane8 = lanes((8, BLK))
    for pair in range(IB // 2):
        found = jnp.dot(
            turned_ref[...], r_ref[:, pair * 2 * BLK : (pair + 1) * 2 * BLK], preferred_element_type=F32
        )
        found = found[:BLK] + found[BLK:]
        for k in range(2):
            j = pair * 2 + k
            s = jnp.zeros((BLK, BLK), F32)
            count = jnp.int32(0)
            for b in range(UB):
                s = s + present(m_ref, b, j) * grams[b]
                count = count + m_ref[b, j]
            counts = counts + jnp.where(lane8 == j, count.astype(F32), 0.0)
            grads[block(j)] = found[:, block(k)].T - exact(q_ref[block(j)], s)
    core = core_ref[0]
    for k in range(8):
        own_ref[k, :CHUNK] = grads[pl.ds(pl.multiple_of(k * 2 * CHUNK + core * CHUNK, 8), CHUNK)]
        other_ref[k, :CHUNK] = grads[pl.ds(pl.multiple_of(k * 2 * CHUNK + (1 - core) * CHUNK, 8), CHUNK)]
        own_ref[k, CHUNK:] = counts
        other_ref[k, CHUNK:] = counts


def scale_kernel(step_ref, user_ref, v_ref, q_ref, o_ref):
    total = v_ref[0]
    for k in range(1, 8):
        total = total + v_ref[k]
    scales = step_ref[1] / (BLK * (1.0 + total[CHUNK : CHUNK + 1]))
    lane1 = lanes((1, BLK))
    for k in range(3):
        block = (user_ref[0] * 3 + k) // 4
        t = jnp.sum(jnp.where(lane1 == block, scales, 0.0), axis=1, keepdims=True)
        start = pl.multiple_of(user_ref[0] * CHUNK + k * 32, 8)
        o_ref[k * 32 : (k + 1) * 32] = q_ref[pl.ds(start, 32)] + t * total[k * 32 : (k + 1) * 32]


def spread_kernel(core_ref, own_ref, other_ref, o_ref):
    core = core_ref[0]
    for k in range(8):
        o_ref[k, pl.ds(pl.multiple_of(core * CHUNK, 8), CHUNK)] = own_ref[...]
        o_ref[k, pl.ds(pl.multiple_of((1 - core) * CHUNK, 8), CHUNK)] = other_ref[...]


def near(value):
    return pltpu.with_memory_space_constraint(value, pltpu.VMEM)


def far(value):
    return pltpu.with_memory_space_constraint(value, pltpu.HBM)


def call(kernel, out_shapes, specs, scratch=(), limit=8):
    single = len(out_shapes) == 1
    return pl.pallas_call(
        kernel,
        out_shape=out_shapes[0] if single else out_shapes,
        in_specs=specs,
        out_specs=VMEM if single else [VMEM] * len(out_shapes),
        scratch_shapes=scratch,
        compiler_params=pltpu.CompilerParams(vmem_limit_bytes=limit << 20),
    )


def body(ratings, presence, user_factors, item_factors, step_sizes):
    user = lax.axis_index("user")
    core = lax.rem(user, 2)
    user1, core1 = user.reshape(1), core.reshape(1)
    swap = [(k, k ^ 1) for k in range(16)]
    chips = [[k + 2 * j for j in range(8)] for k in range(2)]
    x = call(
        user_kernel,
        [pltpu.VMEM((PIECES, PIECE, BLK), F32)],
        [SMEM, HBM, HBM, HBM],
        [
            pltpu.VMEM((USERS, ITEMS), BF16),
            pltpu.VMEM((USERS, BLK), F32),
            pltpu.VMEM((ITEMS, BLK), F32),
            pltpu.VMEM((ITEMS, 2 * BLK), BF16),
            pltpu.VMEM((IB, BLK, BLK), F32),
            pltpu.VMEM((UB * 64, BLK), F32),
            pltpu.SemaphoreType.DMA((UB,)),
            pltpu.SemaphoreType.DMA((4,)),
            pltpu.SemaphoreType.DMA,
        ],
        limit=16,
    )(presence, far(ratings), far(user_factors), far(item_factors))
    y = lax.all_to_all(x, "item", 0, 0, tiled=True)
    z = call(total_kernel, [pltpu.VMEM((PIECES, PIECE, BLK), F32)], [VMEM])(near(y))
    z = lax.all_to_all(z, "item", 0, 0, tiled=True)
    new_users, own, other = call(
        item_kernel,
        [
            jax.ShapeDtypeStruct((USERS, BLK), F32),
            pltpu.VMEM((8, CHUNK + 8, BLK), F32),
            pltpu.VMEM((8, CHUNK + 8, BLK), F32),
        ],
        [SMEM, SMEM, SMEM, HBM, VMEM, VMEM, VMEM],
        [
            pltpu.VMEM((USERS, ITEMS), BF16),
            pltpu.VMEM((2 * BLK, USERS), BF16),
            pltpu.VMEM((UB, BLK, BLK), F32),
            pltpu.VMEM((ITEMS, BLK), F32),
            pltpu.SemaphoreType.DMA((UB,)),
        ],
        limit=16,
    )(presence, step_sizes, core1, far(ratings), near(user_factors), near(item_factors), near(z))
    v = own + lax.ppermute(other, "user", swap)
    v = lax.all_to_all(v, "user", 0, 0, tiled=True, axis_index_groups=chips)
    owned = call(scale_kernel, [pltpu.VMEM((CHUNK, BLK), F32)], [SMEM, SMEM, VMEM, VMEM])(
        step_sizes, user1, near(v), near(item_factors)
    )
    partner = lax.ppermute(owned, "user", swap)
    w = call(spread_kernel, [pltpu.VMEM((8, 2 * CHUNK, BLK), F32)], [SMEM, VMEM, VMEM])(
        core1, near(owned), near(partner)
    )
    w = lax.all_to_all(w, "user", 0, 0, tiled=True, axis_index_groups=chips)
    return new_users, w.reshape(ITEMS, BLK)


def solution(mesh):
    return jax.shard_map(
        body,
        mesh=mesh,
        in_specs=(P("user", "item"), P("user", "item"), P("user", None), P("item", None), P()),
        out_specs=(P("user", None), P("item", None)),
        check_vma=False,
    )
```

time: 117 us -> 108 us (0.923)
  Pallas kernels: 20.1 us -> 14.4 us
  blocking collectives: 63.6 us -> 62.2 us
    pallas_call x5, Pallas kernels: 20.1 us -> 14.4 us  [the longest x1 6.49 us: body(): call(item_kernel, [jax.ShapeDtypeStruct((USERS, BLK), F32), pltpu.VMEM((8...]
where the time goes in v2:
time: 108 us
  blocking collectives  62.2 us (58%)
  waiting for transfers between devices  19.3 us (18%)
  Pallas kernels  14.4 us (13%)
  starting transfers between devices  9.38 us (9%)
  local copies, waits for them, and re-layouts  1.59 us (1%)
    all_to_all x1, blocking collectives, body(): y = lax.all_to_all(x, 'item', 0, 0, tiled=True)  29.6 us
    all_to_all x1, waiting for transfers between devices, body(): z = lax.all_to_all(z, 'item', 0, 0, tiled=True)  17 us
    all_to_all x1, blocking collectives, body(): w = lax.all_to_all(w, 'user', 0, 0, tiled=True, axis_index_groups=chips)  16.5 us
    all_to_all x1, blocking collectives, body(): v = lax.all_to_all(v, 'user', 0, 0, tiled=True, axis_index_groups=chips)  16.1 us
    pallas_call x1, Pallas kernels, body(): call(item_kernel, [jax.ShapeDtypeStruct((USERS, BLK), F32), pltpu.VMEM((8...  6.49 us
    pallas_call x1, Pallas kernels, body(): call(user_kernel, [pltpu.VMEM((PIECES, PIECE, BLK), F32)], [SMEM, HBM, HB...  6.28 us
    ppermute x1, starting transfers between devices, body(): v = own + lax.ppermute(other, 'user', swap)  4.16 us
    all_to_all x1, starting transfers between devices, body(): z = lax.all_to_all(z, 'item', 0, 0, tiled=True)  3.59 us
  transfers between devices with their start and end apart: 3, of which 3 were waited for; matrix products, arithmetic and copies ran while one was open for 0% of the time, Pallas kernels for 0%

profile of v2, /device:TPU:1, one launch (start us, length us, event | category | flops | bytes accessed | tf_op | source)
XLA Modules:
  0.0 107.6 jit_solution(17790487406096040471)
XLA Ops:
  0.6 0.0 copy-start.2
  0.6 0.7 copy-done.2
  1.3 6.3 %shard_map.68 = f32[16,80,128]{2,1,0:T(8,128)S(1)} custom-call(s32[6,12]{1,0:T(8,128)S(1)} %copy-done.2, bf16[768,1536]{1,0:T(8,128)(2,1)} %r_hbm.3, f32[768,128]{1,0:T(8,128)} %p_ref.1, f32[1536,128]{1,0:T(8,128)} %q_ref.3), custom_call_target="tpu_custom_call" | custom-call | tf_op jit(solution)/shard_map/pallas_call | solution.py:250
  7.6 0.0 copy-start
  7.6 0.0 copy-start.1
  7.6 0.0 copy-start.3
  7.6 0.0 copy-start.4
  7.7 29.6 %all_to_all.20.y_ref = f32[16,80,128]{2,1,0:T(8,128)S(1)} all-to-all(f32[16,80,128]{2,1,0:T(8,128)S(1)} %shard_map.68), channel_id=1, replica_groups=mesh['user'=16,'item'=16] {'item'}, dimensions={0} | all-to-all | bytes 1310720 | tf_op jit(solution)/shard_map/all_to_all | solution.py:267
  37.2 0.9 shard_map.69
  38.1 3.6 %all-to-all-start.1 = ((f32[16,80,128]{2,1,0:T(8,128)}), f32[16,80,128]{2,1,0:T(8,128)S(1)}, u32[]{:S(2)}, u32[]{:S(2)}) async-start(f32[16,80,128]{2,1,0:T(8,128)} %shard_map.69), calls=%async_computation.1 | async-start | bytes 1310720 | tf_op jit(solution)/shard_map/all_to_all | solution.py:269
  41.7 17.0 %all-to-all-done.1.z_ref = f32[16,80,128]{2,1,0:T(8,128)S(1)} async-done(((f32[16,80,128]{2,1,0:T(8,128)}), f32[16,80,128]{2,1,0:T(8,128)S(1)}, u32[]{:S(2)}, u32[]{:S(2)}) %all-to-all-start.1) | async-done | bytes 655392 | tf_op jit(solution)/shard_map/all_to_all | solution.py:269
  58.8 0.0 copy-done
  58.8 0.0 copy-done.1
  58.8 0.0 copy-done.3
  58.8 0.0 copy-done.4
  58.8 6.5 %shard_map.70 = (f32[768,128]{1,0:T(8,128)}, f32[8,104,128]{2,1,0:T(8,128)S(1)}, f32[8,104,128]{2,1,0:T(8,128)S(1)}) custom-call(s32[6,12]{1,0:T(8,128)S(1)} %copy-done.3, f32[2]{0:T(128)S(1)} %copy-done.4, s32[1]{0:T(128)} %bitcast.core_ref, bf16[768,1536]{1,0:T(8,128)(2,1)} %r_hbm.3, f32[768,128]{1,0:T(8,128)S(1)} %copy-done.1, f32[1536,128]{1,0:T(8,128)S(1)} %copy-done, ...), custom_call_target="tpu_custom_call" | custom-call | tf_op jit(solution)/shard_map/pallas_call | solution.py:270
  65.3 4.2 %collective-permute-start = (f32[8,104,128]{2,1,0:T(8,128)S(1)}, f32[8,104,128]{2,1,0:T(8,128)S(1)}, u32[]{:S(2)}, u32[]{:S(2)}) collective-permute-start(f32[8,104,128]{2,1,0:T(8,128)S(1)} %get-tuple-element.7), channel_id=1, source_target_pairs={{0,16},{16,0},{32,48},{48,32},{64,80},{80,64},{96,112},{112,96},{1... | collective-permute-start | bytes 1277960 | tf_op jit(solution)/shard_map/ppermute | solution.py:287
  69.4 1.4 %collective-permute-done = f32[8,104,128]{2,1,0:T(8,128)S(1)} collective-permute-done((f32[8,104,128]{2,1,0:T(8,128)S(1)}, f32[8,104,128]{2,1,0:T(8,128)S(1)}, u32[]{:S(2)}, u32[]{:S(2)}) %collective-permute-start) | collective-permute-done | bytes 426016 | tf_op jit(solution)/shard_map/ppermute | solution.py:287
  70.8 0.1 add.3
  70.9 16.1 %all_to_all.21.v_ref = f32[8,104,128]{2,1,0:T(8,128)S(1)} all-to-all(f32[8,104,128]{2,1,0:T(8,128)S(1)} %add.3), channel_id=1, replica_groups={{0,32,64,96,128,160,192,224},{16,48,80,112,144,176,208,240},{1,33,65,97..., dimensions={0} | all-to-all | bytes 851968 | tf_op jit(solution)/shard_map/all_to_all | solution.py:288
  87.0 0.6 shard_map.71.own_ref
  87.7 1.6 %collective-permute-start.1 = (f32[96,128]{1,0:T(8,128)S(1)}, f32[96,128]{1,0:T(8,128)S(1)}, u32[]{:S(2)}, u32[]{:S(2)}) collective-permute-start(f32[96,128]{1,0:T(8,128)S(1)} %shard_map.71.own_ref), channel_id=1, source_target_pairs={{0,16},{16,0},{32,48},{48,32},{64,80},{80,64},{96,112},{112,96},{1... | collective-permute-start | bytes 147464 | tf_op jit(solution)/shard_map/ppermute | solution.py:292
  89.3 0.9 collective-permute-done.1.other_ref
  90.2 0.1 shard_map.72
  90.2 16.5 %all_to_all.22 = f32[8,192,128]{2,1,0:T(8,128)S(1)} all-to-all(f32[8,192,128]{2,1,0:T(8,128)S(1)} %shard_map.72), channel_id=1, replica_groups={{0,32,64,96,128,160,192,224},{16,48,80,112,144,176,208,240},{1,33,65,97..., dimensions={0} | all-to-all | bytes 1572864 | tf_op jit(solution)/shard_map/all_to_all | solution.py:296
  106.8 0.9 copy.8
Async XLA Ops:
  0.6 0.7 copy-start.2
  7.6 51.2 %copy-start = (f32[1536,128]{1,0:T(8,128)S(1)}, f32[1536,128]{1,0:T(8,128)}, u32[]{:S(2)}) copy-start(f32[1536,128]{1,0:T(8,128)} %q_ref.3) | copy-start | bytes 2359300
  7.6 51.1 %copy-start.1 = (f32[768,128]{1,0:T(8,128)S(1)}, f32[768,128]{1,0:T(8,128)}, u32[]{:S(2)}) copy-start(f32[768,128]{1,0:T(8,128)} %p_ref.1) | copy-start | bytes 1179652
  7.6 51.1 %copy-start.3 = (s32[6,12]{1,0:T(8,128)S(1)}, s32[6,12]{1,0:T(8,128)}, u32[]{:S(2)}) copy-start(s32[6,12]{1,0:T(8,128)} %m_ref.3) | copy-start | bytes 868
  7.6 51.1 %copy-start.4 = (f32[2]{0:T(128)S(1)}, f32[2]{0:T(128)}, u32[]{:S(2)}) copy-start(f32[2]{0:T(128)} %step_ref.3) | copy-start | bytes 28
  38.1 20.6 %all-to-all-start.1 = ((f32[16,80,128]{2,1,0:T(8,128)}), f32[16,80,128]{2,1,0:T(8,128)S(1)}, u32[]{:S(2)}, u32[]{:S(2)}) async-start(f32[16,80,128]{2,1,0:T(8,128)} %shard_map.69), calls=%async_computation.1 | async-start | bytes 1310720 | tf_op jit(solution)/shard_map/all_to_all | solution.py:269
  65.3 5.6 %collective-permute-start = (f32[8,104,128]{2,1,0:T(8,128)S(1)}, f32[8,104,128]{2,1,0:T(8,128)S(1)}, u32[]{:S(2)}, u32[]{:S(2)}) collective-permute-start(f32[8,104,128]{2,1,0:T(8,128)S(1)} %get-tuple-element.7), channel_id=1, source_target_pairs={{0,16},{16,0},{32,48},{48,32},{64,80},{80,64},{96,112},{112,96},{1... | collective-permute-start | bytes 1277960 | tf_op jit(solution)/shard_map/ppermute | solution.py:287
  87.7 2.5 %collective-permute-start.1 = (f32[96,128]{1,0:T(8,128)S(1)}, f32[96,128]{1,0:T(8,128)S(1)}, u32[]{:S(2)}, u32[]{:S(2)}) collective-permute-start(f32[96,128]{1,0:T(8,128)S(1)} %shard_map.71.own_ref), channel_id=1, source_target_pairs={{0,16},{16,0},{32,48},{48,32},{64,80},{80,64},{96,112},{112,96},{1... | collective-permute-start | bytes 147464 | tf_op jit(solution)/shard_map/ppermute | solution.py:292

commit v3 on v2

--- a/solution.py
+++ b/solution.py
@@ -75,13 +75,19 @@
     return m_ref[b, j].astype(F32)
 
 
-def fetch_ratings(r_hbm, r_ref, sem):
+def fetch(source, target, sem, parts):
+    rows = source.shape[0] // parts
     copies = []
-    for b in range(UB):
-        rows = pl.ds(b * BLK, BLK)
-        copies.append(pltpu.make_async_copy(r_hbm.at[rows], r_ref.at[rows], sem.at[b]))
+    for k in range(parts):
+        part = pl.ds(k * rows, rows)
+        copies.append(pltpu.make_async_copy(source.at[part], target.at[part], sem.at[k]))
         copies[-1].start()
     return copies
+
+
+def arrive(copies):
+    for copy in copies:
+        copy.wait()
 
 
 def keep_present(m_ref, r_ref, b):
@@ -90,17 +96,11 @@
 
 
 def user_kernel(m_ref, r_hbm, p_hbm, q_hbm, x_ref, r_ref, p_ref, q_ref, qcat, grams, packed, r_sem, q_sem, p_sem):
-    q_copies = []
-    for k in range(4):
-        rows = pl.ds(k * 3 * BLK, 3 * BLK)
-        q_copies.append(pltpu.make_async_copy(q_hbm.at[rows], q_ref.at[rows], q_sem.at[k]))
-        q_copies[-1].start()
-    r_copies = fetch_ratings(r_hbm, r_ref, r_sem)
-    p_copy = pltpu.make_async_copy(p_hbm, p_ref, p_sem)
-    p_copy.start()
+    q_copies = fetch(q_hbm, q_ref, q_sem, 4)
+    p_copies = fetch(p_hbm, p_ref, p_sem, 2)
+    r_copies = fetch(r_hbm, r_ref, r_sem, UB)
+    arrive(q_copies)
     for j in range(IB):
-        if j % 3 == 0:
-            q_copies[j // 3].wait()
         q = q_ref[block(j)]
         both = split(q, 1)
         qcat[block(j)] = both
@@ -108,7 +108,7 @@
     row64, lane64 = sublanes((64, BLK)), lanes((64, BLK))
     extra_row, extra_lane = sublanes((8, BLK)), lanes((8, BLK))
     extra = jnp.zeros((8, BLK), F32)
-    p_copy.wait()
+    arrive(p_copies + r_copies)
     for half in range(2):
         three = range(half * 3, half * 3 + 3)
         corrections = []
@@ -124,7 +124,6 @@
             extra = extra + jnp.where(extra_row == b, jnp.broadcast_to(diagonal, (8, BLK)), 0.0)
             extra = extra + jnp.where((extra_row == 6) & (extra_lane == b), count.astype(F32), 0.0)
             corrections.append(exact(p_ref[block(b)], h))
-            r_copies[b].wait()
             keep_present(m_ref, r_ref, b)
         found = halves(
             jnp.dot(r_ref[half * 3 * BLK : (half + 1) * 3 * BLK], qcat[...], preferred_element_type=F32)
@@ -146,9 +145,9 @@
 
 
 def item_kernel(
-    m_ref, step_ref, core_ref, r_hbm, p_ref, q_ref, z_ref, new_ref, own_ref, other_ref, r_ref, turned_ref, grams, grads, sem
+    m_ref, step_ref, r_hbm, p_ref, q_ref, z_ref, new_ref, own_ref, other_ref, r_ref, turned_ref, grams, grads, sem
 ):
-    copies = fetch_ratings(r_hbm, r_ref, sem)
+    copies = fetch(r_hbm, r_ref, sem, UB)
     extra = z_ref[0, ROWS + HROWS :]
     scales = step_ref[0] / (BLK * (1.0 + extra[6:7]))
     row64, lane64 = sublanes((64, BLK)), lanes((64, BLK))
@@ -175,7 +174,8 @@
         turned = split(new.T, 0)
         turned_ref[:, block(b)] = turned
         grams[b] = gram(split(new, 1), turned)
-        copies[b].wait()
+    arrive(copies)
+    for b in range(UB):
         keep_present(m_ref, r_ref, b)
     counts = jnp.zeros((8, BLK), F32)
     lane8 = lanes((8, BLK))
@@ -193,7 +193,7 @@
                 count = count + m_ref[b, j]
             counts = counts + jnp.where(lane8 == j, count.astype(F32), 0.0)
             grads[block(j)] = found[:, block(k)].T - exact(q_ref[block(j)], s)
-    core = core_ref[0]
+    core = lax.rem(lax.axis_index("user"), 2)
     for k in range(8):
         own_ref[k, :CHUNK] = grads[pl.ds(pl.multiple_of(k * 2 * CHUNK + core * CHUNK, 8), CHUNK)]
         other_ref[k, :CHUNK] = grads[pl.ds(pl.multiple_of(k * 2 * CHUNK + (1 - core) * CHUNK, 8), CHUNK)]
@@ -201,24 +201,31 @@
         other_ref[k, CHUNK:] = counts
 
 
-def scale_kernel(step_ref, user_ref, v_ref, q_ref, o_ref):
+def scale_kernel(step_ref, v_ref, q_ref, o_ref):
+    user = lax.axis_index("user")
     total = v_ref[0]
     for k in range(1, 8):
         total = total + v_ref[k]
     scales = step_ref[1] / (BLK * (1.0 + total[CHUNK : CHUNK + 1]))
     lane1 = lanes((1, BLK))
     for k in range(3):
-        block = (user_ref[0] * 3 + k) // 4
+        block = (user * 3 + k) // 4
         t = jnp.sum(jnp.where(lane1 == block, scales, 0.0), axis=1, keepdims=True)
-        start = pl.multiple_of(user_ref[0] * CHUNK + k * 32, 8)
-        o_ref[k * 32 : (k + 1) * 32] = q_ref[pl.ds(start, 32)] + t * total[k * 32 : (k + 1) * 32]
-
-
-def spread_kernel(core_ref, own_ref, other_ref, o_ref):
-    core = core_ref[0]
+        start = pl.multiple_of(user * CHUNK + k * 32, 8)
+        new = q_ref[pl.ds(start, 32)] + t * total[k * 32 : (k + 1) * 32]
+        for piece in range(8):
+            o_ref[piece, k * 32 : (k + 1) * 32] = new
+
+
+def join_kernel(own_ref, other_ref, o_hbm, sem):
+    core = lax.rem(lax.axis_index("user"), 2)
+    copies = []
     for k in range(8):
-        o_ref[k, pl.ds(pl.multiple_of(core * CHUNK, 8), CHUNK)] = own_ref[...]
-        o_ref[k, pl.ds(pl.multiple_of((1 - core) * CHUNK, 8), CHUNK)] = other_ref[...]
+        for n, (ref, place) in enumerate(((own_ref, core), (other_ref, 1 - core))):
+            rows = pl.ds(pl.multiple_of(k * 2 * CHUNK + place * CHUNK, 8), CHUNK)
+            copies.append(pltpu.make_async_copy(ref.at[k], o_hbm.at[rows], sem.at[k * 2 + n]))
+            copies[-1].start()
+    arrive(copies)
 
 
 def near(value):
@@ -229,22 +236,19 @@
     return pltpu.with_memory_space_constraint(value, pltpu.HBM)
 
 
-def call(kernel, out_shapes, specs, scratch=(), limit=8):
+def call(kernel, out_shapes, specs, scratch=(), limit=8, out_specs=VMEM):
     single = len(out_shapes) == 1
     return pl.pallas_call(
         kernel,
         out_shape=out_shapes[0] if single else out_shapes,
         in_specs=specs,
-        out_specs=VMEM if single else [VMEM] * len(out_shapes),
+        out_specs=out_specs if single else [out_specs] * len(out_shapes),
         scratch_shapes=scratch,
         compiler_params=pltpu.CompilerParams(vmem_limit_bytes=limit << 20),
     )
 
 
 def body(ratings, presence, user_factors, item_factors, step_sizes):
-    user = lax.axis_index("user")
-    core = lax.rem(user, 2)
-    user1, core1 = user.reshape(1), core.reshape(1)
     swap = [(k, k ^ 1) for k in range(16)]
     chips = [[k + 2 * j for j in range(8)] for k in range(2)]
     x = call(
@@ -260,7 +264,7 @@
             pltpu.VMEM((UB * 64, BLK), F32),
             pltpu.SemaphoreType.DMA((UB,)),
             pltpu.SemaphoreType.DMA((4,)),
-            pltpu.SemaphoreType.DMA,
+            pltpu.SemaphoreType.DMA((2,)),
         ],
         limit=16,
     )(presence, far(ratings), far(user_factors), far(item_factors))
@@ -274,7 +278,7 @@
             pltpu.VMEM((8, CHUNK + 8, BLK), F32),
             pltpu.VMEM((8, CHUNK + 8, BLK), F32),
         ],
-        [SMEM, SMEM, SMEM, HBM, VMEM, VMEM, VMEM],
+        [SMEM, SMEM, HBM, VMEM, VMEM, VMEM],
         [
             pltpu.VMEM((USERS, ITEMS), BF16),
             pltpu.VMEM((2 * BLK, USERS), BF16),
@@ -283,18 +287,22 @@
             pltpu.SemaphoreType.DMA((UB,)),
         ],
         limit=16,
-    )(presence, step_sizes, core1, far(ratings), near(user_factors), near(item_factors), near(z))
+    )(presence, step_sizes, far(ratings), near(user_factors), near(item_factors), near(z))
     v = own + lax.ppermute(other, "user", swap)
     v = lax.all_to_all(v, "user", 0, 0, tiled=True, axis_index_groups=chips)
-    owned = call(scale_kernel, [pltpu.VMEM((CHUNK, BLK), F32)], [SMEM, SMEM, VMEM, VMEM])(
-        step_sizes, user1, near(v), near(item_factors)
+    owned = call(scale_kernel, [pltpu.VMEM((8, CHUNK, BLK), F32)], [SMEM, VMEM, VMEM])(
+        step_sizes, near(v), near(item_factors)
     )
-    partner = lax.ppermute(owned, "user", swap)
-    w = call(spread_kernel, [pltpu.VMEM((8, 2 * CHUNK, BLK), F32)], [SMEM, VMEM, VMEM])(
-        core1, near(owned), near(partner)
-    )
-    w = lax.all_to_all(w, "user", 0, 0, tiled=True, axis_index_groups=chips)
-    return new_users, w.reshape(ITEMS, BLK)
+    mine = lax.all_to_all(owned, "user", 0, 0, tiled=True, axis_index_groups=chips)
+    theirs = lax.ppermute(mine, "user", swap)
+    new_items = call(
+        join_kernel,
+        [pltpu.HBM((ITEMS, BLK), F32)],
+        [VMEM, VMEM],
+        [pltpu.SemaphoreType.DMA((16,))],
+        out_specs=HBM,
+    )(near(mine), near(theirs))
+    return new_users, new_items
 
 
 def solution(mesh):

time: 108 us -> 100 us (0.926)
  blocking collectives: 62.2 us -> 79.7 us
  waiting for transfers between devices: 19.3 us -> 2.75 us
  starting transfers between devices: 9.38 us -> 5.01 us
  Pallas kernels: 14.4 us -> 11.3 us
    all_to_all x1 -> x2, blocking collectives: 16.5 us -> 34 us  [the longest x1 23 us: body(): z = lax.all_to_all(z, 'item', 0, 0, tiled=True)]
    all_to_all x1 -> x0, waiting for transfers between devices: 17 us -> none  [body(): z = lax.all_to_all(z, 'item', 0, 0, tiled=True)]
    all_to_all x1 -> x0, starting transfers between devices: 3.59 us -> none  [body(): z = lax.all_to_all(z, 'item', 0, 0, tiled=True)]
    ppermute x1, starting transfers between devices: 4.16 us -> 2.23 us  [body(): v = own + lax.ppermute(other, 'user', swap)]
    pallas_call x1, Pallas kernels: 6.28 us -> 4.42 us  [body(): call(user_kernel, [pltpu.VMEM((PIECES, PIECE, BLK), F32)], [SMEM, HBM, HB...]
    pallas_call x1, Pallas kernels: 6.49 us -> 5.12 us  [body(): call(item_kernel, [jax.ShapeDtypeStruct((USERS, BLK), F32), pltpu.VMEM((8...]
    ppermute x1, starting transfers between devices: 1.63 us -> 2.79 us  [body(): theirs = lax.ppermute(mine, 'user', swap)]
  transfers between devices with their start and end apart: 3 -> 2, of which waited for: 3 -> 2; matrix products, arithmetic and copies ran while one was open for 0% -> 0% of each run, Pallas kernels for 0% -> 0%
where the time goes in v3:
time: 100 us
  blocking collectives  79.7 us (80%)
  Pallas kernels  11.3 us (11%)
  starting transfers between devices  5.01 us (5%)
  waiting for transfers between devices  2.75 us (3%)
    all_to_all x1, blocking collectives, body(): y = lax.all_to_all(x, 'item', 0, 0, tiled=True)  29.6 us
    all_to_all x1, blocking collectives, body(): z = lax.all_to_all(z, 'item', 0, 0, tiled=True)  23 us
    all_to_all x1, blocking collectives, body(): v = lax.all_to_all(v, 'user', 0, 0, tiled=True, axis_index_groups=chips)  16.1 us
    all_to_all x1, blocking collectives, body(): lax.all_to_all(owned, 'user', 0, 0, tiled=True, axis_index_groups=chips)  11 us
    pallas_call x1, Pallas kernels, body(): call(item_kernel, [jax.ShapeDtypeStruct((USERS, BLK), F32), pltpu.VMEM((8...  5.12 us
    pallas_call x1, Pallas kernels, body(): call(user_kernel, [pltpu.VMEM((PIECES, PIECE, BLK), F32)], [SMEM, HBM, HB...  4.42 us
    ppermute x1, starting transfers between devices, body(): theirs = lax.ppermute(mine, 'user', swap)  2.79 us
    ppermute x1, starting transfers between devices, body(): v = own + lax.ppermute(other, 'user', swap)  2.23 us
  transfers between devices with their start and end apart: 2, of which 2 were waited for; matrix products, arithmetic and copies ran while one was open for 0% of the time, Pallas kernels for 0%

profile of v3, /device:TPU:1, one launch (start us, length us, event | category | flops | bytes accessed | tf_op | source)
XLA Modules:
  0.0 100.1 jit_solution(7384095677509118281)
XLA Ops:
  0.6 0.0 copy-start.2
  0.6 0.7 copy-done.2
  1.3 4.4 %shard_map.68 = f32[16,80,128]{2,1,0:T(8,128)S(1)} custom-call(s32[6,12]{1,0:T(8,128)S(1)} %copy-done.2, bf16[768,1536]{1,0:T(8,128)(2,1)} %r_hbm.3, f32[768,128]{1,0:T(8,128)} %p_ref.1, f32[1536,128]{1,0:T(8,128)} %q_ref.3), custom_call_target="tpu_custom_call" | custom-call | tf_op jit(solution)/shard_map/pallas_call | solution.py:254
  5.7 0.0 copy-start
  5.8 0.0 copy-start.1
  5.8 0.0 copy-start.3
  5.8 29.6 %all_to_all.20.y_ref = f32[16,80,128]{2,1,0:T(8,128)S(1)} all-to-all(f32[16,80,128]{2,1,0:T(8,128)S(1)} %shard_map.68), channel_id=1, replica_groups=mesh['user'=16,'item'=16] {'item'}, dimensions={0} | all-to-all | bytes 1310720 | tf_op jit(solution)/shard_map/all_to_all | solution.py:271
  35.4 0.1 shard_map.69
  35.4 23.0 %all_to_all.21.z_ref = f32[16,80,128]{2,1,0:T(8,128)S(1)} all-to-all(f32[16,80,128]{2,1,0:T(8,128)S(1)} %shard_map.69), channel_id=1, replica_groups=mesh['user'=16,'item'=16] {'item'}, dimensions={0} | all-to-all | bytes 1310720 | tf_op jit(solution)/shard_map/all_to_all | solution.py:273
  58.4 0.0 copy-done
  58.4 0.0 copy-done.1
  58.4 0.0 copy-done.3
  58.4 5.1 %shard_map.70 = (f32[768,128]{1,0:T(8,128)}, f32[8,104,128]{2,1,0:T(8,128)S(1)}, f32[8,104,128]{2,1,0:T(8,128)S(1)}) custom-call(s32[6,12]{1,0:T(8,128)S(1)} %copy-done.2, f32[2]{0:T(128)S(1)} %copy-done.3, bf16[768,1536]{1,0:T(8,128)(2,1)} %r_hbm.3, f32[768,128]{1,0:T(8,128)S(1)} %copy-done.1, f32[1536,128]{1,0:T(8,128)S(1)} %copy-done, ...), custom_call_target="tpu_custom_call" | custom-call | tf_op jit(solution)/shard_map/pallas_call | solution.py:274
  63.5 2.2 %collective-permute-start = (f32[8,104,128]{2,1,0:T(8,128)S(1)}, f32[8,104,128]{2,1,0:T(8,128)S(1)}, u32[]{:S(2)}, u32[]{:S(2)}) collective-permute-start(f32[8,104,128]{2,1,0:T(8,128)S(1)} %get-tuple-element.7), channel_id=1, source_target_pairs={{0,16},{16,0},{32,48},{48,32},{64,80},{80,64},{96,112},{112,96},{1... | collective-permute-start | bytes 1277960 | tf_op jit(solution)/shard_map/ppermute | solution.py:291
  65.8 1.4 %collective-permute-done = f32[8,104,128]{2,1,0:T(8,128)S(1)} collective-permute-done((f32[8,104,128]{2,1,0:T(8,128)S(1)}, f32[8,104,128]{2,1,0:T(8,128)S(1)}, u32[]{:S(2)}, u32[]{:S(2)}) %collective-permute-start) | collective-permute-done | bytes 426016 | tf_op jit(solution)/shard_map/ppermute | solution.py:291
  67.2 16.1 %all_to_all.22.v_ref = f32[8,104,128]{2,1,0:T(8,128)S(1)} all-to-all(f32[8,104,128]{2,1,0:T(8,128)S(1)} %add.3), channel_id=1, replica_groups={{0,32,64,96,128,160,192,224},{16,48,80,112,144,176,208,240},{1,33,65,97..., dimensions={0} | all-to-all | bytes 851968 | tf_op jit(solution)/shard_map/all_to_all | solution.py:292
  83.3 0.7 shard_map.71
  84.0 11.0 %all_to_all.23.own_ref = f32[8,96,128]{2,1,0:T(8,128)S(1)} all-to-all(f32[8,96,128]{2,1,0:T(8,128)S(1)} %shard_map.71), channel_id=1, replica_groups={{0,32,64,96,128,160,192,224},{16,48,80,112,144,176,208,240},{1,33,65,97..., dimensions={0} | all-to-all | bytes 786432 | tf_op jit(solution)/shard_map/all_to_all | solution.py:296
  95.0 2.8 %collective-permute-start.1 = (f32[8,96,128]{2,1,0:T(8,128)S(1)}, f32[8,96,128]{2,1,0:T(8,128)S(1)}, u32[]{:S(2)}, u32[]{:S(2)}) collective-permute-start(f32[8,96,128]{2,1,0:T(8,128)S(1)} %all_to_all.23.own_ref), channel_id=1, source_target_pairs={{0,16},{16,0},{32,48},{48,32},{64,80},{80,64},{96,112},{112,96},{1... | collective-permute-start | bytes 1179656 | tf_op jit(solution)/shard_map/ppermute | solution.py:297
  97.8 1.3 %collective-permute-done.1.other_ref = f32[8,96,128]{2,1,0:T(8,128)S(1)} collective-permute-done((f32[8,96,128]{2,1,0:T(8,128)S(1)}, f32[8,96,128]{2,1,0:T(8,128)S(1)}, u32[]{:S(2)}, u32[]{:S(2)}) %collective-permute-start.1) | collective-permute-done | bytes 393248 | tf_op jit(solution)/shard_map/ppermute | solution.py:297
  99.1 1.0 shard_map.72
  (1 shorter events, 0.0 us)
Async XLA Ops:
  0.6 0.7 copy-start.2
  5.7 52.7 %copy-start = (f32[1536,128]{1,0:T(8,128)S(1)}, f32[1536,128]{1,0:T(8,128)}, u32[]{:S(2)}) copy-start(f32[1536,128]{1,0:T(8,128)} %q_ref.3) | copy-start | bytes 2359300
  5.8 52.6 %copy-start.1 = (f32[768,128]{1,0:T(8,128)S(1)}, f32[768,128]{1,0:T(8,128)}, u32[]{:S(2)}) copy-start(f32[768,128]{1,0:T(8,128)} %p_ref.1) | copy-start | bytes 1179652
  5.8 52.6 %copy-start.3 = (f32[2]{0:T(128)S(1)}, f32[2]{0:T(128)}, u32[]{:S(2)}) copy-start(f32[2]{0:T(128)} %step_ref.3) | copy-start | bytes 28
  63.5 3.6 %collective-permute-start = (f32[8,104,128]{2,1,0:T(8,128)S(1)}, f32[8,104,128]{2,1,0:T(8,128)S(1)}, u32[]{:S(2)}, u32[]{:S(2)}) collective-permute-start(f32[8,104,128]{2,1,0:T(8,128)S(1)} %get-tuple-element.7), channel_id=1, source_target_pairs={{0,16},{16,0},{32,48},{48,32},{64,80},{80,64},{96,112},{112,96},{1... | collective-permute-start | bytes 1277960 | tf_op jit(solution)/shard_map/ppermute | solution.py:291
  95.0 4.1 %collective-permute-start.1 = (f32[8,96,128]{2,1,0:T(8,128)S(1)}, f32[8,96,128]{2,1,0:T(8,128)S(1)}, u32[]{:S(2)}, u32[]{:S(2)}) collective-permute-start(f32[8,96,128]{2,1,0:T(8,128)S(1)} %all_to_all.23.own_ref), channel_id=1, source_target_pairs={{0,16},{16,0},{32,48},{48,32},{64,80},{80,64},{96,112},{112,96},{1... | collective-permute-start | bytes 1179656 | tf_op jit(solution)/shard_map/ppermute | solution.py:297

commit v4 on v3

--- a/solution.py
+++ b/solution.py
@@ -13,7 +13,8 @@
 PIECES = 16
 ROWS = USERS // PIECES
 HROWS = UB * 64 // PIECES
-PIECE = ROWS + HROWS + 8
+SENT = ROWS + HROWS
+PIECE = SENT + 8
 CHUNK = ITEMS // 16
 F32 = jnp.float32
 BF16 = jnp.bfloat16
@@ -90,12 +91,16 @@
         copy.wait()
 
 
-def keep_present(m_ref, r_ref, b):
+def keep_present(m_ref, r_ref, kept, b):
     for j in range(IB):
-        r_ref[block(b), block(j)] = r_ref[block(b), block(j)] * present(m_ref, b, j).astype(BF16)
-
-
-def user_kernel(m_ref, r_hbm, p_hbm, q_hbm, x_ref, r_ref, p_ref, q_ref, qcat, grams, packed, r_sem, q_sem, p_sem):
+        kept[block(b), block(j)] = r_ref[block(b), block(j)] * present(m_ref, b, j).astype(BF16)
+
+
+def user_kernel(
+    m_hbm, r_hbm, p_hbm, q_hbm, x_ref, m_ref, r_ref, p_ref, q_ref, qcat, grams, packed, r_sem, q_sem, p_sem, m_sem
+):
+    m_copy = pltpu.make_async_copy(m_hbm, m_ref, m_sem)
+    m_copy.start()
     q_copies = fetch(q_hbm, q_ref, q_sem, 4)
     p_copies = fetch(p_hbm, p_ref, p_sem, 2)
     r_copies = fetch(r_hbm, r_ref, r_sem, UB)
@@ -108,7 +113,7 @@
     row64, lane64 = sublanes((64, BLK)), lanes((64, BLK))
     extra_row, extra_lane = sublanes((8, BLK)), lanes((8, BLK))
     extra = jnp.zeros((8, BLK), F32)
-    arrive(p_copies + r_copies)
+    arrive([m_copy] + p_copies + r_copies)
     for half in range(2):
         three = range(half * 3, half * 3 + 3)
         corrections = []
@@ -124,7 +129,7 @@
             extra = extra + jnp.where(extra_row == b, jnp.broadcast_to(diagonal, (8, BLK)), 0.0)
             extra = extra + jnp.where((extra_row == 6) & (extra_lane == b), count.astype(F32), 0.0)
             corrections.append(exact(p_ref[block(b)], h))
-            keep_present(m_ref, r_ref, b)
+            keep_present(m_ref, r_ref, r_ref, b)
         found = halves(
             jnp.dot(r_ref[half * 3 * BLK : (half + 1) * 3 * BLK], qcat[...], preferred_element_type=F32)
         )
@@ -133,22 +138,22 @@
             x_ref[half * 8 + k, :ROWS] = d[k * ROWS : (k + 1) * ROWS]
     for piece in range(PIECES):
         x_ref[piece, ROWS : ROWS + HROWS] = packed[piece * HROWS : (piece + 1) * HROWS]
-        x_ref[piece, ROWS + HROWS :] = extra if piece == 0 else jnp.zeros((8, BLK), F32)
-
-
-def total_kernel(y_ref, z_ref):
+        x_ref[piece, SENT:] = extra
+
+
+def total_kernel(y_ref, z_ref, extra_ref):
     total = y_ref[0]
     for k in range(1, PIECES):
         total = total + y_ref[k]
+    extra_ref[...] = total[SENT:]
     for k in range(PIECES):
-        z_ref[k] = total
+        z_ref[k] = total[:SENT]
 
 
 def item_kernel(
-    m_ref, step_ref, r_hbm, p_ref, q_ref, z_ref, new_ref, own_ref, other_ref, r_ref, turned_ref, grams, grads, sem
+    m_ref, step_ref, r_ref, p_ref, q_ref, z_ref, extra_ref, new_ref, own_ref, other_ref, kept, turned_ref, grams, grads
 ):
-    copies = fetch(r_hbm, r_ref, sem, UB)
-    extra = z_ref[0, ROWS + HROWS :]
+    extra = extra_ref[...]
     scales = step_ref[0] / (BLK * (1.0 + extra[6:7]))
     row64, lane64 = sublanes((64, BLK)), lanes((64, BLK))
     for b in range(UB):
@@ -174,14 +179,12 @@
         turned = split(new.T, 0)
         turned_ref[:, block(b)] = turned
         grams[b] = gram(split(new, 1), turned)
-    arrive(copies)
-    for b in range(UB):
-        keep_present(m_ref, r_ref, b)
+        keep_present(m_ref, r_ref, kept, b)
     counts = jnp.zeros((8, BLK), F32)
     lane8 = lanes((8, BLK))
     for pair in range(IB // 2):
         found = jnp.dot(
-            turned_ref[...], r_ref[:, pair * 2 * BLK : (pair + 1) * 2 * BLK], preferred_element_type=F32
+            turned_ref[...], kept[:, pair * 2 * BLK : (pair + 1) * 2 * BLK], preferred_element_type=F32
         )
         found = found[:BLK] + found[BLK:]
         for k in range(2):
@@ -193,7 +196,10 @@
                 count = count + m_ref[b, j]
             counts = counts + jnp.where(lane8 == j, count.astype(F32), 0.0)
             grads[block(j)] = found[:, block(k)].T - exact(q_ref[block(j)], s)
-    core = lax.rem(lax.axis_index("user"), 2)
+    user = lax.axis_index("user")
+    core = lax.rem(user, 2)
+    step = jnp.where(user == 0, step_ref[1], 0.0)
+    counts = jnp.where(sublanes((8, BLK)) == 0, counts, step)
     for k in range(8):
         own_ref[k, :CHUNK] = grads[pl.ds(pl.multiple_of(k * 2 * CHUNK + core * CHUNK, 8), CHUNK)]
         other_ref[k, :CHUNK] = grads[pl.ds(pl.multiple_of(k * 2 * CHUNK + (1 - core) * CHUNK, 8), CHUNK)]
@@ -201,12 +207,12 @@
         other_ref[k, CHUNK:] = counts
 
 
-def scale_kernel(step_ref, v_ref, q_ref, o_ref):
+def scale_kernel(v_ref, q_ref, o_ref):
     user = lax.axis_index("user")
     total = v_ref[0]
     for k in range(1, 8):
         total = total + v_ref[k]
-    scales = step_ref[1] / (BLK * (1.0 + total[CHUNK : CHUNK + 1]))
+    scales = total[CHUNK + 1 : CHUNK + 2] / (BLK * (1.0 + total[CHUNK : CHUNK + 1]))
     lane1 = lanes((1, BLK))
     for k in range(3):
         block = (user * 3 + k) // 4
@@ -254,8 +260,9 @@
     x = call(
         user_kernel,
         [pltpu.VMEM((PIECES, PIECE, BLK), F32)],
-        [SMEM, HBM, HBM, HBM],
+        [HBM, HBM, HBM, HBM],
         [
+            pltpu.SMEM((UB, IB), jnp.int32),
             pltpu.VMEM((USERS, ITEMS), BF16),
             pltpu.VMEM((USERS, BLK), F32),
             pltpu.VMEM((ITEMS, BLK), F32),
@@ -265,11 +272,14 @@
             pltpu.SemaphoreType.DMA((UB,)),
             pltpu.SemaphoreType.DMA((4,)),
             pltpu.SemaphoreType.DMA((2,)),
+            pltpu.SemaphoreType.DMA,
         ],
         limit=16,
-    )(presence, far(ratings), far(user_factors), far(item_factors))
+    )(far(presence), far(ratings), far(user_factors), far(item_factors))
     y = lax.all_to_all(x, "item", 0, 0, tiled=True)
-    z = call(total_kernel, [pltpu.VMEM((PIECES, PIECE, BLK), F32)], [VMEM])(near(y))
+    z, extra = call(
+        total_kernel, [pltpu.VMEM((PIECES, SENT, BLK), F32), pltpu.VMEM((8, BLK), F32)], [VMEM]
+    )(near(y))
     z = lax.all_to_all(z, "item", 0, 0, tiled=True)
     new_users, own, other = call(
         item_kernel,
@@ -278,20 +288,19 @@
             pltpu.VMEM((8, CHUNK + 8, BLK), F32),
             pltpu.VMEM((8, CHUNK + 8, BLK), F32),
         ],
-        [SMEM, SMEM, HBM, VMEM, VMEM, VMEM],
+        [SMEM, SMEM, VMEM, VMEM, VMEM, VMEM, VMEM],
         [
             pltpu.VMEM((USERS, ITEMS), BF16),
             pltpu.VMEM((2 * BLK, USERS), BF16),
             pltpu.VMEM((UB, BLK, BLK), F32),
             pltpu.VMEM((ITEMS, BLK), F32),
-            pltpu.SemaphoreType.DMA((UB,)),
         ],
         limit=16,
-    )(presence, step_sizes, far(ratings), near(user_factors), near(item_factors), near(z))
+    )(presence, step_sizes, near(ratings), near(user_factors), near(item_factors), near(z), near(extra))
     v = own + lax.ppermute(other, "user", swap)
     v = lax.all_to_all(v, "user", 0, 0, tiled=True, axis_index_groups=chips)
-    owned = call(scale_kernel, [pltpu.VMEM((8, CHUNK, BLK), F32)], [SMEM, VMEM, VMEM])(
-        step_sizes, near(v), near(item_factors)
+    owned = call(scale_kernel, [pltpu.VMEM((8, CHUNK, BLK), F32)], [VMEM, VMEM])(
+        near(v), near(item_factors)
     )
     mine = lax.all_to_all(owned, "user", 0, 0, tiled=True, axis_index_groups=chips)
     theirs = lax.ppermute(mine, "user", swap)

time: 100 us -> 96.3 us (0.963)
  Pallas kernels: 11.3 us -> 9.02 us
  blocking collectives: 79.7 us -> 78.5 us
    all_to_all x1, blocking collectives: 23 us -> 21.7 us  [body(): z = lax.all_to_all(z, 'item', 0, 0, tiled=True)]
    pallas_call x1, Pallas kernels: 5.12 us -> 3.96 us  [body(): call(item_kernel, [jax.ShapeDtypeStruct((USERS, BLK), F32), pltpu.VMEM((8...]
    pallas_call x3, Pallas kernels: 5.14 us -> 4.06 us  [the longest x1 3.89 us: body(): call(user_kernel, [pltpu.VMEM((PIECES, PIECE, BLK), F32)], [HBM, HBM, HBM...]
where the time goes in v4:
time: 96.3 us; the launch traced here: 96 us
  blocking collectives  78.5 us (82%)
  Pallas kernels  9.02 us (9%)
  starting transfers between devices  4.94 us (5%)
  waiting for transfers between devices  2.75 us (3%)
    all_to_all x1, blocking collectives, body(): y = lax.all_to_all(x, 'item', 0, 0, tiled=True)  29.7 us
    all_to_all x1, blocking collectives, body(): z = lax.all_to_all(z, 'item', 0, 0, tiled=True)  21.7 us
    all_to_all x1, blocking collectives, body(): v = lax.all_to_all(v, 'user', 0, 0, tiled=True, axis_index_groups=chips)  16.1 us
    all_to_all x1, blocking collectives, body(): lax.all_to_all(owned, 'user', 0, 0, tiled=True, axis_index_groups=chips)  11 us
    pallas_call x1, Pallas kernels, body(): call(item_kernel, [jax.ShapeDtypeStruct((USERS, BLK), F32), pltpu.VMEM((8...  3.96 us
    pallas_call x1, Pallas kernels, body(): call(user_kernel, [pltpu.VMEM((PIECES, PIECE, BLK), F32)], [HBM, HBM, HBM...  3.89 us
    ppermute x1, starting transfers between devices, body(): theirs = lax.ppermute(mine, 'user', swap)  2.79 us
    ppermute x1, starting transfers between devices, body(): v = own + lax.ppermute(other, 'user', swap)  2.15 us
  transfers between devices with their start and end apart: 2, of which 2 were waited for; matrix products, arithmetic and copies ran while one was open for 0% of the time, Pallas kernels for 0%

profile of v4, /device:TPU:1, one launch (start us, length us, event | category | flops | bytes accessed | tf_op | source)
XLA Modules:
  0.0 96.0 jit_solution(17869457227587525772)
XLA Ops:
  0.6 0.0 copy-start.2
  0.6 0.0 copy-start.3
  0.6 3.9 %shard_map.68 = f32[16,80,128]{2,1,0:T(8,128)S(1)} custom-call(s32[6,12]{1,0:T(8,128)} %m_ref.1, bf16[768,1536]{1,0:T(8,128)(2,1)} %r_ref.1, f32[768,128]{1,0:T(8,128)} %p_ref.1, f32[1536,128]{1,0:T(8,128)} %q_ref.3), custom_call_target="tpu_custom_call" | custom-call | tf_op jit(solution)/shard_map/pallas_call | solution.py:260
  4.5 0.0 copy-start
  4.6 0.0 copy-start.1
  4.6 0.0 copy-start.4
  4.6 29.7 %all_to_all.20.y_ref = f32[16,80,128]{2,1,0:T(8,128)S(1)} all-to-all(f32[16,80,128]{2,1,0:T(8,128)S(1)} %shard_map.68), channel_id=1, replica_groups=mesh['user'=16,'item'=16] {'item'}, dimensions={0} | all-to-all | bytes 1310720 | tf_op jit(solution)/shard_map/all_to_all | solution.py:279
  34.3 0.1 shard_map.69
  34.4 21.7 %all_to_all.21.z_ref = f32[16,72,128]{2,1,0:T(8,128)S(1)} all-to-all(f32[16,72,128]{2,1,0:T(8,128)S(1)} %get-tuple-element.7), channel_id=1, replica_groups=mesh['user'=16,'item'=16] {'item'}, dimensions={0} | all-to-all | bytes 1179648 | tf_op jit(solution)/shard_map/all_to_all | solution.py:283
  56.0 0.0 copy-done.2
  56.0 0.0 copy-done.3
  56.0 0.0 copy-done
  56.1 0.0 copy-done.1
  56.1 0.0 copy-done.4
  56.1 4.0 %shard_map.70 = (f32[768,128]{1,0:T(8,128)}, f32[8,104,128]{2,1,0:T(8,128)S(1)}, f32[8,104,128]{2,1,0:T(8,128)S(1)}) custom-call(s32[6,12]{1,0:T(8,128)S(1)} %copy-done.3, f32[2]{0:T(128)S(1)} %copy-done.4, bf16[768,1536]{1,0:T(8,128)(2,1)S(1)} %copy-done, f32[768,128]{1,0:T(8,128)S(1)} %copy-done.2, f32[1536,128]{1,0:T(8,128)S(1)} %copy-done.1, ...), custom_call_target="tpu_custom_call" | custom-call | tf_op jit(solution)/shard_map/pallas_call | solution.py:284
  60.0 2.2 %collective-permute-start = (f32[8,104,128]{2,1,0:T(8,128)S(1)}, f32[8,104,128]{2,1,0:T(8,128)S(1)}, u32[]{:S(2)}, u32[]{:S(2)}) collective-permute-start(f32[8,104,128]{2,1,0:T(8,128)S(1)} %get-tuple-element.11), channel_id=1, source_target_pairs={{0,16},{16,0},{32,48},{48,32},{64,80},{80,64},{96,112},{112,96},{1... | collective-permute-start | bytes 1277960 | tf_op jit(solution)/shard_map/ppermute | solution.py:300
  62.2 1.4 %collective-permute-done = f32[8,104,128]{2,1,0:T(8,128)S(1)} collective-permute-done((f32[8,104,128]{2,1,0:T(8,128)S(1)}, f32[8,104,128]{2,1,0:T(8,128)S(1)}, u32[]{:S(2)}, u32[]{:S(2)}) %collective-permute-start) | collective-permute-done | bytes 426016 | tf_op jit(solution)/shard_map/ppermute | solution.py:300
  63.6 0.1 add.3
  63.6 16.1 %all_to_all.22.v_ref = f32[8,104,128]{2,1,0:T(8,128)S(1)} all-to-all(f32[8,104,128]{2,1,0:T(8,128)S(1)} %add.3), channel_id=1, replica_groups={{0,32,64,96,128,160,192,224},{16,48,80,112,144,176,208,240},{1,33,65,97..., dimensions={0} | all-to-all | bytes 851968 | tf_op jit(solution)/shard_map/all_to_all | solution.py:301
  79.8 0.1 shard_map.71
  79.9 11.0 %all_to_all.23.own_ref = f32[8,96,128]{2,1,0:T(8,128)S(1)} all-to-all(f32[8,96,128]{2,1,0:T(8,128)S(1)} %shard_map.71), channel_id=1, replica_groups={{0,32,64,96,128,160,192,224},{16,48,80,112,144,176,208,240},{1,33,65,97..., dimensions={0} | all-to-all | bytes 786432 | tf_op jit(solution)/shard_map/all_to_all | solution.py:305
  90.9 2.8 %collective-permute-start.1 = (f32[8,96,128]{2,1,0:T(8,128)S(1)}, f32[8,96,128]{2,1,0:T(8,128)S(1)}, u32[]{:S(2)}, u32[]{:S(2)}) collective-permute-start(f32[8,96,128]{2,1,0:T(8,128)S(1)} %all_to_all.23.own_ref), channel_id=1, source_target_pairs={{0,16},{16,0},{32,48},{48,32},{64,80},{80,64},{96,112},{112,96},{1... | collective-permute-start | bytes 1179656 | tf_op jit(solution)/shard_map/ppermute | solution.py:306
  93.7 1.3 %collective-permute-done.1.other_ref = f32[8,96,128]{2,1,0:T(8,128)S(1)} collective-permute-done((f32[8,96,128]{2,1,0:T(8,128)S(1)}, f32[8,96,128]{2,1,0:T(8,128)S(1)}, u32[]{:S(2)}, u32[]{:S(2)}) %collective-permute-start.1) | collective-permute-done | bytes 393248 | tf_op jit(solution)/shard_map/ppermute | solution.py:306
  95.0 1.0 %shard_map.72 = f32[1536,128]{1,0:T(8,128)} custom-call(f32[8,96,128]{2,1,0:T(8,128)S(1)} %all_to_all.23.own_ref, f32[8,96,128]{2,1,0:T(8,128)S(1)} %collective-permute-done.1.other_ref), custom_call_target="tpu_custom_call" | custom-call | tf_op jit(solution)/shard_map/pallas_call | solution.py:307
Async XLA Ops:
  0.6 55.4 %copy-start.2 = (f32[768,128]{1,0:T(8,128)S(1)}, f32[768,128]{1,0:T(8,128)}, u32[]{:S(2)}) copy-start(f32[768,128]{1,0:T(8,128)} %p_ref.1) | copy-start | bytes 1179652
  0.6 55.4 %copy-start.3 = (s32[6,12]{1,0:T(8,128)S(1)}, s32[6,12]{1,0:T(8,128)}, u32[]{:S(2)}) copy-start(s32[6,12]{1,0:T(8,128)} %m_ref.1) | copy-start | bytes 868
  4.5 51.5 %copy-start = (bf16[768,1536]{1,0:T(8,128)(2,1)S(1)}, bf16[768,1536]{1,0:T(8,128)(2,1)}, u32[]{:S(2)}) copy-start(bf16[768,1536]{1,0:T(8,128)(2,1)} %r_ref.1) | copy-start | bytes 7077892
  4.6 51.5 %copy-start.1 = (f32[1536,128]{1,0:T(8,128)S(1)}, f32[1536,128]{1,0:T(8,128)}, u32[]{:S(2)}) copy-start(f32[1536,128]{1,0:T(8,128)} %q_ref.3) | copy-start | bytes 2359300
  4.6 51.5 %copy-start.4 = (f32[2]{0:T(128)S(1)}, f32[2]{0:T(128)}, u32[]{:S(2)}) copy-start(f32[2]{0:T(128)} %step_ref.1) | copy-start | bytes 28
  60.0 3.5 %collective-permute-start = (f32[8,104,128]{2,1,0:T(8,128)S(1)}, f32[8,104,128]{2,1,0:T(8,128)S(1)}, u32[]{:S(2)}, u32[]{:S(2)}) collective-permute-start(f32[8,104,128]{2,1,0:T(8,128)S(1)} %get-tuple-element.11), channel_id=1, source_target_pairs={{0,16},{16,0},{32,48},{48,32},{64,80},{80,64},{96,112},{112,96},{1... | collective-permute-start | bytes 1277960 | tf_op jit(solution)/shard_map/ppermute | solution.py:300
  90.9 4.1 %collective-permute-start.1 = (f32[8,96,128]{2,1,0:T(8,128)S(1)}, f32[8,96,128]{2,1,0:T(8,128)S(1)}, u32[]{:S(2)}, u32[]{:S(2)}) collective-permute-start(f32[8,96,128]{2,1,0:T(8,128)S(1)} %all_to_all.23.own_ref), channel_id=1, source_target_pairs={{0,16},{16,0},{32,48},{48,32},{64,80},{80,64},{96,112},{112,96},{1... | collective-permute-start | bytes 1179656 | tf_op jit(solution)/shard_map/ppermute | solution.py:306

commit v5 on v4

--- a/solution.py
+++ b/solution.py
@@ -91,9 +91,21 @@
         copy.wait()
 
 
-def keep_present(m_ref, r_ref, kept, b):
-    for j in range(IB):
-        kept[block(b), block(j)] = r_ref[block(b), block(j)] * present(m_ref, b, j).astype(BF16)
+def only_present(m_ref, r_ref, blocks, columns, first, count):
+    return jnp.concatenate(
+        [
+            jnp.concatenate(
+                [
+                    r_ref[block(b), pl.ds(pl.multiple_of(columns + k * BLK, BLK), BLK)]
+                    * present(m_ref, b, first + k).astype(BF16)
+                    for k in range(count)
+                ],
+                axis=1,
+            )
+            for b in blocks
+        ],
+        axis=0,
+    )
 
 
 def user_kernel(
@@ -129,10 +141,8 @@
             extra = extra + jnp.where(extra_row == b, jnp.broadcast_to(diagonal, (8, BLK)), 0.0)
             extra = extra + jnp.where((extra_row == 6) & (extra_lane == b), count.astype(F32), 0.0)
             corrections.append(exact(p_ref[block(b)], h))
-            keep_present(m_ref, r_ref, r_ref, b)
-        found = halves(
-            jnp.dot(r_ref[half * 3 * BLK : (half + 1) * 3 * BLK], qcat[...], preferred_element_type=F32)
-        )
+        masked = only_present(m_ref, r_ref, three, 0, 0, IB)
+        found = halves(jnp.dot(masked, qcat[...], preferred_element_type=F32))
         d = found - jnp.concatenate(corrections, axis=0)
         for k in range(8):
             x_ref[half * 8 + k, :ROWS] = d[k * ROWS : (k + 1) * ROWS]
@@ -151,7 +161,7 @@
 
 
 def item_kernel(
-    m_ref, step_ref, r_ref, p_ref, q_ref, z_ref, extra_ref, new_ref, own_ref, other_ref, kept, turned_ref, grams, grads
+    m_ref, step_ref, r_ref, p_ref, q_ref, z_ref, extra_ref, new_ref, other_ref, turned_ref, grams
 ):
     extra = extra_ref[...]
     scales = step_ref[0] / (BLK * (1.0 + extra[6:7]))
@@ -179,32 +189,42 @@
         turned = split(new.T, 0)
         turned_ref[:, block(b)] = turned
         grams[b] = gram(split(new, 1), turned)
-        keep_present(m_ref, r_ref, kept, b)
+    core = lax.rem(lax.axis_index("user"), 2)
+    item_half(1 - core, m_ref, step_ref, r_ref, q_ref, turned_ref, grams, other_ref)
+
+
+def item_half(side, m_ref, step_ref, r_ref, q_ref, turned_ref, grams, o_ref):
     counts = jnp.zeros((8, BLK), F32)
-    lane8 = lanes((8, BLK))
-    for pair in range(IB // 2):
-        found = jnp.dot(
-            turned_ref[...], kept[:, pair * 2 * BLK : (pair + 1) * 2 * BLK], preferred_element_type=F32
-        )
+    row8, lane8 = sublanes((8, BLK)), lanes((8, BLK))
+    for j in range(IB):
+        count = jnp.int32(0)
+        for b in range(UB):
+            count = count + m_ref[b, j]
+        counts = counts + jnp.where(lane8 == j, count.astype(F32), 0.0)
+    step = jnp.where(lax.axis_index("user") == 0, step_ref[1], 0.0)
+    counts = jnp.where(row8 == 0, counts, step)
+    first = side * (IB // 2)
+    for pair in range(IB // 4):
+        columns = pl.multiple_of(side * (ITEMS // 2) + pair * 2 * BLK, BLK)
+        masked = only_present(m_ref, r_ref, range(UB), columns, first + pair * 2, 2)
+        found = jnp.dot(turned_ref[...], masked, preferred_element_type=F32)
         found = found[:BLK] + found[BLK:]
         for k in range(2):
-            j = pair * 2 + k
             s = jnp.zeros((BLK, BLK), F32)
-            count = jnp.int32(0)
             for b in range(UB):
-                s = s + present(m_ref, b, j) * grams[b]
-                count = count + m_ref[b, j]
-            counts = counts + jnp.where(lane8 == j, count.astype(F32), 0.0)
-            grads[block(j)] = found[:, block(k)].T - exact(q_ref[block(j)], s)
-    user = lax.axis_index("user")
-    core = lax.rem(user, 2)
-    step = jnp.where(user == 0, step_ref[1], 0.0)
-    counts = jnp.where(sublanes((8, BLK)) == 0, counts, step)
-    for k in range(8):
-        own_ref[k, :CHUNK] = grads[pl.ds(pl.multiple_of(k * 2 * CHUNK + core * CHUNK, 8), CHUNK)]
-        other_ref[k, :CHUNK] = grads[pl.ds(pl.multiple_of(k * 2 * CHUNK + (1 - core) * CHUNK, 8), CHUNK)]
-        own_ref[k, CHUNK:] = counts
-        other_ref[k, CHUNK:] = counts
+                s = s + present(m_ref, b, first + pair * 2 + k) * grams[b]
+            q = q_ref[pl.ds(pl.multiple_of(columns + k * BLK, BLK), BLK)]
+            grad = found[:, block(k)].T - exact(q, s)
+            for part in range(4):
+                piece, at = divmod((pair * 2 + k) * 4 + part, 3)
+                o_ref[piece, at * 32 : (at + 1) * 32] = grad[part * 32 : (part + 1) * 32]
+    for piece in range(8):
+        o_ref[piece, CHUNK:] = counts
+
+
+def own_kernel(m_ref, step_ref, r_ref, q_ref, turned_ref, grams, own_ref):
+    core = lax.rem(lax.axis_index("user"), 2)
+    item_half(core, m_ref, step_ref, r_ref, q_ref, turned_ref, grams, own_ref)
 
 
 def scale_kernel(v_ref, q_ref, o_ref):
@@ -215,23 +235,31 @@
     scales = total[CHUNK + 1 : CHUNK + 2] / (BLK * (1.0 + total[CHUNK : CHUNK + 1]))
     lane1 = lanes((1, BLK))
     for k in range(3):
-        block = (user * 3 + k) // 4
-        t = jnp.sum(jnp.where(lane1 == block, scales, 0.0), axis=1, keepdims=True)
-        start = pl.multiple_of(user * CHUNK + k * 32, 8)
+        place = lax.rem(user, 2) * 24 + (user // 2) * 3 + k
+        t = jnp.sum(jnp.where(lane1 == place // 4, scales, 0.0), axis=1, keepdims=True)
+        start = pl.multiple_of(place * 32, 8)
         new = q_ref[pl.ds(start, 32)] + t * total[k * 32 : (k + 1) * 32]
         for piece in range(8):
             o_ref[piece, k * 32 : (k + 1) * 32] = new
 
 
-def join_kernel(own_ref, other_ref, o_hbm, sem):
+def place_kernel(flip, half_ref, whole, o_hbm, sem):
     core = lax.rem(lax.axis_index("user"), 2)
+    side = 1 - core if flip else core
     copies = []
     for k in range(8):
-        for n, (ref, place) in enumerate(((own_ref, core), (other_ref, 1 - core))):
-            rows = pl.ds(pl.multiple_of(k * 2 * CHUNK + place * CHUNK, 8), CHUNK)
-            copies.append(pltpu.make_async_copy(ref.at[k], o_hbm.at[rows], sem.at[k * 2 + n]))
-            copies[-1].start()
+        rows = pl.ds(pl.multiple_of(side * (ITEMS // 2) + k * CHUNK, 8), CHUNK)
+        copies.append(pltpu.make_async_copy(half_ref.at[k], o_hbm.at[rows], sem.at[k]))
+        copies[-1].start()
     arrive(copies)
+
+
+def place_own_kernel(half_ref, o_hbm, sem):
+    place_kernel(False, half_ref, None, o_hbm, sem)
+
+
+def place_other_kernel(half_ref, whole, o_hbm, sem):
+    place_kernel(True, half_ref, whole, o_hbm, sem)
 
 
 def near(value):
@@ -242,7 +270,7 @@
     return pltpu.with_memory_space_constraint(value, pltpu.HBM)
 
 
-def call(kernel, out_shapes, specs, scratch=(), limit=8, out_specs=VMEM):
+def call(kernel, out_shapes, specs, scratch=(), limit=8, out_specs=VMEM, cost=None, alias={}):
     single = len(out_shapes) == 1
     return pl.pallas_call(
         kernel,
@@ -251,6 +279,8 @@
         out_specs=out_specs if single else [out_specs] * len(out_shapes),
         scratch_shapes=scratch,
         compiler_params=pltpu.CompilerParams(vmem_limit_bytes=limit << 20),
+        cost_estimate=cost,
+        input_output_aliases=alias,
     )
 
 
@@ -281,36 +311,48 @@
         total_kernel, [pltpu.VMEM((PIECES, SENT, BLK), F32), pltpu.VMEM((8, BLK), F32)], [VMEM]
     )(near(y))
     z = lax.all_to_all(z, "item", 0, 0, tiled=True)
-    new_users, own, other = call(
+    new_users, other, turned, grams = call(
         item_kernel,
         [
             jax.ShapeDtypeStruct((USERS, BLK), F32),
             pltpu.VMEM((8, CHUNK + 8, BLK), F32),
-            pltpu.VMEM((8, CHUNK + 8, BLK), F32),
+            pltpu.VMEM((2 * BLK, USERS), BF16),
+            pltpu.VMEM((UB, BLK, BLK), F32),
         ],
         [SMEM, SMEM, VMEM, VMEM, VMEM, VMEM, VMEM],
-        [
-            pltpu.VMEM((USERS, ITEMS), BF16),
-            pltpu.VMEM((2 * BLK, USERS), BF16),
-            pltpu.VMEM((UB, BLK, BLK), F32),
-            pltpu.VMEM((ITEMS, BLK), F32),
-        ],
         limit=16,
     )(presence, step_sizes, near(ratings), near(user_factors), near(item_factors), near(z), near(extra))
-    v = own + lax.ppermute(other, "user", swap)
+    received = lax.ppermute(other, "user", swap)
+    own = call(
+        own_kernel,
+        [pltpu.VMEM((8, CHUNK + 8, BLK), F32)],
+        [SMEM, SMEM, VMEM, VMEM, VMEM, VMEM],
+        limit=16,
+        cost=pl.CostEstimate(flops=1 << 32, bytes_accessed=1 << 23, transcendentals=0),
+    )(presence, step_sizes, near(ratings), near(item_factors), near(turned), near(grams))
+    v = own + received
     v = lax.all_to_all(v, "user", 0, 0, tiled=True, axis_index_groups=chips)
     owned = call(scale_kernel, [pltpu.VMEM((8, CHUNK, BLK), F32)], [VMEM, VMEM])(
         near(v), near(item_factors)
     )
     mine = lax.all_to_all(owned, "user", 0, 0, tiled=True, axis_index_groups=chips)
     theirs = lax.ppermute(mine, "user", swap)
+    half = call(
+        place_own_kernel,
+        [pltpu.HBM((ITEMS, BLK), F32)],
+        [VMEM],
+        [pltpu.SemaphoreType.DMA((8,))],
+        out_specs=HBM,
+        cost=pl.CostEstimate(flops=1 << 30, bytes_accessed=1 << 22, transcendentals=0),
+    )(near(mine))
     new_items = call(
-        join_kernel,
+        place_other_kernel,
         [pltpu.HBM((ITEMS, BLK), F32)],
-        [VMEM, VMEM],
-        [pltpu.SemaphoreType.DMA((16,))],
+        [VMEM, HBM],
+        [pltpu.SemaphoreType.DMA((8,))],
         out_specs=HBM,
-    )(near(mine), near(theirs))
+        alias={1: 0},
+    )(near(theirs), half)
     return new_users, new_items
 
 

time: 96.3 us -> 95 us (0.987)
  waiting for transfers between devices: 2.75 us -> 0.54 us
    pallas_call x1 -> x3, Pallas kernels: 1 us -> 3.13 us  [the longest x1 1.53 us: body(): call(own_kernel, [pltpu.VMEM((8, CHUNK + 8, BLK), F32)], [SMEM, SMEM, VME...]
    ppermute x1, waiting for transfers between devices: 1.4 us -> 0.01 us  [body(): received = lax.ppermute(other, 'user', swap)]
    pallas_call x1, Pallas kernels: 3.96 us -> 2.73 us  [body(): call(item_kernel, [jax.ShapeDtypeStruct((USERS, BLK), F32), pltpu.VMEM((8...]
  transfers between devices with their start and end apart: 2 -> 2, of which waited for: 2 -> 1; matrix products, arithmetic and copies ran while one was open for 0% -> 0% of each run, Pallas kernels for 0% -> 2%
where the time goes in v5:
time: 95 us; the launch traced here: 94.8 us
  blocking collectives  78.6 us (83%)
  Pallas kernels  9.9 us (10%)
  starting transfers between devices  4.89 us (5%)
    all_to_all x1, blocking collectives, body(): y = lax.all_to_all(x, 'item', 0, 0, tiled=True)  29.7 us
    all_to_all x1, blocking collectives, body(): z = lax.all_to_all(z, 'item', 0, 0, tiled=True)  21.7 us
    all_to_all x1, blocking collectives, body(): v = lax.all_to_all(v, 'user', 0, 0, tiled=True, axis_index_groups=chips)  16.3 us
    all_to_all x1, blocking collectives, body(): lax.all_to_all(owned, 'user', 0, 0, tiled=True, axis_index_groups=chips)  11 us
    pallas_call x1, Pallas kernels, body(): call(user_kernel, [pltpu.VMEM((PIECES, PIECE, BLK), F32)], [HBM, HBM, HBM...  3.85 us
    pallas_call x1, Pallas kernels, body(): call(item_kernel, [jax.ShapeDtypeStruct((USERS, BLK), F32), pltpu.VMEM((8...  2.73 us
    ppermute x1, starting transfers between devices, body(): theirs = lax.ppermute(mine, 'user', swap)  2.72 us
    ppermute x1, starting transfers between devices, body(): received = lax.ppermute(other, 'user', swap)  2.17 us
  transfers between devices with their start and end apart: 2, of which 1 were waited for; matrix products, arithmetic and copies ran while one was open for 0% of the time, Pallas kernels for 2%

profile of v5, /device:TPU:1, one launch (start us, length us, event | category | flops | bytes accessed | tf_op | source)
XLA Modules:
  0.0 94.8 jit_solution(10389641732029496303)
XLA Ops:
  0.6 0.0 copy-start.2
  0.6 0.0 copy-start.3
  0.6 3.9 %shard_map.68 = f32[16,80,128]{2,1,0:T(8,128)S(1)} custom-call(s32[6,12]{1,0:T(8,128)} %m_ref.3, bf16[768,1536]{1,0:T(8,128)(2,1)} %r_ref.3, f32[768,128]{1,0:T(8,128)} %p_ref.1, f32[1536,128]{1,0:T(8,128)} %q_ref.5), custom_call_target="tpu_custom_call" | custom-call | tf_op jit(solution)/shard_map/pallas_call | solution.py:290
  4.5 0.0 copy-start
  4.5 0.0 copy-start.1
  4.5 0.0 copy-start.4
  4.5 29.7 %all_to_all.20.y_ref = f32[16,80,128]{2,1,0:T(8,128)S(1)} all-to-all(f32[16,80,128]{2,1,0:T(8,128)S(1)} %shard_map.68), channel_id=1, replica_groups=mesh['user'=16,'item'=16] {'item'}, dimensions={0} | all-to-all | bytes 1310720 | tf_op jit(solution)/shard_map/all_to_all | solution.py:309
  34.3 0.1 shard_map.69
  34.3 21.7 %all_to_all.21.z_ref = f32[16,72,128]{2,1,0:T(8,128)S(1)} all-to-all(f32[16,72,128]{2,1,0:T(8,128)S(1)} %get-tuple-element.8), channel_id=1, replica_groups=mesh['user'=16,'item'=16] {'item'}, dimensions={0} | all-to-all | bytes 1179648 | tf_op jit(solution)/shard_map/all_to_all | solution.py:313
  56.0 0.0 copy-done.2
  56.0 0.0 copy-done.3
  56.0 0.0 copy-done
  56.0 0.0 copy-done.1
  56.0 0.0 copy-done.4
  56.0 2.7 %shard_map.70 = (f32[768,128]{1,0:T(8,128)}, f32[8,104,128]{2,1,0:T(8,128)S(1)}, bf16[256,768]{1,0:T(8,128)(2,1)S(1)}, f32[6,128,128]{2,1,0:T(8,128)S(1)}) custom-call(s32[6,12]{1,0:T(8,128)S(1)} %copy-done.3, f32[2]{0:T(128)S(1)} %copy-done.4, bf16[768,1536]{1,0:T(8,128)(2,1)S(1)} %copy-done, f32[768,128]{1,0:T(8,128)S(1)} %copy-done.2, ...), custom_call_target="tpu_custom_call" | custom-call | tf_op jit(solution)/shard_map/pallas_call | solution.py:314
  58.8 2.2 %collective-permute-start = (f32[8,104,128]{2,1,0:T(8,128)S(1)}, f32[8,104,128]{2,1,0:T(8,128)S(1)}, u32[]{:S(2)}, u32[]{:S(2)}) collective-permute-start(f32[8,104,128]{2,1,0:T(8,128)S(1)} %get-tuple-element.13), channel_id=1, source_target_pairs={{0,16},{16,0},{32,48},{48,32},{64,80},{80,64},{96,112},{112,96},{1... | collective-permute-start | bytes 1277960 | tf_op jit(solution)/shard_map/ppermute | solution.py:325
  60.9 1.5 %shard_map.71 = f32[8,104,128]{2,1,0:T(8,128)S(1)} custom-call(s32[6,12]{1,0:T(8,128)S(1)} %copy-done.3, f32[2]{0:T(128)S(1)} %copy-done.4, bf16[768,1536]{1,0:T(8,128)(2,1)S(1)} %copy-done, f32[1536,128]{1,0:T(8,128)S(1)} %copy-done.1, bf16[256,768]{1,0:T(8,128)(2,1)S(1)} %get-tuple-element.11.turned_ref, f32[6,128,128]{2,1,0:T(8,128)S(1)} %get-tuple-element.12.grams), custom_call_target="tpu_custom_call" | custom-call | flops 4294967296 | bytes 8388608 | tf_op jit(solution)/shard_map/pallas_call | solution.py:326
  62.5 0.0 collective-permute-done
  62.5 16.3 %all_to_all.22.v_ref = f32[8,104,128]{2,1,0:T(8,128)S(1)} all-to-all(f32[8,104,128]{2,1,0:T(8,128)S(1)} %add.3), channel_id=1, replica_groups={{0,32,64,96,128,160,192,224},{16,48,80,112,144,176,208,240},{1,33,65,97..., dimensions={0} | all-to-all | bytes 851968 | tf_op jit(solution)/shard_map/all_to_all | solution.py:334
  78.8 0.1 shard_map.72
  79.0 11.0 %all_to_all.23.half_ref = f32[8,96,128]{2,1,0:T(8,128)S(1)} all-to-all(f32[8,96,128]{2,1,0:T(8,128)S(1)} %shard_map.72), channel_id=1, replica_groups={{0,32,64,96,128,160,192,224},{16,48,80,112,144,176,208,240},{1,33,65,97..., dimensions={0} | all-to-all | bytes 786432 | tf_op jit(solution)/shard_map/all_to_all | solution.py:338
  89.9 2.7 %collective-permute-start.1 = (f32[8,96,128]{2,1,0:T(8,128)S(1)}, f32[8,96,128]{2,1,0:T(8,128)S(1)}, u32[]{:S(2)}, u32[]{:S(2)}) collective-permute-start(f32[8,96,128]{2,1,0:T(8,128)S(1)} %all_to_all.23.half_ref), channel_id=1, source_target_pairs={{0,16},{16,0},{32,48},{48,32},{64,80},{80,64},{96,112},{112,96},{1... | collective-permute-start | bytes 1179656 | tf_op jit(solution)/shard_map/ppermute | solution.py:339
  92.6 0.8 shard_map.73.whole
  93.5 0.5 collective-permute-done.1.half_ref
  94.0 0.8 shard_map.74
  (1 shorter events, 0.0 us)
Async XLA Ops:
  0.6 55.4 %copy-start.2 = (f32[768,128]{1,0:T(8,128)S(1)}, f32[768,128]{1,0:T(8,128)}, u32[]{:S(2)}) copy-start(f32[768,128]{1,0:T(8,128)} %p_ref.1) | copy-start | bytes 1179652
  0.6 55.4 %copy-start.3 = (s32[6,12]{1,0:T(8,128)S(1)}, s32[6,12]{1,0:T(8,128)}, u32[]{:S(2)}) copy-start(s32[6,12]{1,0:T(8,128)} %m_ref.3) | copy-start | bytes 868
  4.5 51.5 %copy-start = (bf16[768,1536]{1,0:T(8,128)(2,1)S(1)}, bf16[768,1536]{1,0:T(8,128)(2,1)}, u32[]{:S(2)}) copy-start(bf16[768,1536]{1,0:T(8,128)(2,1)} %r_ref.3) | copy-start | bytes 7077892
  4.5 51.5 %copy-start.1 = (f32[1536,128]{1,0:T(8,128)S(1)}, f32[1536,128]{1,0:T(8,128)}, u32[]{:S(2)}) copy-start(f32[1536,128]{1,0:T(8,128)} %q_ref.5) | copy-start | bytes 2359300
  4.5 51.5 %copy-start.4 = (f32[2]{0:T(128)S(1)}, f32[2]{0:T(128)}, u32[]{:S(2)}) copy-start(f32[2]{0:T(128)} %step_ref.3) | copy-start | bytes 28
  58.8 3.7 %collective-permute-start = (f32[8,104,128]{2,1,0:T(8,128)S(1)}, f32[8,104,128]{2,1,0:T(8,128)S(1)}, u32[]{:S(2)}, u32[]{:S(2)}) collective-permute-start(f32[8,104,128]{2,1,0:T(8,128)S(1)} %get-tuple-element.13), channel_id=1, source_target_pairs={{0,16},{16,0},{32,48},{48,32},{64,80},{80,64},{96,112},{112,96},{1... | collective-permute-start | bytes 1277960 | tf_op jit(solution)/shard_map/ppermute | solution.py:325
  89.9 4.1 %collective-permute-start.1 = (f32[8,96,128]{2,1,0:T(8,128)S(1)}, f32[8,96,128]{2,1,0:T(8,128)S(1)}, u32[]{:S(2)}, u32[]{:S(2)}) collective-permute-start(f32[8,96,128]{2,1,0:T(8,128)S(1)} %all_to_all.23.half_ref), channel_id=1, source_target_pairs={{0,16},{16,0},{32,48},{48,32},{64,80},{80,64},{96,112},{112,96},{1... | collective-permute-start | bytes 1179656 | tf_op jit(solution)/shard_map/ppermute | solution.py:339

commit v6 on v5

--- a/solution.py
+++ b/solution.py
@@ -14,7 +14,7 @@
 ROWS = USERS // PIECES
 HROWS = UB * 64 // PIECES
 SENT = ROWS + HROWS
-PIECE = SENT + 8
+TILES = SENT // 4 + 1
 CHUNK = ITEMS // 16
 F32 = jnp.float32
 BF16 = jnp.bfloat16
@@ -111,13 +111,14 @@
 def user_kernel(
     m_hbm, r_hbm, p_hbm, q_hbm, x_ref, m_ref, r_ref, p_ref, q_ref, qcat, grams, packed, r_sem, q_sem, p_sem, m_sem
 ):
+    q_copies = fetch(q_hbm, q_ref, q_sem, 4)
     m_copy = pltpu.make_async_copy(m_hbm, m_ref, m_sem)
     m_copy.start()
-    q_copies = fetch(q_hbm, q_ref, q_sem, 4)
     p_copies = fetch(p_hbm, p_ref, p_sem, 2)
     r_copies = fetch(r_hbm, r_ref, r_sem, UB)
-    arrive(q_copies)
     for j in range(IB):
+        if j in (0, 3):
+            arrive(q_copies[:1] if j == 0 else q_copies[1:])
         q = q_ref[block(j)]
         both = split(q, 1)
         qcat[block(j)] = both
@@ -138,33 +139,40 @@
             turned = jnp.concatenate([h[64:, 64:], h[64:, :64]], axis=1)
             packed[b * 64 : (b + 1) * 64] = jnp.where((lane64 < 64) & (lane64 > row64), turned, h[:64])
             diagonal = jnp.sum(jnp.where(lane64 == row64 + 64, h[64:], 0.0), axis=0, keepdims=True)
-            extra = extra + jnp.where(extra_row == b, jnp.broadcast_to(diagonal, (8, BLK)), 0.0)
-            extra = extra + jnp.where((extra_row == 6) & (extra_lane == b), count.astype(F32), 0.0)
+            if b % 2:
+                diagonal = jnp.concatenate([diagonal[:, 64:], diagonal[:, :64]], axis=1)
+            extra = extra + jnp.where(extra_row == b // 2, jnp.broadcast_to(diagonal, (8, BLK)), 0.0)
+            extra = extra + jnp.where((extra_row == 3) & (extra_lane == b), count.astype(F32), 0.0)
             corrections.append(exact(p_ref[block(b)], h))
         masked = only_present(m_ref, r_ref, three, 0, 0, IB)
         found = halves(jnp.dot(masked, qcat[...], preferred_element_type=F32))
         d = found - jnp.concatenate(corrections, axis=0)
-        for k in range(8):
-            x_ref[half * 8 + k, :ROWS] = d[k * ROWS : (k + 1) * ROWS]
+        for k in range(8 * ROWS // 4):
+            x_ref[half * 8 + k // 12, k % 12] = d[k * 4 : (k + 1) * 4]
     for piece in range(PIECES):
-        x_ref[piece, ROWS : ROWS + HROWS] = packed[piece * HROWS : (piece + 1) * HROWS]
-        x_ref[piece, SENT:] = extra
-
-
-def total_kernel(y_ref, z_ref, extra_ref):
-    total = y_ref[0]
-    for k in range(1, PIECES):
-        total = total + y_ref[k]
-    extra_ref[...] = total[SENT:]
-    for k in range(PIECES):
-        z_ref[k] = total[:SENT]
+        for k in range(HROWS // 4):
+            x_ref[piece, ROWS // 4 + k] = packed[piece * HROWS + k * 4 : piece * HROWS + (k + 1) * 4]
+        x_ref[piece, SENT // 4] = extra[:4]
+
+
+def total_kernel(y_ref, z_ref, extra_ref, rows):
+    for k in range(TILES):
+        total = y_ref[0, k]
+        for piece in range(1, PIECES):
+            total = total + y_ref[piece, k]
+        rows[k * 4 : (k + 1) * 4] = total
+    extra_ref[...] = rows[SENT : SENT + 8]
+    total = rows[:SENT]
+    for piece in range(PIECES):
+        z_ref[piece] = total
 
 
 def item_kernel(
     m_ref, step_ref, r_ref, p_ref, q_ref, z_ref, extra_ref, new_ref, other_ref, turned_ref, grams
 ):
     extra = extra_ref[...]
-    scales = step_ref[0] / (BLK * (1.0 + extra[6:7]))
+    scales = step_ref[0] / (BLK * (1.0 + extra[3:4]))
+    flipped = jnp.concatenate([extra[:, 64:], extra[:, :64]], axis=1)
     row64, lane64 = sublanes((64, BLK)), lanes((64, BLK))
     for b in range(UB):
         tiles = []
@@ -181,7 +189,7 @@
         top = jnp.where(lane64 < row64, half, jnp.where(lane64 == row64, 0.5 * half, 0.0))
         top = jnp.where(lane64 >= 64, half, top)
         bottom = jnp.where(lane64 > row64 + 64, turned, 0.0)
-        bottom = jnp.where(lane64 == row64 + 64, 0.5 * extra[b : b + 1], bottom)
+        bottom = jnp.where(lane64 == row64 + 64, 0.5 * (flipped if b % 2 else extra)[b // 2 : b // 2 + 1], bottom)
         w = jnp.concatenate([top, bottom], axis=0)
         s = scales[:, b : b + 1]
         new = p_ref[block(b)] + (2.0 * s) * d - (s * s) * exact(d, w + w.T)
@@ -222,9 +230,11 @@
         o_ref[piece, CHUNK:] = counts
 
 
-def own_kernel(m_ref, step_ref, r_ref, q_ref, turned_ref, grams, own_ref):
+def own_kernel(m_ref, step_ref, r_ref, q_ref, turned_ref, grams, new_ref, own_ref, o_hbm, sem):
+    copies = fetch(new_ref, o_hbm, sem, 2)
     core = lax.rem(lax.axis_index("user"), 2)
     item_half(core, m_ref, step_ref, r_ref, q_ref, turned_ref, grams, own_ref)
+    arrive(copies)
 
 
 def scale_kernel(v_ref, q_ref, o_ref):
@@ -247,9 +257,9 @@
     core = lax.rem(lax.axis_index("user"), 2)
     side = 1 - core if flip else core
     copies = []
-    for k in range(8):
-        rows = pl.ds(pl.multiple_of(side * (ITEMS // 2) + k * CHUNK, 8), CHUNK)
-        copies.append(pltpu.make_async_copy(half_ref.at[k], o_hbm.at[rows], sem.at[k]))
+    for k in range(4):
+        rows = pl.ds(pl.multiple_of(side * (ITEMS // 2) + k * 192, 8), 192)
+        copies.append(pltpu.make_async_copy(half_ref.at[pl.ds(k * 192, 192)], o_hbm.at[rows], sem.at[k]))
         copies[-1].start()
     arrive(copies)
 
@@ -276,7 +286,7 @@
         kernel,
         out_shape=out_shapes[0] if single else out_shapes,
         in_specs=specs,
-        out_specs=out_specs if single else [out_specs] * len(out_shapes),
+        out_specs=out_specs if single or isinstance(out_specs, list) else [out_specs] * len(out_shapes),
         scratch_shapes=scratch,
         compiler_params=pltpu.CompilerParams(vmem_limit_bytes=limit << 20),
         cost_estimate=cost,
@@ -289,7 +299,7 @@
     chips = [[k + 2 * j for j in range(8)] for k in range(2)]
     x = call(
         user_kernel,
-        [pltpu.VMEM((PIECES, PIECE, BLK), F32)],
+        [pltpu.VMEM((PIECES, TILES, 4, BLK), F32)],
         [HBM, HBM, HBM, HBM],
         [
             pltpu.SMEM((UB, IB), jnp.int32),
@@ -308,13 +318,16 @@
     )(far(presence), far(ratings), far(user_factors), far(item_factors))
     y = lax.all_to_all(x, "item", 0, 0, tiled=True)
     z, extra = call(
-        total_kernel, [pltpu.VMEM((PIECES, SENT, BLK), F32), pltpu.VMEM((8, BLK), F32)], [VMEM]
+        total_kernel,
+        [pltpu.VMEM((PIECES, SENT, BLK), F32), pltpu.VMEM((8, BLK), F32)],
+        [VMEM],
+        [pltpu.VMEM((SENT + 8, BLK), F32)],
     )(near(y))
     z = lax.all_to_all(z, "item", 0, 0, tiled=True)
-    new_users, other, turned, grams = call(
+    new, other, turned, grams = call(
         item_kernel,
         [
-            jax.ShapeDtypeStruct((USERS, BLK), F32),
+            pltpu.VMEM((USERS, BLK), F32),
             pltpu.VMEM((8, CHUNK + 8, BLK), F32),
             pltpu.VMEM((2 * BLK, USERS), BF16),
             pltpu.VMEM((UB, BLK, BLK), F32),
@@ -323,13 +336,15 @@
         limit=16,
     )(presence, step_sizes, near(ratings), near(user_factors), near(item_factors), near(z), near(extra))
     received = lax.ppermute(other, "user", swap)
-    own = call(
+    own, new_users = call(
         own_kernel,
-        [pltpu.VMEM((8, CHUNK + 8, BLK), F32)],
-        [SMEM, SMEM, VMEM, VMEM, VMEM, VMEM],
+        [pltpu.VMEM((8, CHUNK + 8, BLK), F32), pltpu.HBM((USERS, BLK), F32)],
+        [SMEM, SMEM, VMEM, VMEM, VMEM, VMEM, VMEM],
+        [pltpu.SemaphoreType.DMA((2,))],
         limit=16,
+        out_specs=[VMEM, HBM],
         cost=pl.CostEstimate(flops=1 << 32, bytes_accessed=1 << 23, transcendentals=0),
-    )(presence, step_sizes, near(ratings), near(item_factors), near(turned), near(grams))
+    )(presence, step_sizes, near(ratings), near(item_factors), near(turned), near(grams), near(new))
     v = own + received
     v = lax.all_to_all(v, "user", 0, 0, tiled=True, axis_index_groups=chips)
     owned = call(scale_kernel, [pltpu.VMEM((8, CHUNK, BLK), F32)], [VMEM, VMEM])(
@@ -341,18 +356,18 @@
         place_own_kernel,
         [pltpu.HBM((ITEMS, BLK), F32)],
         [VMEM],
-        [pltpu.SemaphoreType.DMA((8,))],
+        [pltpu.SemaphoreType.DMA((4,))],
         out_specs=HBM,
         cost=pl.CostEstimate(flops=1 << 30, bytes_accessed=1 << 22, transcendentals=0),
-    )(near(mine))
+    )(near(mine.reshape(ITEMS // 2, BLK)))
     new_items = call(
         place_other_kernel,
         [pltpu.HBM((ITEMS, BLK), F32)],
         [VMEM, HBM],
-        [pltpu.SemaphoreType.DMA((8,))],
+        [pltpu.SemaphoreType.DMA((4,))],
         out_specs=HBM,
         alias={1: 0},
-    )(near(theirs), half)
+    )(near(theirs.reshape(ITEMS // 2, BLK)), half)
     return new_users, new_items
 
 

time: 95 us -> 94.6 us (level)
  transfers between devices with their start and end apart: 2 -> 2, of which waited for: 1 -> 1; matrix products, arithmetic and copies ran while one was open for 0% -> 0% of each run, Pallas kernels for 2% -> 3%
where the time goes in v6:
time: 94.6 us; the launch traced here: 94.3 us
  blocking collectives  78 us (82%)
  Pallas kernels  9.84 us (10%)
  starting transfers between devices  5.11 us (5%)
    all_to_all x1, blocking collectives, body(): y = lax.all_to_all(x, 'item', 0, 0, tiled=True)  29.3 us
    all_to_all x1, blocking collectives, body(): z = lax.all_to_all(z, 'item', 0, 0, tiled=True)  21 us
    all_to_all x1, blocking collectives, body(): v = lax.all_to_all(v, 'user', 0, 0, tiled=True, axis_index_groups=chips)  16.2 us
    all_to_all x1, blocking collectives, body(): lax.all_to_all(owned, 'user', 0, 0, tiled=True, axis_index_groups=chips)  11.4 us
    pallas_call x1, Pallas kernels, body(): call(user_kernel, [pltpu.VMEM((PIECES, TILES, 4, BLK), F32)], [HBM, HBM,...  3.82 us
    ppermute x1, starting transfers between devices, body(): received = lax.ppermute(other, 'user', swap)  2.6 us
    ppermute x1, starting transfers between devices, body(): theirs = lax.ppermute(mine, 'user', swap)  2.51 us
    pallas_call x1, Pallas kernels, body(): call(item_kernel, [pltpu.VMEM((USERS, BLK), F32), pltpu.VMEM((8, CHUNK +...  2.37 us
  transfers between devices with their start and end apart: 2, of which 1 were waited for; matrix products, arithmetic and copies ran while one was open for 0% of the time, Pallas kernels for 3%

profile of v6, /device:TPU:1, one launch (start us, length us, event | category | flops | bytes accessed | tf_op | source)
XLA Modules:
  0.0 94.3 jit_solution(15990847863538130576)
XLA Ops:
  0.6 0.0 copy-start.1
  0.6 3.8 %shard_map.68 = f32[16,19,4,128]{3,2,1,0:T(4,128)S(1)} custom-call(s32[6,12]{1,0:T(8,128)} %m_ref.3, bf16[768,1536]{1,0:T(8,128)(2,1)} %r_ref.3, f32[768,128]{1,0:T(8,128)} %p_ref.1, f32[1536,128]{1,0:T(8,128)} %q_ref.5), custom_call_target="tpu_custom_call" | custom-call | tf_op jit(solution)/shard_map/pallas_call | solution.py:300
  4.5 0.0 copy-start
  4.5 0.0 copy-start.2
  4.5 0.0 copy-start.3
  4.5 0.0 copy-start.4
  4.5 29.3 %all_to_all.20.y_ref = f32[16,19,4,128]{3,2,1,0:T(4,128)S(1)} all-to-all(f32[16,19,4,128]{3,2,1,0:T(4,128)S(1)} %shard_map.68), channel_id=1, replica_groups=mesh['user'=16,'item'=16] {'item'}, dimensions={0} | all-to-all | bytes 1245184 | tf_op jit(solution)/shard_map/all_to_all | solution.py:319
  33.8 0.1 shard_map.69
  33.9 21.0 %all_to_all.21.z_ref = f32[16,72,128]{2,1,0:T(8,128)S(1)} all-to-all(f32[16,72,128]{2,1,0:T(8,128)S(1)} %get-tuple-element.10), channel_id=1, replica_groups=mesh['user'=16,'item'=16] {'item'}, dimensions={0} | all-to-all | bytes 1179648 | tf_op jit(solution)/shard_map/all_to_all | solution.py:326
  54.9 0.0 copy-done.1
  54.9 0.0 copy-done
  54.9 0.0 copy-done.2
  54.9 0.0 copy-done.3
  54.9 0.0 copy-done.4
  55.0 2.4 %shard_map.70 = (f32[768,128]{1,0:T(8,128)S(1)}, f32[8,104,128]{2,1,0:T(8,128)S(1)}, bf16[256,768]{1,0:T(8,128)(2,1)S(1)}, f32[6,128,128]{2,1,0:T(8,128)S(1)}) custom-call(s32[6,12]{1,0:T(8,128)S(1)} %copy-done.3, f32[2]{0:T(128)S(1)} %copy-done.4, bf16[768,1536]{1,0:T(8,128)(2,1)S(1)} %copy-done, f32[768,128]{1,0:T(8,128)S(1)} %copy-done.2, ...), custom_call_target="tpu_custom_call" | custom-call | tf_op jit(solution)/shard_map/pallas_call | solution.py:327
  57.3 2.6 %collective-permute-start = (f32[8,104,128]{2,1,0:T(8,128)S(1)}, f32[8,104,128]{2,1,0:T(8,128)S(1)}, u32[]{:S(2)}, u32[]{:S(2)}) collective-permute-start(f32[8,104,128]{2,1,0:T(8,128)S(1)} %get-tuple-element.17), channel_id=1, source_target_pairs={{0,16},{16,0},{32,48},{48,32},{64,80},{80,64},{96,112},{112,96},{1... | collective-permute-start | bytes 1277960 | tf_op jit(solution)/shard_map/ppermute | solution.py:338
  59.9 1.9 %shard_map.71 = (f32[8,104,128]{2,1,0:T(8,128)S(1)}, f32[768,128]{1,0:T(8,128)}) custom-call(s32[6,12]{1,0:T(8,128)S(1)} %copy-done.3, f32[2]{0:T(128)S(1)} %copy-done.4, bf16[768,1536]{1,0:T(8,128)(2,1)S(1)} %copy-done, f32[1536,128]{1,0:T(8,128)S(1)} %copy-done.1, bf16[256,768]{1,0:T(8,128)(2,1)S(1)} %get-tuple-element.12.turned_ref, ...), custom_call_target="tpu_custom_call" | custom-call | flops 4294967296 | bytes 8388608 | tf_op jit(solution)/shard_map/pallas_call | solution.py:339
  61.8 0.0 collective-permute-done
  61.8 0.1 add.3
  61.9 16.2 %all_to_all.22.v_ref = f32[8,104,128]{2,1,0:T(8,128)S(1)} all-to-all(f32[8,104,128]{2,1,0:T(8,128)S(1)} %add.3), channel_id=1, replica_groups={{0,32,64,96,128,160,192,224},{16,48,80,112,144,176,208,240},{1,33,65,97..., dimensions={0} | all-to-all | bytes 851968 | tf_op jit(solution)/shard_map/all_to_all | solution.py:349
  78.1 0.1 shard_map.72
  78.3 11.4 %all_to_all.23 = f32[8,96,128]{2,1,0:T(8,128)S(1)} all-to-all(f32[8,96,128]{2,1,0:T(8,128)S(1)} %shard_map.72), channel_id=1, replica_groups={{0,32,64,96,128,160,192,224},{16,48,80,112,144,176,208,240},{1,33,65,97..., dimensions={0} | all-to-all | bytes 786432 | tf_op jit(solution)/shard_map/all_to_all | solution.py:353
  89.7 2.5 %collective-permute-start.1 = (f32[8,96,128]{2,1,0:T(8,128)S(1)}, f32[8,96,128]{2,1,0:T(8,128)S(1)}, u32[]{:S(2)}, u32[]{:S(2)}) collective-permute-start(f32[8,96,128]{2,1,0:T(8,128)S(1)} %all_to_all.23), channel_id=1, source_target_pairs={{0,16},{16,0},{32,48},{48,32},{64,80},{80,64},{96,112},{112,96},{1... | collective-permute-start | bytes 1179656 | tf_op jit(solution)/shard_map/ppermute | solution.py:354
  92.2 0.8 shard_map.73.whole
  93.0 0.6 collective-permute-done.1
  93.5 0.8 shard_map.74
Async XLA Ops:
  0.6 54.3 %copy-start.1 = (f32[1536,128]{1,0:T(8,128)S(1)}, f32[1536,128]{1,0:T(8,128)}, u32[]{:S(2)}) copy-start(f32[1536,128]{1,0:T(8,128)} %q_ref.5) | copy-start | bytes 2359300
  4.5 50.5 %copy-start = (bf16[768,1536]{1,0:T(8,128)(2,1)S(1)}, bf16[768,1536]{1,0:T(8,128)(2,1)}, u32[]{:S(2)}) copy-start(bf16[768,1536]{1,0:T(8,128)(2,1)} %r_ref.3) | copy-start | bytes 7077892
  4.5 50.5 %copy-start.2 = (f32[768,128]{1,0:T(8,128)S(1)}, f32[768,128]{1,0:T(8,128)}, u32[]{:S(2)}) copy-start(f32[768,128]{1,0:T(8,128)} %p_ref.1) | copy-start | bytes 1179652
  4.5 50.4 %copy-start.3 = (s32[6,12]{1,0:T(8,128)S(1)}, s32[6,12]{1,0:T(8,128)}, u32[]{:S(2)}) copy-start(s32[6,12]{1,0:T(8,128)} %m_ref.3) | copy-start | bytes 868
  4.5 50.4 %copy-start.4 = (f32[2]{0:T(128)S(1)}, f32[2]{0:T(128)}, u32[]{:S(2)}) copy-start(f32[2]{0:T(128)} %step_ref.3) | copy-start | bytes 28
  57.3 4.5 %collective-permute-start = (f32[8,104,128]{2,1,0:T(8,128)S(1)}, f32[8,104,128]{2,1,0:T(8,128)S(1)}, u32[]{:S(2)}, u32[]{:S(2)}) collective-permute-start(f32[8,104,128]{2,1,0:T(8,128)S(1)} %get-tuple-element.17), channel_id=1, source_target_pairs={{0,16},{16,0},{32,48},{48,32},{64,80},{80,64},{96,112},{112,96},{1... | collective-permute-start | bytes 1277960 | tf_op jit(solution)/shard_map/ppermute | solution.py:338
  89.7 3.9 %collective-permute-start.1 = (f32[8,96,128]{2,1,0:T(8,128)S(1)}, f32[8,96,128]{2,1,0:T(8,128)S(1)}, u32[]{:S(2)}, u32[]{:S(2)}) collective-permute-start(f32[8,96,128]{2,1,0:T(8,128)S(1)} %all_to_all.23), channel_id=1, source_target_pairs={{0,16},{16,0},{32,48},{48,32},{64,80},{80,64},{96,112},{112,96},{1... | collective-permute-start | bytes 1179656 | tf_op jit(solution)/shard_map/ppermute | solution.py:354

commit v7 on v6

--- a/solution.py
+++ b/solution.py
@@ -127,28 +127,26 @@
     extra_row, extra_lane = sublanes((8, BLK)), lanes((8, BLK))
     extra = jnp.zeros((8, BLK), F32)
     arrive([m_copy] + p_copies + r_copies)
-    for half in range(2):
-        three = range(half * 3, half * 3 + 3)
-        corrections = []
-        for b in three:
-            h = jnp.zeros((BLK, BLK), F32)
-            count = jnp.int32(0)
-            for j in range(IB):
-                h = h + present(m_ref, b, j) * grams[j]
-                count = count + m_ref[b, j]
-            turned = jnp.concatenate([h[64:, 64:], h[64:, :64]], axis=1)
-            packed[b * 64 : (b + 1) * 64] = jnp.where((lane64 < 64) & (lane64 > row64), turned, h[:64])
-            diagonal = jnp.sum(jnp.where(lane64 == row64 + 64, h[64:], 0.0), axis=0, keepdims=True)
-            if b % 2:
-                diagonal = jnp.concatenate([diagonal[:, 64:], diagonal[:, :64]], axis=1)
-            extra = extra + jnp.where(extra_row == b // 2, jnp.broadcast_to(diagonal, (8, BLK)), 0.0)
-            extra = extra + jnp.where((extra_row == 3) & (extra_lane == b), count.astype(F32), 0.0)
-            corrections.append(exact(p_ref[block(b)], h))
-        masked = only_present(m_ref, r_ref, three, 0, 0, IB)
-        found = halves(jnp.dot(masked, qcat[...], preferred_element_type=F32))
-        d = found - jnp.concatenate(corrections, axis=0)
-        for k in range(8 * ROWS // 4):
-            x_ref[half * 8 + k // 12, k % 12] = d[k * 4 : (k + 1) * 4]
+    masked = only_present(m_ref, r_ref, range(UB), 0, 0, IB)
+    found = halves(jnp.dot(masked, qcat[...], preferred_element_type=F32))
+    corrections = []
+    for b in range(UB):
+        h = jnp.zeros((BLK, BLK), F32)
+        count = jnp.int32(0)
+        for j in range(IB):
+            h = h + present(m_ref, b, j) * grams[j]
+            count = count + m_ref[b, j]
+        turned = jnp.concatenate([h[64:, 64:], h[64:, :64]], axis=1)
+        packed[b * 64 : (b + 1) * 64] = jnp.where((lane64 < 64) & (lane64 > row64), turned, h[:64])
+        diagonal = jnp.sum(jnp.where(lane64 == row64 + 64, h[64:], 0.0), axis=0, keepdims=True)
+        if b % 2:
+            diagonal = jnp.concatenate([diagonal[:, 64:], diagonal[:, :64]], axis=1)
+        extra = extra + jnp.where(extra_row == b // 2, jnp.broadcast_to(diagonal, (8, BLK)), 0.0)
+        extra = extra + jnp.where((extra_row == 3) & (extra_lane == b), count.astype(F32), 0.0)
+        corrections.append(exact(p_ref[block(b)], h))
+    d = found - jnp.concatenate(corrections, axis=0)
+    for k in range(PIECES * ROWS // 4):
+        x_ref[k // 12, k % 12] = d[k * 4 : (k + 1) * 4]
     for piece in range(PIECES):
         for k in range(HROWS // 4):
             x_ref[piece, ROWS // 4 + k] = packed[piece * HROWS + k * 4 : piece * HROWS + (k + 1) * 4]
@@ -230,11 +228,9 @@
         o_ref[piece, CHUNK:] = counts
 
 
-def own_kernel(m_ref, step_ref, r_ref, q_ref, turned_ref, grams, new_ref, own_ref, o_hbm, sem):
-    copies = fetch(new_ref, o_hbm, sem, 2)
+def own_kernel(m_ref, step_ref, r_ref, q_ref, turned_ref, grams, own_ref):
     core = lax.rem(lax.axis_index("user"), 2)
     item_half(core, m_ref, step_ref, r_ref, q_ref, turned_ref, grams, own_ref)
-    arrive(copies)
 
 
 def scale_kernel(v_ref, q_ref, o_ref):
@@ -253,23 +249,23 @@
             o_ref[piece, k * 32 : (k + 1) * 32] = new
 
 
-def place_kernel(flip, half_ref, whole, o_hbm, sem):
-    core = lax.rem(lax.axis_index("user"), 2)
-    side = 1 - core if flip else core
+def place(side, half_ref, o_hbm, sem):
     copies = []
     for k in range(4):
         rows = pl.ds(pl.multiple_of(side * (ITEMS // 2) + k * 192, 8), 192)
         copies.append(pltpu.make_async_copy(half_ref.at[pl.ds(k * 192, 192)], o_hbm.at[rows], sem.at[k]))
         copies[-1].start()
-    arrive(copies)
-
-
-def place_own_kernel(half_ref, o_hbm, sem):
-    place_kernel(False, half_ref, None, o_hbm, sem)
+    return copies
+
+
+def place_own_kernel(half_ref, new_ref, o_hbm, new_hbm, sem, new_sem):
+    core = lax.rem(lax.axis_index("user"), 2)
+    arrive(place(core, half_ref, o_hbm, sem) + fetch(new_ref, new_hbm, new_sem, 4))
 
 
 def place_other_kernel(half_ref, whole, o_hbm, sem):
-    place_kernel(True, half_ref, whole, o_hbm, sem)
+    core = lax.rem(lax.axis_index("user"), 2)
+    arrive(place(1 - core, half_ref, o_hbm, sem))
 
 
 def near(value):
@@ -336,15 +332,13 @@
         limit=16,
     )(presence, step_sizes, near(ratings), near(user_factors), near(item_factors), near(z), near(extra))
     received = lax.ppermute(other, "user", swap)
-    own, new_users = call(
+    own = call(
         own_kernel,
-        [pltpu.VMEM((8, CHUNK + 8, BLK), F32), pltpu.HBM((USERS, BLK), F32)],
-        [SMEM, SMEM, VMEM, VMEM, VMEM, VMEM, VMEM],
-        [pltpu.SemaphoreType.DMA((2,))],
+        [pltpu.VMEM((8, CHUNK + 8, BLK), F32)],
+        [SMEM, SMEM, VMEM, VMEM, VMEM, VMEM],
         limit=16,
-        out_specs=[VMEM, HBM],
         cost=pl.CostEstimate(flops=1 << 32, bytes_accessed=1 << 23, transcendentals=0),
-    )(presence, step_sizes, near(ratings), near(item_factors), near(turned), near(grams), near(new))
+    )(presence, step_sizes, near(ratings), near(item_factors), near(turned), near(grams))
     v = own + received
     v = lax.all_to_all(v, "user", 0, 0, tiled=True, axis_index_groups=chips)
     owned = call(scale_kernel, [pltpu.VMEM((8, CHUNK, BLK), F32)], [VMEM, VMEM])(
@@ -352,14 +346,14 @@
     )
     mine = lax.all_to_all(owned, "user", 0, 0, tiled=True, axis_index_groups=chips)
     theirs = lax.ppermute(mine, "user", swap)
-    half = call(
+    half, new_users = call(
         place_own_kernel,
-        [pltpu.HBM((ITEMS, BLK), F32)],
-        [VMEM],
-        [pltpu.SemaphoreType.DMA((4,))],
+        [pltpu.HBM((ITEMS, BLK), F32), pltpu.HBM((USERS, BLK), F32)],
+        [VMEM, VMEM],
+        [pltpu.SemaphoreType.DMA((4,)), pltpu.SemaphoreType.DMA((4,))],
         out_specs=HBM,
         cost=pl.CostEstimate(flops=1 << 30, bytes_accessed=1 << 22, transcendentals=0),
-    )(near(mine.reshape(ITEMS // 2, BLK)))
+    )(near(mine.reshape(ITEMS // 2, BLK)), near(new))
     new_items = call(
         place_other_kernel,
         [pltpu.HBM((ITEMS, BLK), F32)],

time: 94.6 us -> 93.9 us (level)
  no operation moved by 1% of the time
where the time goes in v7:
time: 93.9 us; the launch traced here: 93.7 us
  blocking collectives  77.6 us (83%)
  Pallas kernels  9.57 us (10%)
  starting transfers between devices  5.32 us (6%)
    all_to_all x1, blocking collectives, body(): y = lax.all_to_all(x, 'item', 0, 0, tiled=True)  29.3 us
    all_to_all x1, blocking collectives, body(): z = lax.all_to_all(z, 'item', 0, 0, tiled=True)  21 us
    all_to_all x1, blocking collectives, body(): v = lax.all_to_all(v, 'user', 0, 0, tiled=True, axis_index_groups=chips)  16.3 us
    all_to_all x1, blocking collectives, body(): lax.all_to_all(owned, 'user', 0, 0, tiled=True, axis_index_groups=chips)  11 us
    pallas_call x1, Pallas kernels, body(): call(user_kernel, [pltpu.VMEM((PIECES, TILES, 4, BLK), F32)], [HBM, HBM,...  3.74 us
    ppermute x1, starting transfers between devices, body(): theirs = lax.ppermute(mine, 'user', swap)  2.72 us
    ppermute x1, starting transfers between devices, body(): received = lax.ppermute(other, 'user', swap)  2.6 us
    pallas_call x1, Pallas kernels, body(): call(item_kernel, [pltpu.VMEM((USERS, BLK), F32), pltpu.VMEM((8, CHUNK +...  2.36 us
  transfers between devices with their start and end apart: 2, of which 1 were waited for; matrix products, arithmetic and copies ran while one was open for 0% of the time, Pallas kernels for 3%

profile of v7, /device:TPU:1, one launch (start us, length us, event | category | flops | bytes accessed | tf_op | source)
XLA Modules:
  0.0 93.7 jit_solution(6995880053681648557)
XLA Ops:
  0.6 0.0 copy-start.1
  0.6 3.7 %shard_map.68 = f32[16,19,4,128]{3,2,1,0:T(4,128)S(1)} custom-call(s32[6,12]{1,0:T(8,128)} %m_ref.3, bf16[768,1536]{1,0:T(8,128)(2,1)} %r_ref.3, f32[768,128]{1,0:T(8,128)} %p_ref.1, f32[1536,128]{1,0:T(8,128)} %q_ref.5), custom_call_target="tpu_custom_call" | custom-call | tf_op jit(solution)/shard_map/pallas_call | solution.py:296
  4.4 0.0 copy-start
  4.4 0.0 copy-start.2
  4.4 0.0 copy-start.3
  4.4 0.0 copy-start.4
  4.4 29.3 %all_to_all.20.y_ref = f32[16,19,4,128]{3,2,1,0:T(4,128)S(1)} all-to-all(f32[16,19,4,128]{3,2,1,0:T(4,128)S(1)} %shard_map.68), channel_id=1, replica_groups=mesh['user'=16,'item'=16] {'item'}, dimensions={0} | all-to-all | bytes 1245184 | tf_op jit(solution)/shard_map/all_to_all | solution.py:315
  33.7 0.1 shard_map.69
  33.8 21.0 %all_to_all.21.z_ref = f32[16,72,128]{2,1,0:T(8,128)S(1)} all-to-all(f32[16,72,128]{2,1,0:T(8,128)S(1)} %get-tuple-element.10), channel_id=1, replica_groups=mesh['user'=16,'item'=16] {'item'}, dimensions={0} | all-to-all | bytes 1179648 | tf_op jit(solution)/shard_map/all_to_all | solution.py:322
  54.8 0.0 copy-done.1
  54.8 0.0 copy-done
  54.9 0.0 copy-done.2
  54.9 0.0 copy-done.3
  54.9 0.0 copy-done.4
  54.9 2.4 %shard_map.70 = (f32[768,128]{1,0:T(8,128)S(1)}, f32[8,104,128]{2,1,0:T(8,128)S(1)}, bf16[256,768]{1,0:T(8,128)(2,1)S(1)}, f32[6,128,128]{2,1,0:T(8,128)S(1)}) custom-call(s32[6,12]{1,0:T(8,128)S(1)} %copy-done.3, f32[2]{0:T(128)S(1)} %copy-done.4, bf16[768,1536]{1,0:T(8,128)(2,1)S(1)} %copy-done, f32[768,128]{1,0:T(8,128)S(1)} %copy-done.2, ...), custom_call_target="tpu_custom_call" | custom-call | tf_op jit(solution)/shard_map/pallas_call | solution.py:323
  57.2 2.6 %collective-permute-start = (f32[8,104,128]{2,1,0:T(8,128)S(1)}, f32[8,104,128]{2,1,0:T(8,128)S(1)}, u32[]{:S(2)}, u32[]{:S(2)}) collective-permute-start(f32[8,104,128]{2,1,0:T(8,128)S(1)} %get-tuple-element.14), channel_id=1, source_target_pairs={{0,16},{16,0},{32,48},{48,32},{64,80},{80,64},{96,112},{112,96},{1... | collective-permute-start | bytes 1277960 | tf_op jit(solution)/shard_map/ppermute | solution.py:334
  59.8 1.5 %shard_map.71 = f32[8,104,128]{2,1,0:T(8,128)S(1)} custom-call(s32[6,12]{1,0:T(8,128)S(1)} %copy-done.3, f32[2]{0:T(128)S(1)} %copy-done.4, bf16[768,1536]{1,0:T(8,128)(2,1)S(1)} %copy-done, f32[1536,128]{1,0:T(8,128)S(1)} %copy-done.1, bf16[256,768]{1,0:T(8,128)(2,1)S(1)} %get-tuple-element.12.turned_ref, f32[6,128,128]{2,1,0:T(8,128)S(1)} %get-tuple-element.13.grams), custom_call_target="tpu_custom_call" | custom-call | flops 4294967296 | bytes 8388608 | tf_op jit(solution)/shard_map/pallas_call | solution.py:335
  61.4 0.0 collective-permute-done
  61.4 16.3 %all_to_all.22.v_ref = f32[8,104,128]{2,1,0:T(8,128)S(1)} all-to-all(f32[8,104,128]{2,1,0:T(8,128)S(1)} %add.3), channel_id=1, replica_groups={{0,32,64,96,128,160,192,224},{16,48,80,112,144,176,208,240},{1,33,65,97..., dimensions={0} | all-to-all | bytes 851968 | tf_op jit(solution)/shard_map/all_to_all | solution.py:343
  77.7 0.1 shard_map.72
  77.8 11.0 %all_to_all.23 = f32[8,96,128]{2,1,0:T(8,128)S(1)} all-to-all(f32[8,96,128]{2,1,0:T(8,128)S(1)} %shard_map.72), channel_id=1, replica_groups={{0,32,64,96,128,160,192,224},{16,48,80,112,144,176,208,240},{1,33,65,97..., dimensions={0} | all-to-all | bytes 786432 | tf_op jit(solution)/shard_map/all_to_all | solution.py:347
  88.8 2.7 %collective-permute-start.1 = (f32[8,96,128]{2,1,0:T(8,128)S(1)}, f32[8,96,128]{2,1,0:T(8,128)S(1)}, u32[]{:S(2)}, u32[]{:S(2)}) collective-permute-start(f32[8,96,128]{2,1,0:T(8,128)S(1)} %all_to_all.23), channel_id=1, source_target_pairs={{0,16},{16,0},{32,48},{48,32},{64,80},{80,64},{96,112},{112,96},{1... | collective-permute-start | bytes 1179656 | tf_op jit(solution)/shard_map/ppermute | solution.py:348
  91.5 0.9 %shard_map.73 = (f32[1536,128]{1,0:T(8,128)}, f32[768,128]{1,0:T(8,128)}) custom-call(f32[768,128]{1,0:T(8,128)S(1)} %bitcast.2, f32[768,128]{1,0:T(8,128)S(1)} %get-tuple-element.15.new_ref), custom_call_target="tpu_custom_call" | custom-call | flops 1073741824 | bytes 4194304 | tf_op jit(solution)/shard_map/pallas_call | solution.py:349
  92.5 0.4 collective-permute-done.1
  92.9 0.8 shard_map.74
  (1 shorter events, 0.0 us)
Async XLA Ops:
  0.6 54.2 %copy-start.1 = (f32[1536,128]{1,0:T(8,128)S(1)}, f32[1536,128]{1,0:T(8,128)}, u32[]{:S(2)}) copy-start(f32[1536,128]{1,0:T(8,128)} %q_ref.5) | copy-start | bytes 2359300
  4.4 50.5 %copy-start = (bf16[768,1536]{1,0:T(8,128)(2,1)S(1)}, bf16[768,1536]{1,0:T(8,128)(2,1)}, u32[]{:S(2)}) copy-start(bf16[768,1536]{1,0:T(8,128)(2,1)} %r_ref.3) | copy-start | bytes 7077892
  4.4 50.5 %copy-start.2 = (f32[768,128]{1,0:T(8,128)S(1)}, f32[768,128]{1,0:T(8,128)}, u32[]{:S(2)}) copy-start(f32[768,128]{1,0:T(8,128)} %p_ref.1) | copy-start | bytes 1179652
  4.4 50.4 %copy-start.3 = (s32[6,12]{1,0:T(8,128)S(1)}, s32[6,12]{1,0:T(8,128)}, u32[]{:S(2)}) copy-start(s32[6,12]{1,0:T(8,128)} %m_ref.3) | copy-start | bytes 868
  4.4 50.4 %copy-start.4 = (f32[2]{0:T(128)S(1)}, f32[2]{0:T(128)}, u32[]{:S(2)}) copy-start(f32[2]{0:T(128)} %step_ref.3) | copy-start | bytes 28
  57.2 4.1 %collective-permute-start = (f32[8,104,128]{2,1,0:T(8,128)S(1)}, f32[8,104,128]{2,1,0:T(8,128)S(1)}, u32[]{:S(2)}, u32[]{:S(2)}) collective-permute-start(f32[8,104,128]{2,1,0:T(8,128)S(1)} %get-tuple-element.14), channel_id=1, source_target_pairs={{0,16},{16,0},{32,48},{48,32},{64,80},{80,64},{96,112},{112,96},{1... | collective-permute-start | bytes 1277960 | tf_op jit(solution)/shard_map/ppermute | solution.py:334
  88.8 4.1 %collective-permute-start.1 = (f32[8,96,128]{2,1,0:T(8,128)S(1)}, f32[8,96,128]{2,1,0:T(8,128)S(1)}, u32[]{:S(2)}, u32[]{:S(2)}) collective-permute-start(f32[8,96,128]{2,1,0:T(8,128)S(1)} %all_to_all.23), channel_id=1, source_target_pairs={{0,16},{16,0},{32,48},{48,32},{64,80},{80,64},{96,112},{112,96},{1... | collective-permute-start | bytes 1179656 | tf_op jit(solution)/shard_map/ppermute | solution.py:348

commit v8 on v7

--- a/solution.py
+++ b/solution.py
@@ -109,7 +109,7 @@
 
 
 def user_kernel(
-    m_hbm, r_hbm, p_hbm, q_hbm, x_ref, m_ref, r_ref, p_ref, q_ref, qcat, grams, packed, r_sem, q_sem, p_sem, m_sem
+    m_hbm, r_hbm, p_hbm, q_hbm, x_ref, m_ref, r_ref, p_ref, q_ref, qcat, turned, grams, packed, r_sem, q_sem, p_sem, m_sem
 ):
     q_copies = fetch(q_hbm, q_ref, q_sem, 4)
     m_copy = pltpu.make_async_copy(m_hbm, m_ref, m_sem)
@@ -120,9 +120,10 @@
         if j in (0, 3):
             arrive(q_copies[:1] if j == 0 else q_copies[1:])
         q = q_ref[block(j)]
-        both = split(q, 1)
-        qcat[block(j)] = both
-        grams[j] = gram(both, split(q.T, 0))
+        qcat[block(j)] = split(q, 1)
+        turned[j] = split(q.T, 0)
+    for j in range(IB):
+        grams[j] = gram(qcat[block(j)], turned[j])
     row64, lane64 = sublanes((64, BLK)), lanes((64, BLK))
     extra_row, extra_lane = sublanes((8, BLK)), lanes((8, BLK))
     extra = jnp.zeros((8, BLK), F32)
@@ -136,8 +137,8 @@
         for j in range(IB):
             h = h + present(m_ref, b, j) * grams[j]
             count = count + m_ref[b, j]
-        turned = jnp.concatenate([h[64:, 64:], h[64:, :64]], axis=1)
-        packed[b * 64 : (b + 1) * 64] = jnp.where((lane64 < 64) & (lane64 > row64), turned, h[:64])
+        moved = jnp.concatenate([h[64:, 64:], h[64:, :64]], axis=1)
+        packed[b * 64 : (b + 1) * 64] = jnp.where((lane64 < 64) & (lane64 > row64), moved, h[:64])
         diagonal = jnp.sum(jnp.where(lane64 == row64 + 64, h[64:], 0.0), axis=0, keepdims=True)
         if b % 2:
             diagonal = jnp.concatenate([diagonal[:, 64:], diagonal[:, :64]], axis=1)
@@ -192,6 +193,8 @@
         s = scales[:, b : b + 1]
         new = p_ref[block(b)] + (2.0 * s) * d - (s * s) * exact(d, w + w.T)
         new_ref[block(b)] = new
+    for b in range(UB):
+        new = new_ref[block(b)]
         turned = split(new.T, 0)
         turned_ref[:, block(b)] = turned
         grams[b] = gram(split(new, 1), turned)
@@ -210,20 +213,19 @@
     step = jnp.where(lax.axis_index("user") == 0, step_ref[1], 0.0)
     counts = jnp.where(row8 == 0, counts, step)
     first = side * (IB // 2)
-    for pair in range(IB // 4):
-        columns = pl.multiple_of(side * (ITEMS // 2) + pair * 2 * BLK, BLK)
-        masked = only_present(m_ref, r_ref, range(UB), columns, first + pair * 2, 2)
-        found = jnp.dot(turned_ref[...], masked, preferred_element_type=F32)
-        found = found[:BLK] + found[BLK:]
-        for k in range(2):
-            s = jnp.zeros((BLK, BLK), F32)
-            for b in range(UB):
-                s = s + present(m_ref, b, first + pair * 2 + k) * grams[b]
-            q = q_ref[pl.ds(pl.multiple_of(columns + k * BLK, BLK), BLK)]
-            grad = found[:, block(k)].T - exact(q, s)
-            for part in range(4):
-                piece, at = divmod((pair * 2 + k) * 4 + part, 3)
-                o_ref[piece, at * 32 : (at + 1) * 32] = grad[part * 32 : (part + 1) * 32]
+    columns = pl.multiple_of(side * (ITEMS // 2), BLK)
+    masked = only_present(m_ref, r_ref, range(UB), columns, first, IB // 2)
+    found = jnp.dot(turned_ref[...], masked, preferred_element_type=F32)
+    found = found[:BLK] + found[BLK:]
+    for k in range(IB // 2):
+        s = jnp.zeros((BLK, BLK), F32)
+        for b in range(UB):
+            s = s + present(m_ref, b, first + k) * grams[b]
+        q = q_ref[pl.ds(pl.multiple_of(columns + k * BLK, BLK), BLK)]
+        grad = found[:, block(k)].T - exact(q, s)
+        for part in range(4):
+            piece, at = divmod(k * 4 + part, 3)
+            o_ref[piece, at * 32 : (at + 1) * 32] = grad[part * 32 : (part + 1) * 32]
     for piece in range(8):
         o_ref[piece, CHUNK:] = counts
 
@@ -303,6 +305,7 @@
             pltpu.VMEM((USERS, BLK), F32),
             pltpu.VMEM((ITEMS, BLK), F32),
             pltpu.VMEM((ITEMS, 2 * BLK), BF16),
+            pltpu.VMEM((IB, 2 * BLK, BLK), BF16),
             pltpu.VMEM((IB, BLK, BLK), F32),
             pltpu.VMEM((UB * 64, BLK), F32),
             pltpu.SemaphoreType.DMA((UB,)),

time: 93.9 us -> 93.6 us (level)
  no operation moved by 1% of the time
where the time goes in v8:
time: 93.6 us; the launch traced here: 93.3 us
  blocking collectives  77.6 us (83%)
  Pallas kernels  9.25 us (10%)
  starting transfers between devices  5.32 us (6%)
    all_to_all x1, blocking collectives, body(): y = lax.all_to_all(x, 'item', 0, 0, tiled=True)  29.3 us
    all_to_all x1, blocking collectives, body(): z = lax.all_to_all(z, 'item', 0, 0, tiled=True)  21 us
    all_to_all x1, blocking collectives, body(): v = lax.all_to_all(v, 'user', 0, 0, tiled=True, axis_index_groups=chips)  16.2 us
    all_to_all x1, blocking collectives, body(): lax.all_to_all(owned, 'user', 0, 0, tiled=True, axis_index_groups=chips)  11.1 us
    pallas_call x1, Pallas kernels, body(): call(user_kernel, [pltpu.VMEM((PIECES, TILES, 4, BLK), F32)], [HBM, HBM,...  3.76 us
    ppermute x1, starting transfers between devices, body(): theirs = lax.ppermute(mine, 'user', swap)  2.73 us
    ppermute x1, starting transfers between devices, body(): received = lax.ppermute(other, 'user', swap)  2.59 us
    pallas_call x1, Pallas kernels, body(): call(item_kernel, [pltpu.VMEM((USERS, BLK), F32), pltpu.VMEM((8, CHUNK +...  2.11 us
  transfers between devices with their start and end apart: 2, of which 1 were waited for; matrix products, arithmetic and copies ran while one was open for 0% of the time, Pallas kernels for 3%

profile of v8, /device:TPU:1, one launch (start us, length us, event | category | flops | bytes accessed | tf_op | source)
XLA Modules:
  0.0 93.3 jit_solution(9449060567442765465)
XLA Ops:
  0.6 0.0 copy-start.1
  0.6 3.8 %shard_map.68 = f32[16,19,4,128]{3,2,1,0:T(4,128)S(1)} custom-call(s32[6,12]{1,0:T(8,128)} %m_ref.3, bf16[768,1536]{1,0:T(8,128)(2,1)} %r_ref.3, f32[768,128]{1,0:T(8,128)} %p_ref.1, f32[1536,128]{1,0:T(8,128)} %q_ref.5), custom_call_target="tpu_custom_call" | custom-call | tf_op jit(solution)/shard_map/pallas_call | solution.py:298
  4.4 0.0 copy-start
  4.4 0.0 copy-start.2
  4.4 0.0 copy-start.3
  4.4 0.0 copy-start.4
  4.5 29.3 %all_to_all.20.y_ref = f32[16,19,4,128]{3,2,1,0:T(4,128)S(1)} all-to-all(f32[16,19,4,128]{3,2,1,0:T(4,128)S(1)} %shard_map.68), channel_id=1, replica_groups=mesh['user'=16,'item'=16] {'item'}, dimensions={0} | all-to-all | bytes 1245184 | tf_op jit(solution)/shard_map/all_to_all | solution.py:318
  33.7 0.1 shard_map.69
  33.8 21.0 %all_to_all.21.z_ref = f32[16,72,128]{2,1,0:T(8,128)S(1)} all-to-all(f32[16,72,128]{2,1,0:T(8,128)S(1)} %get-tuple-element.10), channel_id=1, replica_groups=mesh['user'=16,'item'=16] {'item'}, dimensions={0} | all-to-all | bytes 1179648 | tf_op jit(solution)/shard_map/all_to_all | solution.py:325
  54.9 0.0 copy-done.1
  54.9 0.0 copy-done
  54.9 0.0 copy-done.2
  54.9 0.0 copy-done.3
  54.9 0.0 copy-done.4
  54.9 2.1 %shard_map.70 = (f32[768,128]{1,0:T(8,128)S(1)}, f32[8,104,128]{2,1,0:T(8,128)S(1)}, bf16[256,768]{1,0:T(8,128)(2,1)S(1)}, f32[6,128,128]{2,1,0:T(8,128)S(1)}) custom-call(s32[6,12]{1,0:T(8,128)S(1)} %copy-done.3, f32[2]{0:T(128)S(1)} %copy-done.4, bf16[768,1536]{1,0:T(8,128)(2,1)S(1)} %copy-done, f32[768,128]{1,0:T(8,128)S(1)} %copy-done.2, ...), custom_call_target="tpu_custom_call" | custom-call | tf_op jit(solution)/shard_map/pallas_call | solution.py:326
  57.0 2.6 %collective-permute-start = (f32[8,104,128]{2,1,0:T(8,128)S(1)}, f32[8,104,128]{2,1,0:T(8,128)S(1)}, u32[]{:S(2)}, u32[]{:S(2)}) collective-permute-start(f32[8,104,128]{2,1,0:T(8,128)S(1)} %get-tuple-element.14), channel_id=1, source_target_pairs={{0,16},{16,0},{32,48},{48,32},{64,80},{80,64},{96,112},{112,96},{1... | collective-permute-start | bytes 1277960 | tf_op jit(solution)/shard_map/ppermute | solution.py:337
  59.6 1.4 %shard_map.71 = f32[8,104,128]{2,1,0:T(8,128)S(1)} custom-call(s32[6,12]{1,0:T(8,128)S(1)} %copy-done.3, f32[2]{0:T(128)S(1)} %copy-done.4, bf16[768,1536]{1,0:T(8,128)(2,1)S(1)} %copy-done, f32[1536,128]{1,0:T(8,128)S(1)} %copy-done.1, bf16[256,768]{1,0:T(8,128)(2,1)S(1)} %get-tuple-element.12.turned_ref, f32[6,128,128]{2,1,0:T(8,128)S(1)} %get-tuple-element.13.grams), custom_call_target="tpu_custom_call" | custom-call | flops 4294967296 | bytes 8388608 | tf_op jit(solution)/shard_map/pallas_call | solution.py:338
  61.1 0.0 collective-permute-done
  61.1 16.2 %all_to_all.22.v_ref = f32[8,104,128]{2,1,0:T(8,128)S(1)} all-to-all(f32[8,104,128]{2,1,0:T(8,128)S(1)} %add.3), channel_id=1, replica_groups={{0,32,64,96,128,160,192,224},{16,48,80,112,144,176,208,240},{1,33,65,97..., dimensions={0} | all-to-all | bytes 851968 | tf_op jit(solution)/shard_map/all_to_all | solution.py:346
  77.3 0.1 shard_map.72
  77.4 11.1 %all_to_all.23 = f32[8,96,128]{2,1,0:T(8,128)S(1)} all-to-all(f32[8,96,128]{2,1,0:T(8,128)S(1)} %shard_map.72), channel_id=1, replica_groups={{0,32,64,96,128,160,192,224},{16,48,80,112,144,176,208,240},{1,33,65,97..., dimensions={0} | all-to-all | bytes 786432 | tf_op jit(solution)/shard_map/all_to_all | solution.py:350
  88.5 2.7 %collective-permute-start.1 = (f32[8,96,128]{2,1,0:T(8,128)S(1)}, f32[8,96,128]{2,1,0:T(8,128)S(1)}, u32[]{:S(2)}, u32[]{:S(2)}) collective-permute-start(f32[8,96,128]{2,1,0:T(8,128)S(1)} %all_to_all.23), channel_id=1, source_target_pairs={{0,16},{16,0},{32,48},{48,32},{64,80},{80,64},{96,112},{112,96},{1... | collective-permute-start | bytes 1179656 | tf_op jit(solution)/shard_map/ppermute | solution.py:351
  91.2 0.9 %shard_map.73 = (f32[1536,128]{1,0:T(8,128)}, f32[768,128]{1,0:T(8,128)}) custom-call(f32[768,128]{1,0:T(8,128)S(1)} %bitcast.2, f32[768,128]{1,0:T(8,128)S(1)} %get-tuple-element.15.new_ref), custom_call_target="tpu_custom_call" | custom-call | flops 1073741824 | bytes 4194304 | tf_op jit(solution)/shard_map/pallas_call | solution.py:352
  92.2 0.4 collective-permute-done.1
  92.6 0.8 shard_map.74
  (1 shorter events, 0.0 us)
Async XLA Ops:
  0.6 54.2 %copy-start.1 = (f32[1536,128]{1,0:T(8,128)S(1)}, f32[1536,128]{1,0:T(8,128)}, u32[]{:S(2)}) copy-start(f32[1536,128]{1,0:T(8,128)} %q_ref.5) | copy-start | bytes 2359300
  4.4 50.5 %copy-start = (bf16[768,1536]{1,0:T(8,128)(2,1)S(1)}, bf16[768,1536]{1,0:T(8,128)(2,1)}, u32[]{:S(2)}) copy-start(bf16[768,1536]{1,0:T(8,128)(2,1)} %r_ref.3) | copy-start | bytes 7077892
  4.4 50.5 %copy-start.2 = (f32[768,128]{1,0:T(8,128)S(1)}, f32[768,128]{1,0:T(8,128)}, u32[]{:S(2)}) copy-start(f32[768,128]{1,0:T(8,128)} %p_ref.1) | copy-start | bytes 1179652
  4.4 50.5 %copy-start.3 = (s32[6,12]{1,0:T(8,128)S(1)}, s32[6,12]{1,0:T(8,128)}, u32[]{:S(2)}) copy-start(s32[6,12]{1,0:T(8,128)} %m_ref.3) | copy-start | bytes 868
  4.4 50.4 %copy-start.4 = (f32[2]{0:T(128)S(1)}, f32[2]{0:T(128)}, u32[]{:S(2)}) copy-start(f32[2]{0:T(128)} %step_ref.3) | copy-start | bytes 28
  57.0 4.0 %collective-permute-start = (f32[8,104,128]{2,1,0:T(8,128)S(1)}, f32[8,104,128]{2,1,0:T(8,128)S(1)}, u32[]{:S(2)}, u32[]{:S(2)}) collective-permute-start(f32[8,104,128]{2,1,0:T(8,128)S(1)} %get-tuple-element.14), channel_id=1, source_target_pairs={{0,16},{16,0},{32,48},{48,32},{64,80},{80,64},{96,112},{112,96},{1... | collective-permute-start | bytes 1277960 | tf_op jit(solution)/shard_map/ppermute | solution.py:337
  88.5 4.1 %collective-permute-start.1 = (f32[8,96,128]{2,1,0:T(8,128)S(1)}, f32[8,96,128]{2,1,0:T(8,128)S(1)}, u32[]{:S(2)}, u32[]{:S(2)}) collective-permute-start(f32[8,96,128]{2,1,0:T(8,128)S(1)} %all_to_all.23), channel_id=1, source_target_pairs={{0,16},{16,0},{32,48},{48,32},{64,80},{80,64},{96,112},{112,96},{1... | collective-permute-start | bytes 1179656 | tf_op jit(solution)/shard_map/ppermute | solution.py:351

commit v9 on v8

--- a/solution.py
+++ b/solution.py
@@ -251,23 +251,29 @@
             o_ref[piece, k * 32 : (k + 1) * 32] = new
 
 
-def place(side, half_ref, o_hbm, sem):
+def place(first, half_ref, o_hbm, sem):
+    rows = half_ref.shape[0] // sem.shape[0]
     copies = []
-    for k in range(4):
-        rows = pl.ds(pl.multiple_of(side * (ITEMS // 2) + k * 192, 8), 192)
-        copies.append(pltpu.make_async_copy(half_ref.at[pl.ds(k * 192, 192)], o_hbm.at[rows], sem.at[k]))
+    for k in range(sem.shape[0]):
+        target = pl.ds(pl.multiple_of(first + k * rows, 8), rows)
+        copies.append(pltpu.make_async_copy(half_ref.at[pl.ds(k * rows, rows)], o_hbm.at[target], sem.at[k]))
         copies[-1].start()
     return copies
 
 
 def place_own_kernel(half_ref, new_ref, o_hbm, new_hbm, sem, new_sem):
     core = lax.rem(lax.axis_index("user"), 2)
-    arrive(place(core, half_ref, o_hbm, sem) + fetch(new_ref, new_hbm, new_sem, 4))
-
-
-def place_other_kernel(half_ref, whole, o_hbm, sem):
-    core = lax.rem(lax.axis_index("user"), 2)
-    arrive(place(1 - core, half_ref, o_hbm, sem))
+    arrive(place(core * (ITEMS // 2), half_ref, o_hbm, sem) + fetch(new_ref, new_hbm, new_sem, 4))
+
+
+def place_early_kernel(part_ref, whole, o_hbm, sem):
+    core = lax.rem(lax.axis_index("user"), 2)
+    arrive(place((1 - core) * (ITEMS // 2), part_ref, o_hbm, sem))
+
+
+def place_late_kernel(part_ref, whole, o_hbm, sem):
+    core = lax.rem(lax.axis_index("user"), 2)
+    arrive(place((1 - core) * (ITEMS // 2) + ITEMS // 4, part_ref, o_hbm, sem))
 
 
 def near(value):
@@ -348,7 +354,7 @@
         near(v), near(item_factors)
     )
     mine = lax.all_to_all(owned, "user", 0, 0, tiled=True, axis_index_groups=chips)
-    theirs = lax.ppermute(mine, "user", swap)
+    theirs = [lax.ppermute(mine[k : k + 4], "user", swap) for k in (0, 4)]
     half, new_users = call(
         place_own_kernel,
         [pltpu.HBM((ITEMS, BLK), F32), pltpu.HBM((USERS, BLK), F32)],
@@ -357,14 +363,17 @@
         out_specs=HBM,
         cost=pl.CostEstimate(flops=1 << 30, bytes_accessed=1 << 22, transcendentals=0),
     )(near(mine.reshape(ITEMS // 2, BLK)), near(new))
-    new_items = call(
-        place_other_kernel,
-        [pltpu.HBM((ITEMS, BLK), F32)],
-        [VMEM, HBM],
-        [pltpu.SemaphoreType.DMA((4,))],
-        out_specs=HBM,
-        alias={1: 0},
-    )(near(theirs.reshape(ITEMS // 2, BLK)), half)
+    for kernel, part in zip((place_early_kernel, place_late_kernel), theirs):
+        half = call(
+            kernel,
+            [pltpu.HBM((ITEMS, BLK), F32)],
+            [VMEM, HBM],
+            [pltpu.SemaphoreType.DMA((2,))],
+            out_specs=HBM,
+            cost=pl.CostEstimate(flops=1 << 29, bytes_accessed=1 << 21, transcendentals=0),
+            alias={1: 0},
+        )(near(part.reshape(ITEMS // 4, BLK)), half)
+    new_items = half
     return new_users, new_items
 
 

time: 93.6 us -> 94.1 us (level)
    ppermute x1 -> x2, starting transfers between devices: 2.73 us -> 2.91 us  [body(): theirs = [lax.ppermute(mine[k:k + 4], 'user', swap) for k in (0, 4)]]
  transfers between devices with their start and end apart: 2 -> 3, of which waited for: 1 -> 0; matrix products, arithmetic and copies ran while one was open for 0% -> 0% of each run, Pallas kernels for 3% -> 3%
where the time goes in v9:
time: 94.1 us; the launch traced here: 93.8 us
  blocking collectives  77.6 us (82%)
  Pallas kernels  9.88 us (10%)
  starting transfers between devices  5.5 us (6%)
    all_to_all x1, blocking collectives, body(): y = lax.all_to_all(x, 'item', 0, 0, tiled=True)  29.3 us
    all_to_all x1, blocking collectives, body(): z = lax.all_to_all(z, 'item', 0, 0, tiled=True)  21 us
    all_to_all x1, blocking collectives, body(): v = lax.all_to_all(v, 'user', 0, 0, tiled=True, axis_index_groups=chips)  16.2 us
    all_to_all x1, blocking collectives, body(): lax.all_to_all(owned, 'user', 0, 0, tiled=True, axis_index_groups=chips)  11.1 us
    pallas_call x1, Pallas kernels, body(): call(user_kernel, [pltpu.VMEM((PIECES, TILES, 4, BLK), F32)], [HBM, HBM,...  3.76 us
    ppermute x2, starting transfers between devices, body(): theirs = [lax.ppermute(mine[k:k + 4], 'user', swap) for k in (0, 4)]  2.91 us
    ppermute x1, starting transfers between devices, body(): received = lax.ppermute(other, 'user', swap)  2.59 us
    pallas_call x1, Pallas kernels, body(): call(item_kernel, [pltpu.VMEM((USERS, BLK), F32), pltpu.VMEM((8, CHUNK +...  2.11 us
  transfers between devices with their start and end apart: 3, of which 0 were waited for; matrix products, arithmetic and copies ran while one was open for 0% of the time, Pallas kernels for 3%

profile of v9, /device:TPU:1, one launch (start us, length us, event | category | flops | bytes accessed | tf_op | source)
XLA Modules:
  0.0 93.8 jit_solution(12512579453345817236)
XLA Ops:
  0.6 0.0 copy-start.1
  0.6 3.8 %shard_map.68 = f32[16,19,4,128]{3,2,1,0:T(4,128)S(1)} custom-call(s32[6,12]{1,0:T(8,128)} %m_ref.3, bf16[768,1536]{1,0:T(8,128)(2,1)} %r_ref.3, f32[768,128]{1,0:T(8,128)} %p_ref.1, f32[1536,128]{1,0:T(8,128)} %q_ref.5), custom_call_target="tpu_custom_call" | custom-call | tf_op jit(solution)/shard_map/pallas_call | solution.py:304
  4.4 0.0 copy-start
  4.4 0.0 copy-start.2
  4.4 0.0 copy-start.3
  4.4 0.0 copy-start.4
  4.5 29.3 %all_to_all.20.y_ref = f32[16,19,4,128]{3,2,1,0:T(4,128)S(1)} all-to-all(f32[16,19,4,128]{3,2,1,0:T(4,128)S(1)} %shard_map.68), channel_id=1, replica_groups=mesh['user'=16,'item'=16] {'item'}, dimensions={0} | all-to-all | bytes 1245184 | tf_op jit(solution)/shard_map/all_to_all | solution.py:324
  33.7 0.1 shard_map.69
  33.8 21.0 %all_to_all.21.z_ref = f32[16,72,128]{2,1,0:T(8,128)S(1)} all-to-all(f32[16,72,128]{2,1,0:T(8,128)S(1)} %get-tuple-element.10), channel_id=1, replica_groups=mesh['user'=16,'item'=16] {'item'}, dimensions={0} | all-to-all | bytes 1179648 | tf_op jit(solution)/shard_map/all_to_all | solution.py:331
  54.9 0.0 copy-done.1
  54.9 0.0 copy-done
  54.9 0.0 copy-done.2
  54.9 0.0 copy-done.3
  54.9 0.0 copy-done.4
  54.9 2.1 %shard_map.70 = (f32[768,128]{1,0:T(8,128)S(1)}, f32[8,104,128]{2,1,0:T(8,128)S(1)}, bf16[256,768]{1,0:T(8,128)(2,1)S(1)}, f32[6,128,128]{2,1,0:T(8,128)S(1)}) custom-call(s32[6,12]{1,0:T(8,128)S(1)} %copy-done.3, f32[2]{0:T(128)S(1)} %copy-done.4, bf16[768,1536]{1,0:T(8,128)(2,1)S(1)} %copy-done, f32[768,128]{1,0:T(8,128)S(1)} %copy-done.2, ...), custom_call_target="tpu_custom_call" | custom-call | tf_op jit(solution)/shard_map/pallas_call | solution.py:332
  57.0 2.6 %collective-permute-start = (f32[8,104,128]{2,1,0:T(8,128)S(1)}, f32[8,104,128]{2,1,0:T(8,128)S(1)}, u32[]{:S(2)}, u32[]{:S(2)}) collective-permute-start(f32[8,104,128]{2,1,0:T(8,128)S(1)} %get-tuple-element.14), channel_id=1, source_target_pairs={{0,16},{16,0},{32,48},{48,32},{64,80},{80,64},{96,112},{112,96},{1... | collective-permute-start | bytes 1277960 | tf_op jit(solution)/shard_map/ppermute | solution.py:343
  59.6 1.4 %shard_map.71 = f32[8,104,128]{2,1,0:T(8,128)S(1)} custom-call(s32[6,12]{1,0:T(8,128)S(1)} %copy-done.3, f32[2]{0:T(128)S(1)} %copy-done.4, bf16[768,1536]{1,0:T(8,128)(2,1)S(1)} %copy-done, f32[1536,128]{1,0:T(8,128)S(1)} %copy-done.1, bf16[256,768]{1,0:T(8,128)(2,1)S(1)} %get-tuple-element.12.turned_ref, f32[6,128,128]{2,1,0:T(8,128)S(1)} %get-tuple-element.13.grams), custom_call_target="tpu_custom_call" | custom-call | flops 4294967296 | bytes 8388608 | tf_op jit(solution)/shard_map/pallas_call | solution.py:344
  61.1 0.0 collective-permute-done
  61.1 16.2 %all_to_all.22.v_ref = f32[8,104,128]{2,1,0:T(8,128)S(1)} all-to-all(f32[8,104,128]{2,1,0:T(8,128)S(1)} %add.3), channel_id=1, replica_groups={{0,32,64,96,128,160,192,224},{16,48,80,112,144,176,208,240},{1,33,65,97..., dimensions={0} | all-to-all | bytes 851968 | tf_op jit(solution)/shard_map/all_to_all | solution.py:352
  77.3 0.1 shard_map.72
  77.4 11.1 %all_to_all.23 = f32[8,96,128]{2,1,0:T(8,128)S(1)} all-to-all(f32[8,96,128]{2,1,0:T(8,128)S(1)} %shard_map.72), channel_id=1, replica_groups={{0,32,64,96,128,160,192,224},{16,48,80,112,144,176,208,240},{1,33,65,97..., dimensions={0} | all-to-all | bytes 786432 | tf_op jit(solution)/shard_map/all_to_all | solution.py:356
  88.5 2.8 %collective-permute-start.2 = (f32[4,96,128]{2,1,0:T(8,128)S(1)}, f32[4,96,128]{2,1,0:T(8,128)S(1)}, u32[]{:S(2)}, u32[]{:S(2)}) collective-permute-start(f32[4,96,128]{2,1,0:T(8,128)S(1)} %get-tuple-element.18), channel_id=1, source_target_pairs={{0,16},{16,0},{32,48},{48,32},{64,80},{80,64},{96,112},{112,96},{1... | collective-permute-start | bytes 589832 | tf_op jit(solution)/shard_map/ppermute | solution.py:357
  91.3 0.1 collective-permute-start.1
  91.4 0.9 %shard_map.73 = (f32[1536,128]{1,0:T(8,128)}, f32[768,128]{1,0:T(8,128)}) custom-call(f32[768,128]{1,0:T(8,128)S(1)} %bitcast.3, f32[768,128]{1,0:T(8,128)S(1)} %get-tuple-element.15.new_ref), custom_call_target="tpu_custom_call" | custom-call | flops 1073741824 | bytes 4194304 | tf_op jit(solution)/shard_map/pallas_call | solution.py:358
  92.4 0.0 collective-permute-done.2
  92.4 0.7 shard_map.74.whole
  93.1 0.0 collective-permute-done.1
  93.1 0.7 shard_map.75
  (2 shorter events, 0.1 us)
Async XLA Ops:
  0.6 54.2 %copy-start.1 = (f32[1536,128]{1,0:T(8,128)S(1)}, f32[1536,128]{1,0:T(8,128)}, u32[]{:S(2)}) copy-start(f32[1536,128]{1,0:T(8,128)} %q_ref.5) | copy-start | bytes 2359300
  4.4 50.5 %copy-start = (bf16[768,1536]{1,0:T(8,128)(2,1)S(1)}, bf16[768,1536]{1,0:T(8,128)(2,1)}, u32[]{:S(2)}) copy-start(bf16[768,1536]{1,0:T(8,128)(2,1)} %r_ref.3) | copy-start | bytes 7077892
  4.4 50.5 %copy-start.2 = (f32[768,128]{1,0:T(8,128)S(1)}, f32[768,128]{1,0:T(8,128)}, u32[]{:S(2)}) copy-start(f32[768,128]{1,0:T(8,128)} %p_ref.1) | copy-start | bytes 1179652
  4.4 50.5 %copy-start.3 = (s32[6,12]{1,0:T(8,128)S(1)}, s32[6,12]{1,0:T(8,128)}, u32[]{:S(2)}) copy-start(s32[6,12]{1,0:T(8,128)} %m_ref.3) | copy-start | bytes 868
  4.4 50.4 %copy-start.4 = (f32[2]{0:T(128)S(1)}, f32[2]{0:T(128)}, u32[]{:S(2)}) copy-start(f32[2]{0:T(128)} %step_ref.3) | copy-start | bytes 28
  57.0 4.0 %collective-permute-start = (f32[8,104,128]{2,1,0:T(8,128)S(1)}, f32[8,104,128]{2,1,0:T(8,128)S(1)}, u32[]{:S(2)}, u32[]{:S(2)}) collective-permute-start(f32[8,104,128]{2,1,0:T(8,128)S(1)} %get-tuple-element.14), channel_id=1, source_target_pairs={{0,16},{16,0},{32,48},{48,32},{64,80},{80,64},{96,112},{112,96},{1... | collective-permute-start | bytes 1277960 | tf_op jit(solution)/shard_map/ppermute | solution.py:343
  88.5 3.9 %collective-permute-start.2 = (f32[4,96,128]{2,1,0:T(8,128)S(1)}, f32[4,96,128]{2,1,0:T(8,128)S(1)}, u32[]{:S(2)}, u32[]{:S(2)}) collective-permute-start(f32[4,96,128]{2,1,0:T(8,128)S(1)} %get-tuple-element.18), channel_id=1, source_target_pairs={{0,16},{16,0},{32,48},{48,32},{64,80},{80,64},{96,112},{112,96},{1... | collective-permute-start | bytes 589832 | tf_op jit(solution)/shard_map/ppermute | solution.py:357
  91.3 1.8 %collective-permute-start.1 = (f32[4,96,128]{2,1,0:T(8,128)S(1)}, f32[4,96,128]{2,1,0:T(8,128)S(1)}, u32[]{:S(2)}, u32[]{:S(2)}) collective-permute-start(f32[4,96,128]{2,1,0:T(8,128)S(1)} %get-tuple-element.19), channel_id=1, source_target_pairs={{0,16},{16,0},{32,48},{48,32},{64,80},{80,64},{96,112},{112,96},{1... | collective-permute-start | bytes 589832 | tf_op jit(solution)/shard_map/ppermute | solution.py:357

commit v10 on v8

--- a/solution.py
+++ b/solution.py
@@ -111,14 +111,14 @@
 def user_kernel(
     m_hbm, r_hbm, p_hbm, q_hbm, x_ref, m_ref, r_ref, p_ref, q_ref, qcat, turned, grams, packed, r_sem, q_sem, p_sem, m_sem
 ):
-    q_copies = fetch(q_hbm, q_ref, q_sem, 4)
+    q_copies = fetch(q_hbm, q_ref, q_sem, 12)
     m_copy = pltpu.make_async_copy(m_hbm, m_ref, m_sem)
     m_copy.start()
     p_copies = fetch(p_hbm, p_ref, p_sem, 2)
-    r_copies = fetch(r_hbm, r_ref, r_sem, UB)
+    r_copies = fetch(r_hbm, r_ref, r_sem, 2 * UB)
     for j in range(IB):
         if j in (0, 3):
-            arrive(q_copies[:1] if j == 0 else q_copies[1:])
+            arrive(q_copies[:3] if j == 0 else q_copies[3:])
         q = q_ref[block(j)]
         qcat[block(j)] = split(q, 1)
         turned[j] = split(q.T, 0)
@@ -308,8 +308,8 @@
             pltpu.VMEM((IB, 2 * BLK, BLK), BF16),
             pltpu.VMEM((IB, BLK, BLK), F32),
             pltpu.VMEM((UB * 64, BLK), F32),
-            pltpu.SemaphoreType.DMA((UB,)),
-            pltpu.SemaphoreType.DMA((4,)),
+            pltpu.SemaphoreType.DMA((2 * UB,)),
+            pltpu.SemaphoreType.DMA((12,)),
             pltpu.SemaphoreType.DMA((2,)),
             pltpu.SemaphoreType.DMA,
         ],

time: 93.6 us -> 93.8 us (level)
  no operation moved by 1% of the time
where the time goes in v10:
time: 93.8 us; the launch traced here: 93.6 us
  blocking collectives  77.5 us (83%)
  Pallas kernels  9.48 us (10%)
  starting transfers between devices  5.32 us (6%)
    all_to_all x1, blocking collectives, body(): y = lax.all_to_all(x, 'item', 0, 0, tiled=True)  29.3 us
    all_to_all x1, blocking collectives, body(): z = lax.all_to_all(z, 'item', 0, 0, tiled=True)  21 us
    all_to_all x1, blocking collectives, body(): v = lax.all_to_all(v, 'user', 0, 0, tiled=True, axis_index_groups=chips)  16.2 us
    all_to_all x1, blocking collectives, body(): lax.all_to_all(owned, 'user', 0, 0, tiled=True, axis_index_groups=chips)  11.1 us
    pallas_call x1, Pallas kernels, body(): call(user_kernel, [pltpu.VMEM((PIECES, TILES, 4, BLK), F32)], [HBM, HBM,...  4 us
    ppermute x1, starting transfers between devices, body(): theirs = lax.ppermute(mine, 'user', swap)  2.73 us
    ppermute x1, starting transfers between devices, body(): received = lax.ppermute(other, 'user', swap)  2.59 us
    pallas_call x1, Pallas kernels, body(): call(item_kernel, [pltpu.VMEM((USERS, BLK), F32), pltpu.VMEM((8, CHUNK +...  2.11 us
  transfers between devices with their start and end apart: 2, of which 1 were waited for; matrix products, arithmetic and copies ran while one was open for 0% of the time, Pallas kernels for 3%

profile of v10, /device:TPU:1, one launch (start us, length us, event | category | flops | bytes accessed | tf_op | source)
XLA Modules:
  0.0 93.6 jit_solution(3786697114832010366)
XLA Ops:
  0.6 0.0 copy-start.1
  0.6 4.0 %shard_map.68 = f32[16,19,4,128]{3,2,1,0:T(4,128)S(1)} custom-call(s32[6,12]{1,0:T(8,128)} %m_ref.3, bf16[768,1536]{1,0:T(8,128)(2,1)} %r_ref.3, f32[768,128]{1,0:T(8,128)} %p_ref.1, f32[1536,128]{1,0:T(8,128)} %q_ref.5), custom_call_target="tpu_custom_call" | custom-call | tf_op jit(solution)/shard_map/pallas_call | solution.py:298
  4.6 0.0 copy-start
  4.7 0.0 copy-start.2
  4.7 0.0 copy-start.3
  4.7 0.0 copy-start.4
  4.7 29.3 %all_to_all.20.y_ref = f32[16,19,4,128]{3,2,1,0:T(4,128)S(1)} all-to-all(f32[16,19,4,128]{3,2,1,0:T(4,128)S(1)} %shard_map.68), channel_id=1, replica_groups=mesh['user'=16,'item'=16] {'item'}, dimensions={0} | all-to-all | bytes 1245184 | tf_op jit(solution)/shard_map/all_to_all | solution.py:318
  34.0 0.1 shard_map.69
  34.1 21.0 %all_to_all.21.z_ref = f32[16,72,128]{2,1,0:T(8,128)S(1)} all-to-all(f32[16,72,128]{2,1,0:T(8,128)S(1)} %get-tuple-element.10), channel_id=1, replica_groups=mesh['user'=16,'item'=16] {'item'}, dimensions={0} | all-to-all | bytes 1179648 | tf_op jit(solution)/shard_map/all_to_all | solution.py:325
  55.1 0.0 copy-done.1
  55.1 0.0 copy-done
  55.1 0.0 copy-done.2
  55.1 0.0 copy-done.3
  55.1 0.0 copy-done.4
  55.1 2.1 %shard_map.70 = (f32[768,128]{1,0:T(8,128)S(1)}, f32[8,104,128]{2,1,0:T(8,128)S(1)}, bf16[256,768]{1,0:T(8,128)(2,1)S(1)}, f32[6,128,128]{2,1,0:T(8,128)S(1)}) custom-call(s32[6,12]{1,0:T(8,128)S(1)} %copy-done.3, f32[2]{0:T(128)S(1)} %copy-done.4, bf16[768,1536]{1,0:T(8,128)(2,1)S(1)} %copy-done, f32[768,128]{1,0:T(8,128)S(1)} %copy-done.2, ...), custom_call_target="tpu_custom_call" | custom-call | tf_op jit(solution)/shard_map/pallas_call | solution.py:326
  57.3 2.6 %collective-permute-start = (f32[8,104,128]{2,1,0:T(8,128)S(1)}, f32[8,104,128]{2,1,0:T(8,128)S(1)}, u32[]{:S(2)}, u32[]{:S(2)}) collective-permute-start(f32[8,104,128]{2,1,0:T(8,128)S(1)} %get-tuple-element.14), channel_id=1, source_target_pairs={{0,16},{16,0},{32,48},{48,32},{64,80},{80,64},{96,112},{112,96},{1... | collective-permute-start | bytes 1277960 | tf_op jit(solution)/shard_map/ppermute | solution.py:337
  59.8 1.4 %shard_map.71 = f32[8,104,128]{2,1,0:T(8,128)S(1)} custom-call(s32[6,12]{1,0:T(8,128)S(1)} %copy-done.3, f32[2]{0:T(128)S(1)} %copy-done.4, bf16[768,1536]{1,0:T(8,128)(2,1)S(1)} %copy-done, f32[1536,128]{1,0:T(8,128)S(1)} %copy-done.1, bf16[256,768]{1,0:T(8,128)(2,1)S(1)} %get-tuple-element.12.turned_ref, f32[6,128,128]{2,1,0:T(8,128)S(1)} %get-tuple-element.13.grams), custom_call_target="tpu_custom_call" | custom-call | flops 4294967296 | bytes 8388608 | tf_op jit(solution)/shard_map/pallas_call | solution.py:338
  61.3 0.0 collective-permute-done
  61.4 16.2 %all_to_all.22.v_ref = f32[8,104,128]{2,1,0:T(8,128)S(1)} all-to-all(f32[8,104,128]{2,1,0:T(8,128)S(1)} %add.3), channel_id=1, replica_groups={{0,32,64,96,128,160,192,224},{16,48,80,112,144,176,208,240},{1,33,65,97..., dimensions={0} | all-to-all | bytes 851968 | tf_op jit(solution)/shard_map/all_to_all | solution.py:346
  77.5 0.1 shard_map.72
  77.7 11.1 %all_to_all.23 = f32[8,96,128]{2,1,0:T(8,128)S(1)} all-to-all(f32[8,96,128]{2,1,0:T(8,128)S(1)} %shard_map.72), channel_id=1, replica_groups={{0,32,64,96,128,160,192,224},{16,48,80,112,144,176,208,240},{1,33,65,97..., dimensions={0} | all-to-all | bytes 786432 | tf_op jit(solution)/shard_map/all_to_all | solution.py:350
  88.7 2.7 %collective-permute-start.1 = (f32[8,96,128]{2,1,0:T(8,128)S(1)}, f32[8,96,128]{2,1,0:T(8,128)S(1)}, u32[]{:S(2)}, u32[]{:S(2)}) collective-permute-start(f32[8,96,128]{2,1,0:T(8,128)S(1)} %all_to_all.23), channel_id=1, source_target_pairs={{0,16},{16,0},{32,48},{48,32},{64,80},{80,64},{96,112},{112,96},{1... | collective-permute-start | bytes 1179656 | tf_op jit(solution)/shard_map/ppermute | solution.py:351
  91.4 0.9 %shard_map.73 = (f32[1536,128]{1,0:T(8,128)}, f32[768,128]{1,0:T(8,128)}) custom-call(f32[768,128]{1,0:T(8,128)S(1)} %bitcast.2, f32[768,128]{1,0:T(8,128)S(1)} %get-tuple-element.15.new_ref), custom_call_target="tpu_custom_call" | custom-call | flops 1073741824 | bytes 4194304 | tf_op jit(solution)/shard_map/pallas_call | solution.py:352
  92.4 0.4 collective-permute-done.1
  92.8 0.8 shard_map.74
  (1 shorter events, 0.0 us)
Async XLA Ops:
  0.6 54.5 %copy-start.1 = (f32[1536,128]{1,0:T(8,128)S(1)}, f32[1536,128]{1,0:T(8,128)}, u32[]{:S(2)}) copy-start(f32[1536,128]{1,0:T(8,128)} %q_ref.5) | copy-start | bytes 2359300
  4.6 50.5 %copy-start = (bf16[768,1536]{1,0:T(8,128)(2,1)S(1)}, bf16[768,1536]{1,0:T(8,128)(2,1)}, u32[]{:S(2)}) copy-start(bf16[768,1536]{1,0:T(8,128)(2,1)} %r_ref.3) | copy-start | bytes 7077892
  4.7 50.5 %copy-start.2 = (f32[768,128]{1,0:T(8,128)S(1)}, f32[768,128]{1,0:T(8,128)}, u32[]{:S(2)}) copy-start(f32[768,128]{1,0:T(8,128)} %p_ref.1) | copy-start | bytes 1179652
  4.7 50.4 %copy-start.3 = (s32[6,12]{1,0:T(8,128)S(1)}, s32[6,12]{1,0:T(8,128)}, u32[]{:S(2)}) copy-start(s32[6,12]{1,0:T(8,128)} %m_ref.3) | copy-start | bytes 868
  4.7 50.4 %copy-start.4 = (f32[2]{0:T(128)S(1)}, f32[2]{0:T(128)}, u32[]{:S(2)}) copy-start(f32[2]{0:T(128)} %step_ref.3) | copy-start | bytes 28
  57.3 4.0 %collective-permute-start = (f32[8,104,128]{2,1,0:T(8,128)S(1)}, f32[8,104,128]{2,1,0:T(8,128)S(1)}, u32[]{:S(2)}, u32[]{:S(2)}) collective-permute-start(f32[8,104,128]{2,1,0:T(8,128)S(1)} %get-tuple-element.14), channel_id=1, source_target_pairs={{0,16},{16,0},{32,48},{48,32},{64,80},{80,64},{96,112},{112,96},{1... | collective-permute-start | bytes 1277960 | tf_op jit(solution)/shard_map/ppermute | solution.py:337
  88.7 4.1 %collective-permute-start.1 = (f32[8,96,128]{2,1,0:T(8,128)S(1)}, f32[8,96,128]{2,1,0:T(8,128)S(1)}, u32[]{:S(2)}, u32[]{:S(2)}) collective-permute-start(f32[8,96,128]{2,1,0:T(8,128)S(1)} %all_to_all.23), channel_id=1, source_target_pairs={{0,16},{16,0},{32,48},{48,32},{64,80},{80,64},{96,112},{112,96},{1... | collective-permute-start | bytes 1179656 | tf_op jit(solution)/shard_map/ppermute | solution.py:351
